TPU v7x, 32 devices: a whole 2x2x4 slice. The times are simulated.
32 devices in a mesh: dp: 8 (over y, x, core), chan: 4 (over z).
Axes of the slice: x: 2, y: 2, z: 4, core: 2. Of those that a mesh axis runs over, the one named last changes fastest.
Arguments:
- clips_in: bfloat16 [128, 256, 512], P('dp', None, 'chan'), may hold values from -6 to 6
- speaker: int32 [128], P('dp'), may hold values from 0 to 63
- counts: int32 [8], P('dp'), may hold values from 4 to 16, as said below
- conv_weight: bfloat16 [7, 512], P(None, 'chan'), may hold values from -2 to 2
- conv_bias: bfloat16 [512], P('chan'), may hold values from -1.5 to 1.5
- scale_table: bfloat16 [64, 512], P(None, 'chan'), may hold values from 0.099609375 to 1.8984375
- shift_table: bfloat16 [64, 512], P(None, 'chan'), may hold values from -1.5 to 1.5
- w_in: bfloat16 [512, 1536], P(None, 'chan'), may hold values from -0.25 to 0.25
- b_in: bfloat16 [1536], P('chan'), may hold values from -2.5 to 2.5
- w_out: bfloat16 [1536, 512], P('chan'), may hold values from -0.21875 to 0.21875
- b_out: bfloat16 [512], P('chan'), may hold values from -1.5 to 1.5
- layer_scale: bfloat16 [512], P('chan'), may hold values from 0.5 to 1.5
- grad_out: bfloat16 [128, 256, 512], P('dp', None, 'chan'), may hold values from -6 to 6
Outputs:
- clips_out: bfloat16 [128, 256, 512], P('dp', None, 'chan')
- grad_clips: float32 [128, 256, 512], P('dp', None, 'chan')
- grad_conv_weight: float32 [7, 512], P(None, 'chan')
- grad_conv_bias: float32 [512], P('chan')
- grad_scale_table: float32 [64, 512], P(None, 'chan')
- grad_shift_table: float32 [64, 512], P(None, 'chan')
- grad_w_in: float32 [512, 1536], P(None, 'chan')
- grad_b_in: float32 [1536], P('chan')
- grad_w_out: float32 [1536, 512], P('chan')
- grad_b_out: float32 [512], P('chan')
- grad_layer_scale: float32 [512], P('chan')
Inputs may be any that keep to these rules, and one draw needn't show every extreme that they name: `counts`: each index of dp holds 16 clip slots; the slots below its count are live clips, the rest padding. Some index has all 16 slots live.
All inputs are finite; a program needn't handle non-finite values.
Results may differ from a plain program's by a relative error of at most 0.0063.
Values may be sent and summed in bfloat16 or wider, within the bound.
No kernel may reach another device: no remote copies, remote signals or barrier semaphores. Data moves between devices by JAX's collectives and lax.ppermute only.
A program may use at most 128 MiB of HBM per device.

v0:
```python
import jax
import jax.numpy as jnp
from jax import lax
from jax.sharding import PartitionSpec as P

epsilon = 1e-06
root_half = 0.7071067811865476
root_two_pi = 2.5066282746310002


def gelu_value(values):
    return 0.5 * values * (1.0 + jax.scipy.special.erf(values * root_half))


def gelu_slope(values):
    return (
        0.5 * (1.0 + jax.scipy.special.erf(values * root_half))
        + values * jnp.exp(-0.5 * values * values) / root_two_pi
    )


def contract(left, right, left_dim, right_dim):
    return lax.dot_general(
        left, right, (((left_dim,), (right_dim,)), ((), ())), preferred_element_type=jnp.float32
    )


def per_device(
    clips_in,
    speaker,
    counts,
    conv_weight,
    conv_bias,
    scale_table,
    shift_table,
    w_in,
    b_in,
    w_out,
    b_out,
    layer_scale,
    grad_out,
):
    clip_num, length, chan_width = clips_in.shape
    row_total = clip_num * length
    chan_count = lax.axis_size("chan")
    full_width = chan_width * chan_count
    speaker_count = scale_table.shape[0]
    tap_count = conv_weight.shape[0]
    margin = tap_count // 2
    inputs = clips_in.astype(jnp.float32)
    kernel = conv_weight.astype(jnp.float32)
    padded = jnp.pad(inputs, ((0, 0), (margin, margin), (0, 0)))
    conv_out = conv_bias.astype(jnp.float32) + sum(
        (kernel[offset] * padded[:, offset : offset + length] for offset in range(tap_count))
    )
    conv_flat = conv_out.reshape(row_total, chan_width)
    live = (jnp.arange(clip_num) < counts[0]).astype(jnp.float32)
    live_rows = jnp.broadcast_to(live[:, None], (clip_num, length)).reshape(row_total, 1)
    row_sum = lax.psum(jnp.sum(conv_flat, 1), "chan")
    row_mean = row_sum / full_width
    centered = conv_flat - row_mean[:, None]
    variance = lax.psum(jnp.sum(centered * centered, 1), "chan") / full_width
    inv_std = lax.rsqrt(variance + epsilon)[:, None]
    normed = centered * inv_std
    normed_clips = normed.reshape(clip_num, length, chan_width)
    speaker_hot = (speaker[:, None] == jnp.arange(speaker_count)[None, :]).astype(jnp.float32)
    clip_scale = jnp.dot(
        speaker_hot, scale_table.astype(jnp.float32), precision=lax.Precision.HIGHEST
    )
    clip_shift = jnp.dot(
        speaker_hot, shift_table.astype(jnp.float32), precision=lax.Precision.HIGHEST
    )
    norm_low = (
        (normed_clips * clip_scale[:, None, :] + clip_shift[:, None, :])
        .astype(jnp.bfloat16)
        .reshape(row_total, chan_width)
    )
    norm_all = lax.all_gather(norm_low, "chan", axis=1, tiled=True)
    pre_act = jnp.dot(norm_all, w_in, preferred_element_type=jnp.float32) + b_in.astype(jnp.float32)
    act_low = gelu_value(pre_act).astype(jnp.bfloat16)
    partial_out = jnp.dot(act_low, w_out, preferred_element_type=jnp.float32)
    branch = lax.psum_scatter(partial_out, "chan", scatter_dimension=1, tiled=True) + b_out.astype(
        jnp.float32
    )
    gain_vec = layer_scale.astype(jnp.float32)
    result = (
        (inputs.reshape(row_total, chan_width) + branch * gain_vec * live_rows)
        .astype(jnp.bfloat16)
        .reshape(clips_in.shape)
    )
    upstream = grad_out.astype(jnp.float32).reshape(row_total, chan_width)
    masked = upstream * live_rows
    grad_gain = jnp.sum(masked * branch, 0)
    grad_branch = masked * gain_vec
    grad_b_out = jnp.sum(grad_branch, 0)
    branch_low = grad_branch.astype(jnp.bfloat16)
    branch_all = lax.all_gather(branch_low, "chan", axis=1, tiled=True)
    grad_w_out = contract(act_low, branch_all, 0, 0)
    grad_act = contract(branch_all, w_out, 1, 1)
    grad_pre = grad_act * gelu_slope(pre_act)
    grad_b_in = jnp.sum(grad_pre, 0)
    pre_low = grad_pre.astype(jnp.bfloat16)
    grad_w_in = contract(norm_all, pre_low, 0, 0)
    norm_part = contract(pre_low, w_in, 1, 1)
    grad_norm = lax.psum_scatter(norm_part, "chan", scatter_dimension=1, tiled=True).reshape(
        clip_num, length, chan_width
    )
    grad_scale_tab = jnp.dot(
        speaker_hot.T, jnp.sum(grad_norm * normed_clips, 1), precision=lax.Precision.HIGHEST
    )
    grad_shift_tab = jnp.dot(speaker_hot.T, jnp.sum(grad_norm, 1), precision=lax.Precision.HIGHEST)
    grad_normed = (grad_norm * clip_scale[:, None, :]).reshape(row_total, chan_width)
    first_sum, second_sum = (
        lax.psum(jnp.sum(grad_normed, 1).astype(jnp.bfloat16), "chan").astype(jnp.float32),
        lax.psum(jnp.sum(grad_normed * normed, 1).astype(jnp.bfloat16), "chan").astype(jnp.float32),
    )
    grad_conv = (
        grad_normed - first_sum[:, None] / full_width - normed * (second_sum[:, None] / full_width)
    ) * inv_std
    grad_conv = grad_conv.reshape(clip_num, length, chan_width)
    grad_conv_b = jnp.sum(grad_conv, (0, 1))
    padded_grad = jnp.pad(grad_conv, ((0, 0), (margin, margin), (0, 0)))
    grad_input = upstream.reshape(clips_in.shape) + sum(
        (
            kernel[offset]
            * padded_grad[:, tap_count - 1 - offset : tap_count - 1 - offset + length]
            for offset in range(tap_count)
        )
    )
    grad_kernel = jnp.stack(
        [
            jnp.sum(padded[:, offset : offset + length] * grad_conv, (0, 1))
            for offset in range(tap_count)
        ]
    )
    summed = lax.psum(
        (
            grad_kernel,
            grad_conv_b,
            grad_scale_tab,
            grad_shift_tab,
            grad_w_in,
            grad_b_in,
            grad_w_out,
            grad_b_out,
            grad_gain,
        ),
        "dp",
    )
    return (
        result,
        grad_input,
        summed[0],
        summed[1],
        summed[2],
        summed[3],
        summed[4],
        summed[5],
        summed[6],
        summed[7],
        summed[8],
    )


def solution(mesh):
    in_specs = (
        P("dp", None, "chan"),
        P("dp"),
        P("dp"),
        P(None, "chan"),
        P("chan"),
        P(None, "chan"),
        P(None, "chan"),
        P(None, "chan"),
        P("chan"),
        P("chan", None),
        P("chan"),
        P("chan"),
        P("dp", None, "chan"),
    )
    out_specs = (
        P("dp", None, "chan"),
        P("dp", None, "chan"),
        P(None, "chan"),
        P("chan"),
        P(None, "chan"),
        P(None, "chan"),
        P(None, "chan"),
        P("chan"),
        P("chan", None),
        P("chan"),
        P("chan"),
    )
    return jax.shard_map(
        per_device, mesh=mesh, in_specs=in_specs, out_specs=out_specs, check_vma=False
    )
```

profile of v0, /device:TPU:0, one launch (start us, length us, event | category | flops | bytes accessed | tf_op | source)
XLA Modules:
  0.0 667.7 jit_solution(2383264202741851544)
XLA Ops:
  9.5 2.1 fusion.24
  11.7 20.5 %psum.91 = f32[4096]{0:T(1024)S(1)} all-reduce(f32[4096]{0:T(1024)S(1)} %bitcast.93), channel_id=1, replica_groups=mesh['dp'=8,'chan'=4] {'chan'}, use_global_device_ids=true, to_apply=%region_1.2 | all-reduce | flops 4096 | bytes 32768 | tf_op jit(solution)/shard_map/psum | solution.py:59
  33.6 15.5 %psum.92 = f32[4096]{0:T(1024)S(1)} all-reduce(f32[4096]{0:T(1024)S(1)} %bitcast.94), channel_id=1, replica_groups=mesh['dp'=8,'chan'=4] {'chan'}, use_global_device_ids=true, to_apply=%region_3.4 | all-reduce | flops 4096 | bytes 32768 | tf_op jit(solution)/shard_map/psum | solution.py:62
  49.6 2.0 add_convert_fusion
  51.8 79.1 %all-gather.3.cloned.1.call-done = bf16[4096,512]{1,0:T(8,128)(2,1)} async-done(((bf16[4096,128]{1,0:T(8,128)(2,1)}), bf16[4096,512]{1,0:T(8,128)(2,1)}) %all-gather.3.cloned.1.call-update) | async-done | bytes 4194320 | tf_op jit(solution)/shard_map/all_gather | solution.py:78
  130.9 6.3 multiply_convert_fusion
  138.9 5.6 fusion.26
  148.3 139.2 %reduce-scatter.3.cloned.1.call-done = f32[4096,128]{1,0:T(8,128)} async-done(((f32[4096,512]{1,0:T(8,128)}), f32[4096,128]{1,0:T(8,128)}) %reduce-scatter.3.cloned.1.call-update) | async-done | bytes 2097168 | tf_op jit(solution)/shard_map/reduce_scatter | solution.py:82
  287.5 3.9 multiply_reduce_fusion
  291.5 81.2 %all-gather.5.cloned.1.call-done = bf16[4096,512]{1,0:T(8,128)(2,1)} async-done(((bf16[4096,128]{1,0:T(8,128)(2,1)}), bf16[4096,512]{1,0:T(8,128)(2,1)}) %all-gather.5.cloned.1.call-update) | async-done | bytes 4194320 | tf_op jit(solution)/shard_map/all_gather | solution.py:97
  372.7 7.4 %fusion.25 = (f32[384]{0:T(512)}, bf16[4096,384]{1,0:T(8,128)(2,1)S(1)}) fusion(f32[4096,384]{1,0:T(8,128)} %get-tuple-element.50, bf16[4096,512]{1,0:T(8,128)(2,1)} %all-gather.5.cloned.1.call-done, bf16[384,512]{1,0:T(8,128)(2,1)} %param.22), kind=kOutput, calls=%fused_computation.72 | convolution fusion | flops 1627913856 | bytes 14026240 | tf_op jit(solution)/shard_map/dot_general | solution.py:23
  381.8 5.6 fusion.13
  387.7 6.0 fusion.27
  393.7 3.2 fusion.11
  397.0 133.3 %reduce-scatter.5.cloned.1.call-done = f32[4096,128]{1,0:T(8,128)} async-done(((f32[4096,512]{1,0:T(8,128)}), f32[4096,128]{1,0:T(8,128)}) %reduce-scatter.5.cloned.1.call-update) | async-done | bytes 2097168 | tf_op jit(solution)/shard_map/reduce_scatter | solution.py:105
  530.4 4.4 fusion.10
  534.8 19.3 %all-reduce.4 = (bf16[4096]{0:T(1024)(128)(2,1)}, bf16[4096]{0:T(1024)(128)(2,1)}) all-reduce(bf16[4096]{0:T(1024)(128)(2,1)} %get-tuple-element.18, bf16[4096]{0:T(1024)(128)(2,1)} %get-tuple-element.17), channel_id=1, replica_groups=mesh['dp'=8,'chan'=4] {'chan'}, use_global_device_ids=true, to_apply=%region_9.10 | all-reduce | flops 8192 | bytes 32768 | tf_op jit(solution)/shard_map/psum | solution.py:115
  554.9 4.8 fusion.23
  559.7 2.5 multiply_reduce_fusion.3
  562.2 1.9 bitcast_reduce_fusion
  567.9 10.1 %multiply_reduce_fusion.1 = (f32[128]{0:T(128)}, f32[16,256,128]{2,1,0:T(8,128)}) fusion(bf16[16,256,128]{2,1,0:T(8,128)(2,1)S(1)} %copy-done.6, f32[128]{0:T(128)} %convert_element_type.68, f32[16]{0:T(128)} %copy-done.24, f32[128]{0:T(128)} %copy-done.18, f32[128]{0:T(128)} %copy-done.19, f32[128]{0:T(128)} %copy-done.20, f32[16,256,128]{2,1,0:T(8,128)} %bitcast.87, ...), kind=kLoop, calls=%fused_computation.17 | loop fusion | flops 9437056 | bytes 5247552 | tf_op jit(solution)/shard_map/reduce_sum | solution.py:95
  578.0 16.3 %all-reduce.10.cloned.1.call-done = (f32[512,384]{1,0:T(8,128)}, f32[384,512]{1,0:T(8,128)}) async-done(((f32[512,384]{1,0:T(8,128)}, f32[384,512]{1,0:T(8,128)}), (f32[512,384]{1,0:T(8,128)}, f32[384,512]{1,0:T(8,128)})) %all-reduce.10.cloned.1.call-update) | async-done | bytes 1572880 | tf_op jit(solution)/shard_map/psum | solution.py:136
  594.4 56.2 %all-reduce.8.cloned.1.call-done = (f32[7,128]{1,0:T(8,128)}, f32[128]{0:T(128)}, f32[64,128]{1,0:T(8,128)}, f32[64,128]{1,0:T(8,128)}, f32[384]{0:T(512)}, /*index=5*/f32[128]{0:T(128)}, f32[128]{0:T(128)}) async-done(((f32[7,128]{1,0:T(8,128)}, f32[128]{0:T(128)}, f32[64,128]{1,0:T(8,128)}, f32[64,128]{1,0:T(8,128)}, f32[384]{0:T(512)}, /*index=5*/f32[128]{0:T(128)}, f32[128]{0:T(128)}), ...) | async-done | bytes 72208 | tf_op jit(solution)/shard_map/psum | solution.py:136
  655.7 2.1 copy.41
  (111 shorter events, 23.9 us)
Async XLA Ops:
  7.2 123.7 %copy-start = (bf16[512,384]{1,0:T(8,128)(2,1)S(1)}, bf16[512,384]{1,0:T(8,128)(2,1)}, u32[]{:S(2)}) copy-start(bf16[512,384]{1,0:T(8,128)(2,1)} %param.20) | copy-start | bytes 1179652
  7.2 123.7 %all-gather.3.cloned.1.call-start = ((), (), s32[]{:S(2)}) async-start(), calls=%async_computation.2 | async-start | bytes 5242880 | tf_op jit(solution)/shard_map/all_gather | solution.py:78
  8.0 3.6 copy-start.19
  8.0 3.6 copy-start.20
  8.0 3.6 copy-start.21
  8.0 3.6 copy-start.22
  11.7 37.5 %copy-start.27 = (bf16[64,128]{1,0:T(8,128)(2,1)S(1)}, bf16[64,128]{1,0:T(8,128)(2,1)}, u32[]{:S(2)}) copy-start(bf16[64,128]{1,0:T(8,128)(2,1)} %param.18) | copy-start | bytes 49156
  11.7 37.5 %copy-start.30 = (s32[16]{0:T(128)S(1)}, s32[16]{0:T(128)}, u32[]{:S(2)}) copy-start(s32[16]{0:T(128)} %param.14) | copy-start | bytes 196
  11.7 37.7 %copy-start.28 = (bf16[64,128]{1,0:T(8,128)(2,1)S(1)}, bf16[64,128]{1,0:T(8,128)(2,1)}, u32[]{:S(2)}) copy-start(bf16[64,128]{1,0:T(8,128)(2,1)} %param.19) | copy-start | bytes 49156
  32.3 19.4 %copy-start.12 = (f32[4096]{0:T(1024)}, f32[4096]{0:T(1024)S(1)}, u32[]{:S(2)}) copy-start(f32[4096]{0:T(1024)S(1)} %broadcast_multiply_fusion) | copy-start | bytes 49156
  51.7 235.8 %reduce-scatter.3.cloned.1.call-start = ((), (), s32[]{:S(2)}) async-start(), calls=%async_computation.3 | async-start | bytes 10485760 | tf_op jit(solution)/shard_map/reduce_scatter | solution.py:82
  51.7 87.1 %copy-start.11 = (bf16[384,512]{1,0:T(8,128)(2,1)S(1)}, bf16[384,512]{1,0:T(8,128)(2,1)}, u32[]{:S(2)}) copy-start(bf16[384,512]{1,0:T(8,128)(2,1)} %param.22) | copy-start | bytes 1179652
  144.5 143.0 %copy-start.5 = (bf16[16,256,128]{2,1,0:T(8,128)(2,1)S(1)}, bf16[16,256,128]{2,1,0:T(8,128)(2,1)}, u32[]{:S(2)}) copy-start(bf16[16,256,128]{2,1,0:T(8,128)(2,1)} %param.13) | copy-start | bytes 3145732
  144.5 228.2 %all-gather.5.cloned.1.call-start = ((), (), s32[]{:S(2)}) async-start(), calls=%async_computation.4 | async-start | bytes 5242880 | tf_op jit(solution)/shard_map/all_gather | solution.py:97
  291.4 239.0 %reduce-scatter.5.cloned.1.call-start = ((), (), s32[]{:S(2)}) async-start(), calls=%async_computation.5 | async-start | bytes 10485760 | tf_op jit(solution)/shard_map/reduce_scatter | solution.py:105
  387.4 206.9 %all-reduce.10.cloned.1.call-start = ((), (), s32[]{:S(2)}) async-start(), calls=%async_computation.7 | async-start | bytes 3145728 | tf_op jit(solution)/shard_map/psum | solution.py:136
  387.7 6.0 copy-start.9
  387.7 6.1 copy-start.26
  397.0 253.6 %all-reduce.8.cloned.1.call-start = ((), (), s32[]{:S(2)}) async-start(), calls=%async_computation.6 | async-start | bytes 146432 | tf_op jit(solution)/shard_map/psum | solution.py:136
  554.9 4.8 copy-start.2
  562.2 5.7 copy-start.6
  594.4 64.6 %copy-start.10 = (f32[384,512]{1,0:T(8,128)S(1)}, f32[384,512]{1,0:T(8,128)}, u32[]{:S(2)}) copy-start(f32[384,512]{1,0:T(8,128)} %get-tuple-element.65) | copy-start | bytes 2359300
  650.5 9.3 %copy-start.33 = (f32[128]{0:T(128)S(1)}, f32[128]{0:T(128)}, u32[]{:S(2)}) copy-start(f32[128]{0:T(128)} %get-tuple-element.66) | copy-start | bytes 1540
  650.6 9.8 %copy-start.32 = (f32[128]{0:T(128)S(1)}, f32[128]{0:T(128)}, u32[]{:S(2)}) copy-start(f32[128]{0:T(128)} %get-tuple-element.67) | copy-start | bytes 1540
  (16 other events, 38.3 us)
Sparse Core Ops, SparseCore 0:
  51.8 79.0 all-gather.2
  144.6 142.8 reduce-scatter.2
  291.5 81.1 all-gather.4
  387.6 142.7 reduce-scatter.4
  534.7 59.6 all-reduce.9
  599.3 51.1 all-reduce.7
where the time goes:
time: 669 us; the launch traced here: 668 us
  waiting for transfers between devices  505 us (75%)
  blocking collectives  55.4 us (8%)
  other arithmetic  38.3 us (6%)
  matrix products  36.9 us (6%)
  local copies, waits for them, and re-layouts  16 us (2%)
  between operations  15.2 us (2%)
    reduce_scatter x1, waiting for transfers between devices, per_device(): lax.psum_scatter(partial_out, 'chan', scatter_dimension=1, tiled=True)  139 us
    reduce_scatter x1, waiting for transfers between devices, per_device(): lax.psum_scatter(norm_part, 'chan', scatter_dimension=1, tiled=True)  133 us
    all_gather x1, waiting for transfers between devices, per_device(): branch_all = lax.all_gather(branch_low, 'chan', axis=1, tiled=True)  81.2 us
    all_gather x1, waiting for transfers between devices, per_device(): norm_all = lax.all_gather(norm_low, 'chan', axis=1, tiled=True)  79.1 us
    psum x2, waiting for transfers between devices, per_device(): lax.psum((grad_kernel, grad_conv_b, grad_scale_tab, grad_shift_tab, grad_...  72.5 us
    dot_general x4, matrix products, contract(): lax.dot_general(left, right, (((left_dim,), (right_dim,)), ((), ())), pre...  22.2 us
    psum x1, blocking collectives, per_device(): row_sum = lax.psum(jnp.sum(conv_flat, 1), 'chan')  20.5 us
    psum x1, blocking collectives, per_device(): lax.psum(jnp.sum(grad_normed * normed, 1).astype(jnp.bfloat16), 'chan')  19.3 us
  transfers between devices with their start and end apart: 6, of which 6 were waited for; matrix products, arithmetic and copies ran while one was open for 6% of the time, Pallas kernels for 0%

commit v1 on v0

v1 whole, which is shorter than its diff:
```python
import functools

import jax
import jax.numpy as jnp
from jax import lax
from jax.experimental import pallas as pl
from jax.experimental.pallas import tpu as pltpu
from jax.sharding import PartitionSpec as P

CHUNKS = 1

EPS = 1e-06
ROOT_TWO_PI = 2.5066282746310002
F32 = jnp.float32
BF16 = jnp.bfloat16
PAD = 8


def gelu_pair(v):
    z = jnp.abs(v)
    t = 1.0 / (1.0 + (0.3275911 * 0.7071067811865476) * z)
    e = jnp.exp(v * v * -0.5)
    poly = t * (0.5 * 0.254829592 + t * (0.5 * -0.284496736 + t * (0.5 * 1.421413741 + t * (0.5 * -1.453152027 + t * (0.5 * 1.061405429)))))
    tail = poly * e
    cdf = jnp.where(v >= 0.0, 1.0 - tail, tail)
    return v * cdf, cdf + v * (e * (1.0 / ROOT_TWO_PI))


def dot(a, b, ca, cb):
    return lax.dot_general(a, b, (((ca,), (cb,)), ((), ())), preferred_element_type=F32)


def body(n_blocks, taps, speakers, first,
         order_ref, spk_ref, live_ref, *refs):
    nb = n_blocks
    p = refs[:nb]
    prm, w_in, w_out = refs[nb:nb + 3]
    k = nb + 3
    if not first:
        got = refs[k:k + 3]
        k += 3
    o = refs[k:k + nb]
    gwi, gwo, gsm, grow = refs[k + nb:k + nb + 4]
    (xpad, gpad, normed, nlow, blow, act, slope, plow, wide, b_in) = refs[k + nb + 4:]
    i = pl.program_id(0)
    length, lanes = normed.shape[1], normed.shape[2]
    width = nb * lanes
    ff = act.shape[1]
    per = ff // nb
    margin = taps // 2
    r_conv, r_cb = 2 * speakers, 2 * speakers + taps
    r_bo, r_ls, r_bi = r_cb + 1, r_cb + 2, r_cb + 3
    cols = [pl.multiple_of(order_ref[d] * lanes, lanes) for d in range(nb)]

    @pl.when(i == 0)
    def _():
        for d in range(nb):
            zero = jnp.zeros((PAD, lanes), F32)
            xpad[d, 0:PAD, :] = zero
            xpad[d, PAD + length:, :] = zero
            gpad[d, 0:PAD, :] = zero
            gpad[d, PAD + length:, :] = zero
            for r in range(per // lanes):
                at = pl.multiple_of(order_ref[d] * per + r * lanes, lanes)
                b_in[:, pl.ds(at, lanes)] = prm[d, r_bi + r:r_bi + r + 1, :]
        if first:
            gwi[...] = jnp.zeros_like(gwi)
            gwo[...] = jnp.zeros_like(gwo)
            gsm[...] = jnp.zeros_like(gsm)
        else:
            gwi[...] = got[0][...]
            gwo[...] = got[1][...]
            gsm[...] = got[2][...]

    spk = spk_ref[i]
    live = live_ref[i].astype(F32)
    total = jnp.zeros((length, 1), F32)
    for d in range(nb):
        xpad[d, PAD:PAD + length, :] = p[d][0, 0].astype(F32)
        acc = jnp.broadcast_to(prm[d, r_cb:r_cb + 1, :], (length, lanes))
        for t in range(taps):
            s = PAD - margin + t
            acc = acc + prm[d, r_conv + t:r_conv + t + 1, :] * xpad[d, s:s + length, :]
        normed[d] = acc
        total = total + jnp.sum(acc, 1, keepdims=True)
    mean = total / width
    square = jnp.zeros((length, 1), F32)
    for d in range(nb):
        c = normed[d] - mean
        normed[d] = c
        square = square + jnp.sum(c * c, 1, keepdims=True)
    inv = lax.rsqrt(square / width + EPS)
    for d in range(nb):
        v = normed[d] * inv
        normed[d] = v
        sc = prm[d, pl.ds(spk, 1), :]
        sh = prm[d, pl.ds(speakers + spk, 1), :]
        nlow[:, pl.ds(cols[d], lanes)] = (v * sc + sh).astype(BF16)

    step = 256
    for f in range(0, ff, step):
        pre = dot(nlow[...], w_in[:, f:f + step], 1, 0) + b_in[:, f:f + step]
        a, s = gelu_pair(pre)
        act[:, f:f + step] = a.astype(BF16)
        slope[:, f:f + step] = s
    wide[...] = dot(act[...], w_out[...], 1, 0)
    for d in range(nb):
        b = wide[:, pl.ds(cols[d], lanes)] + prm[d, r_bo:r_bo + 1, :]
        ls = prm[d, r_ls:r_ls + 1, :] * live
        x = p[d][0, 0].astype(F32)
        g = p[d][1, 0].astype(F32)
        o[d][0, 0] = (x + b * ls).astype(BF16)
        gb = g * ls
        gsm[d, taps + 1:taps + 2, :] += jnp.sum(gb, 0, keepdims=True)
        gsm[d, taps + 2:taps + 3, :] += jnp.sum(g * b, 0, keepdims=True) * live
        blow[:, pl.ds(cols[d], lanes)] = gb.astype(BF16)
    for f in range(0, ff, step):
        gp = dot(blow[...], w_out[f:f + step, :], 1, 1) * slope[:, f:f + step]
        low = gp.astype(BF16)
        plow[:, f:f + step] = low
        at = f // lanes
        gsum = jnp.sum(gp, 0, keepdims=True)
        for r in range(step // lanes):
            q = (f + r * lanes) // lanes
            row = taps + 3 + q % (per // lanes)
            gsm[q // (per // lanes) + nb, row:row + 1, :] += gsum[:, r * lanes:(r + 1) * lanes]
        da = dot(nlow[...], low, 0, 0)
        db = dot(blow[...], act[:, f:f + step], 0, 0)
        for r in range(step // lanes):
            gwi[at + r] += da[:, r * lanes:(r + 1) * lanes]
            gwo[at + r] += db[:, r * lanes:(r + 1) * lanes]
    wide[...] = dot(plow[...], w_in[...], 1, 1)
    m1 = jnp.zeros((length, 1), F32)
    m2 = jnp.zeros((length, 1), F32)
    for d in range(nb):
        gn = wide[:, pl.ds(cols[d], lanes)]
        v = normed[d]
        gv = gn * v
        grow[d, pl.ds(i, 1), :] = jnp.sum(gv, 0, keepdims=True)
        grow[d + nb, pl.ds(i, 1), :] = jnp.sum(gn, 0, keepdims=True)
        sc = prm[d, pl.ds(spk, 1), :]
        m1 = m1 + jnp.sum(gn * sc, 1, keepdims=True)
        m2 = m2 + jnp.sum(gv * sc, 1, keepdims=True)
    m1 = m1 / width
    m2 = m2 / width
    for d in range(nb):
        sc = prm[d, pl.ds(spk, 1), :]
        gc = (wide[:, pl.ds(cols[d], lanes)] * sc - m1 - normed[d] * m2) * inv
        gpad[d, PAD:PAD + length, :] = gc
        gsm[d, taps:taps + 1, :] += jnp.sum(gc, 0, keepdims=True)
        acc = jnp.zeros((length, lanes), F32)
        for t in range(taps):
            s = PAD - margin + t
            gsm[d, t:t + 1, :] += jnp.sum(xpad[d, s:s + length, :] * gc, 0, keepdims=True)
            s = PAD + margin - t
            acc = acc + prm[d, r_conv + t:r_conv + t + 1, :] * gpad[d, s:s + length, :]
        o[d][1, 0] = acc.astype(BF16)


def block_call(order, spk, live, packed, prm, w_in, w_out, taps, speakers, carried=None):
    nb = len(packed)
    _, n, length, lanes = packed[0].shape
    width = nb * lanes
    ff = w_in.shape[1]
    rows = 16
    first = carried is None
    full = lambda shape: pl.BlockSpec(shape, lambda i, *_: (0,) * len(shape), pipeline_mode=pl.Buffered(1))
    fullo = lambda shape: pl.BlockSpec(shape, lambda i, *_: (0,) * len(shape))
    pspec = pl.BlockSpec((2, 1, length, lanes), lambda i, *_: (0, i, 0, 0))
    in_specs = [pspec] * nb + [full(prm.shape), full(w_in.shape), full(w_out.shape)]
    out_shape = [jax.ShapeDtypeStruct(packed[0].shape, BF16)] * nb + [
        jax.ShapeDtypeStruct((ff // lanes, width, lanes), F32),
        jax.ShapeDtypeStruct((ff // lanes, width, lanes), F32),
        jax.ShapeDtypeStruct((2 * nb, rows, lanes), F32),
        jax.ShapeDtypeStruct((2 * nb, max(8, n), lanes), F32),
    ]
    out_specs = [pspec] * nb + [fullo((ff // lanes, width, lanes)), fullo((ff // lanes, width, lanes)), fullo((2 * nb, rows, lanes)), fullo((2 * nb, max(8, n), lanes))]
    args = list(packed) + [prm, w_in, w_out]
    if not first:
        args += list(carried)
        in_specs += [full(v.shape) for v in carried]
    scratch = [
        pltpu.VMEM((nb, length + 2 * PAD, lanes), F32),
        pltpu.VMEM((nb, length + 2 * PAD, lanes), F32),
        pltpu.VMEM((nb, length, lanes), F32),
        pltpu.VMEM((length, width), BF16),
        pltpu.VMEM((length, width), BF16),
        pltpu.VMEM((length, ff), BF16),
        pltpu.VMEM((length, ff), F32),
        pltpu.VMEM((length, ff), BF16),
        pltpu.VMEM((length, width), F32),
        pltpu.VMEM((1, ff), F32),
    ]
    return pl.pallas_call(
        functools.partial(body, nb, taps, speakers, first),
        out_shape=out_shape,
        grid_spec=pltpu.PrefetchScalarGridSpec(
            num_scalar_prefetch=3, grid=(n,), in_specs=in_specs, out_specs=out_specs, scratch_shapes=scratch),
        cost_estimate=pl.CostEstimate(flops=12 * n * length * width * ff, transcendentals=2 * n * length * ff, bytes_accessed=16 * n * length * width),
        compiler_params=pltpu.CompilerParams(dimension_semantics=("arbitrary",), vmem_limit_bytes=50 << 20),
        name="block",
    )(order, spk, live, *args)


def ring(axis, size, shift):
    return lambda v: lax.ppermute(v, axis, [(i, (i + shift) % size) for i in range(size)])


def flip(axis, size, mask):
    return lambda v: lax.ppermute(v, axis, [(i, i ^ mask) for i in range(size)])


def stages(dp_count):
    low, out = 2, []
    while low < dp_count:
        out.append((low, min(4, dp_count // low)))
        low *= 4
    return out


def pick(v, index, axis=0):
    return lax.dynamic_index_in_dim(v, index, axis, keepdims=False)


def spread(pieces, indices, count):
    out = jnp.zeros((count,) + pieces[0].shape, pieces[0].dtype)
    for piece, index in zip(pieces, indices):
        out = lax.dynamic_update_index_in_dim(out, piece, index, 0)
    return out


def gather_dp(v, dp, dp_count):
    for low, count in stages(dp_count):
        here = (dp // low) % count
        v = spread([v] + [flip("dp", dp_count, low * m)(v) for m in range(1, count)],
                   [here] + [here ^ m for m in range(1, count)], count)
        v = v.reshape((-1,) + v.shape[2:]) if v.ndim > 4 else v
    core = dp % 2
    other = flip("dp", dp_count, 1)(v)
    return jnp.where(core == 0, jnp.stack([v, other], 1), jnp.stack([other, v], 1))


def per_device(clips_in, speaker, counts, conv_weight, conv_bias, scale_table, shift_table,
               w_in, b_in, w_out, b_out, layer_scale, grad_out):
    clip_num, length, lanes = clips_in.shape
    nb = lax.axis_size("chan")
    dp_count = lax.axis_size("dp")
    me = lax.axis_index("chan")
    dp = lax.axis_index("dp")
    speakers = scale_table.shape[0]
    taps = conv_weight.shape[0]
    per = w_in.shape[1]
    width, ff = nb * lanes, nb * per
    order = (me - jnp.arange(nb, dtype=jnp.int32)) % nb
    n = clip_num // nb // CHUNKS

    packed = []
    for k in range(CHUNKS):
        part = []
        for d in range(nb):
            at = (k * nb + (me + d) % nb) * n
            block = jnp.stack([lax.dynamic_slice_in_dim(clips_in, at, n), lax.dynamic_slice_in_dim(grad_out, at, n)])
            part.append(ring("chan", nb, d)(block) if d else block)
        packed.append(part)

    rows = [scale_table, shift_table, conv_weight, conv_bias[None], b_out[None], layer_scale[None], b_in.reshape(-1, lanes)]
    prm = jnp.concatenate(rows, 0)
    prm = jnp.pad(prm, ((0, -prm.shape[0] % 16), (0, 0)))
    prm = jnp.stack([prm] + [ring("chan", nb, d)(prm) for d in range(1, nb)]).astype(F32)

    ra, rb = width // dp_count, per // dp_count
    wa = lax.dynamic_slice_in_dim(w_in, dp * ra, ra).reshape(ra, per // lanes, lanes).transpose(1, 0, 2).reshape(-1, lanes)
    wb = lax.dynamic_slice_in_dim(w_out, dp * rb, rb).reshape(rb, nb, lanes).transpose(1, 0, 2).reshape(-1, lanes)
    share = jnp.concatenate([wa, wb])
    share = spread([share] + [ring("chan", nb, d)(share) for d in range(1, nb)],
                   [order[d] for d in range(nb)], nb)
    whole = gather_dp(share, dp, dp_count).reshape(dp_count, nb, -1, lanes)
    split = wa.shape[0]
    w_in_all = whole[:, :, :split].reshape(dp_count, nb, per // lanes, ra, lanes).transpose(0, 3, 1, 2, 4).reshape(width, ff)
    w_out_all = whole[:, :, split:].reshape(dp_count, nb, nb, rb, lanes).transpose(1, 0, 3, 2, 4).reshape(ff, width)

    carried = None
    back = []
    scale_rows, shift_rows, hots = [], [], []
    for k in range(CHUNKS):
        slots = (k * nb + me) * n + jnp.arange(n)
        spk = lax.dynamic_slice_in_dim(speaker, (k * nb + me) * n, n)
        live = (slots < counts[0]).astype(jnp.int32)
        out = block_call(order, spk, live, packed[k], prm, w_in_all, w_out_all, taps, speakers, carried)
        carried = out[nb:nb + 3]
        grow = out[nb + 3]
        hots.append((spk[:, None] == jnp.arange(speakers)[None]).astype(F32))
        scale_rows.append(grow[:nb, :n])
        shift_rows.append(grow[nb:, :n])
        back.append([out[0]] + [ring("chan", nb, -d)(out[d]) for d in range(1, nb)])

    clips_out = jnp.zeros(clips_in.shape, BF16)
    grad_clips = grad_out.astype(F32)
    for k in range(CHUNKS):
        for d in range(nb):
            at = (k * nb + (me + d) % nb) * n
            clips_out = lax.dynamic_update_slice_in_dim(clips_out, back[k][d][0], at, 0)
            g = lax.dynamic_slice_in_dim(grad_out, at, n).astype(F32) + back[k][d][1].astype(F32)
            grad_clips = lax.dynamic_update_slice_in_dim(grad_clips, g, at, 0)

    gwi, gwo, gsm = carried
    hot = jnp.concatenate(hots)
    table = lambda r: jnp.einsum("ns,dnl->dsl", hot, jnp.concatenate(r, 1), precision=lax.Precision.HIGHEST)
    inverse = lambda v: jnp.take(v, order, axis=0)
    small = jnp.concatenate([inverse(table(scale_rows)), inverse(table(shift_rows)), inverse(gsm[:nb]) + gsm[nb:]], 1)
    used = small.shape[1]
    unit = dp_count * 16
    small = jnp.pad(small, ((0, 0), (0, -used % unit), (0, 0)))
    sizes = [gwi.shape[0] // nb * gwi.shape[1], gwo.shape[0] // nb * gwo.shape[1], small.shape[1]]
    parts = [v.reshape(nb, dp_count // 2, 2, -1, lanes) for v in (gwi, gwo, small)]
    core = dp % 2
    mine = jnp.concatenate([pick(v, core, 2) for v in parts], 2)
    other = jnp.concatenate([pick(v, 1 - core, 2) for v in parts], 2).astype(BF16)
    total = mine + flip("dp", dp_count, 1)(other).astype(F32)
    for low, count in reversed(stages(dp_count)):
        here = (dp // low) % count
        v = total.reshape(nb, count, -1, total.shape[-2], lanes)
        total = pick(v, here, 1)
        for m in range(1, count):
            total = total + flip("dp", dp_count, low * m)(pick(v, here ^ m, 1).astype(BF16)).astype(F32)
    v = total.reshape(nb, -1, lanes)
    total = pick(v, me)
    for d in range(1, nb):
        total = total + ring("chan", nb, d)(pick(v, (me + d) % nb).astype(BF16)).astype(F32)
    whole = gather_dp(total.astype(BF16)[None], dp, dp_count).reshape(dp_count, -1, lanes).astype(F32)
    cut = [s // dp_count for s in sizes]
    g_in = whole[:, :cut[0]].reshape(per // lanes, width, lanes).transpose(1, 0, 2).reshape(width, per)
    g_out = whole[:, cut[0]:cut[0] + cut[1]].reshape(per // lanes, width, lanes).transpose(0, 2, 1).reshape(per, width)
    small = whole[:, cut[0] + cut[1]:].reshape(-1, lanes)
    at = 2 * speakers
    return (
        clips_out,
        grad_clips,
        small[at:at + taps],
        small[at + taps],
        small[:speakers],
        small[speakers:at],
        g_in,
        small[at + taps + 3:at + taps + 3 + per // lanes].reshape(per),
        g_out,
        small[at + taps + 1],
        small[at + taps + 2],
    )


def solution(mesh):
    act = P("dp", None, "chan")
    col, vec, row = P(None, "chan"), P("chan"), P("chan", None)
    in_specs = (act, P("dp"), P("dp"), col, vec, col, col, col, vec, row, vec, vec, act)
    out_specs = (act, act, col, vec, col, col, col, vec, row, vec, vec)
    return jax.shard_map(per_device, mesh=mesh, in_specs=in_specs, out_specs=out_specs, check_vma=False)
```

time: 669 us -> 213 us (0.32)
  waiting for transfers between devices: 505 us -> 84 us
  blocking collectives: 55.4 us -> 0 us
  matrix products: 36.9 us -> 0.64 us
  Pallas kernels: 0 us -> 32.4 us
  starting transfers between devices: 0.43 us -> 32.5 us
  other arithmetic: 38.3 us -> 13.1 us
  local copies, waits for them, and re-layouts: 16 us -> 39.8 us
    reduce_scatter x2 -> x0, waiting for transfers between devices: 272 us -> none  [the longest x1 139 us: per_device(): lax.psum_scatter(partial_out, 'chan', scatter_dimension=1, tiled=True)]
    all_gather x2 -> x0, waiting for transfers between devices: 160 us -> none  [the longest x1 81.2 us: per_device(): branch_all = lax.all_gather(branch_low, 'chan', axis=1, tiled=True)]
    ppermute x0 -> x27, waiting for transfers between devices: none -> 84 us  [the longest x15 65.1 us: ring(): lax.ppermute(v, axis, [(i, (i + shift) % size) for i in range(size)])]
    psum x2 -> x0, waiting for transfers between devices: 72.5 us -> none  [per_device(): lax.psum((grad_kernel, grad_conv_b, grad_scale_tab, grad_shift_tab, grad_...]
    psum x3 -> x0, blocking collectives: 55.4 us -> none  [the longest x1 20.5 us: per_device(): row_sum = lax.psum(jnp.sum(conv_flat, 1), 'chan')]
    dot_general x10 -> x2, matrix products: 36.9 us -> 0.64 us  [per_device(): jnp.einsum('ns,dnl->dsl', hot, jnp.concatenate(r, 1), precision=lax.Preci...]
    ppermute x0 -> x27, starting transfers between devices: none -> 32.5 us  [the longest x15 21.5 us: ring(): lax.ppermute(v, axis, [(i, (i + shift) % size) for i in range(size)])]
    pallas_call x0 -> x1, Pallas kernels: none -> 32.4 us  [block_call(): pl.pallas_call(functools.partial(body, nb, taps, speakers, first), out_sh...]
  transfers between devices with their start and end apart: 6 -> 27, of which waited for: 6 -> 11; matrix products, arithmetic and copies ran while one was open for 6% -> 15% of each run, Pallas kernels for 0% -> 0%
where the time goes in v1:
time: 213 us; the launch traced here: 212 us
  waiting for transfers between devices  84 us (39%)
  local copies, waits for them, and re-layouts  39.8 us (19%)
  starting transfers between devices  32.5 us (15%)
  Pallas kernels  32.4 us (15%)
  other arithmetic  13.1 us (6%)
  between operations  9.75 us (5%)
    ppermute x15, waiting for transfers between devices, ring(): lax.ppermute(v, axis, [(i, (i + shift) % size) for i in range(size)])  65.1 us
    pallas_call x1, Pallas kernels, block_call(): pl.pallas_call(functools.partial(body, nb, taps, speakers, first), out_sh...  32.4 us
    ppermute x15, starting transfers between devices, ring(): lax.ppermute(v, axis, [(i, (i + shift) % size) for i in range(size)])  21.5 us
    ppermute x12, waiting for transfers between devices, flip(): return lambda v: lax.ppermute(v, axis, [(i, i ^ mask) for i in range(size)])  18.9 us
    ppermute x12, starting transfers between devices, flip(): return lambda v: lax.ppermute(v, axis, [(i, i ^ mask) for i in range(size)])  10.9 us
    unnamed x50, local copies, waits for them, and re-layouts  9.44 us
    reshape x1, local copies, waits for them, and re-layouts, per_device(): whole[:, :, :split].reshape(dp_count, nb, per // lanes, ra, lanes)  5.09 us
    squeeze x6, local copies, waits for them, and re-layouts, pick(): return lax.dynamic_index_in_dim(v, index, axis, keepdims=False)  4.82 us
  transfers between devices with their start and end apart: 27, of which 11 were waited for; matrix products, arithmetic and copies ran while one was open for 15% of the time, Pallas kernels for 0%

profile of v1, /device:TPU:0, one launch (start us, length us, event | category | flops | bytes accessed | tf_op | source)
XLA Modules:
  0.0 212.1 jit_solution(13533026067879089690)
XLA Ops:
  2.6 3.1 %collective-permute-start.6 = (bf16[384,128]{1,0:T(8,128)(2,1)S(1)}, bf16[384,128]{1,0:T(8,128)(2,1)S(1)}, u32[]{:S(2)}, u32[]{:S(2)}) collective-permute-start(bf16[384,128]{1,0:T(8,128)(2,1)S(1)} %pad_maximum_fusion.5), channel_id=1, source_target_pairs={{0,1},{1,2},{2,3},{3,0},{4,5},{5,6},{6,7},{7,4},{8,9},{9,10},{10,1... | collective-permute-start | bytes 294920 | tf_op jit(solution)/shard_map/ppermute | solution.py:206
  5.7 2.6 %collective-permute-start.7 = (bf16[384,128]{1,0:T(8,128)(2,1)S(1)}, bf16[384,128]{1,0:T(8,128)(2,1)S(1)}, u32[]{:S(2)}, u32[]{:S(2)}) collective-permute-start(bf16[384,128]{1,0:T(8,128)(2,1)S(1)} %pad_maximum_fusion.5), channel_id=1, source_target_pairs={{0,2},{1,3},{2,0},{3,1},{4,6},{5,7},{6,4},{7,5},{8,10},{9,11},{10,... | collective-permute-start | bytes 294920 | tf_op jit(solution)/shard_map/ppermute | solution.py:206
  24.2 6.1 %collective-permute-done.9 = bf16[4,384,128]{2,1,0:T(8,128)(2,1)S(1)} collective-permute-done((bf16[4,384,128]{2,1,0:T(8,128)(2,1)S(1)}, bf16[4,384,128]{2,1,0:T(8,128)(2,1)S(1)}, u32[]{:S(2)}, u32[]{:S(2)}) %collective-permute-start.9) | collective-permute-done | bytes 393248 | tf_op jit(solution)/shard_map/ppermute | solution.py:210
  31.0 7.1 %collective-permute-done.10 = bf16[4,384,128]{2,1,0:T(8,128)(2,1)S(1)} collective-permute-done((bf16[4,384,128]{2,1,0:T(8,128)(2,1)S(1)}, bf16[4,384,128]{2,1,0:T(8,128)(2,1)S(1)}, u32[]{:S(2)}, u32[]{:S(2)}) %collective-permute-start.10) | collective-permute-done | bytes 393248 | tf_op jit(solution)/shard_map/ppermute | solution.py:210
  41.3 2.8 %collective-permute-start.5 = (bf16[144,128]{1,0:T(8,128)(2,1)}, bf16[144,128]{1,0:T(8,128)(2,1)}, u32[]{:S(2)}, u32[]{:S(2)}) collective-permute-start(bf16[144,128]{1,0:T(8,128)(2,1)} %get-tuple-element.76), channel_id=1, source_target_pairs={{0,3},{1,0},{2,1},{3,2},{4,7},{5,4},{6,5},{7,6},{8,11},{9,8},{10,9... | collective-permute-start | bytes 110600 | tf_op jit(solution)/shard_map/ppermute | solution.py:206
  47.2 1.9 pad_maximum_fusion.3
  50.9 2.0 collective-permute-start
  53.8 3.6 %maximum_select_fusion = bf16[4,2,4,384,128]{4,3,2,1,0:T(8,128)(2,1)S(1)} fusion(bf16[4,1,4,384,128]{4,3,2,1,0:T(8,128)(2,1)} %bitcast.34, bf16[4,1,4,384,128]{4,3,2,1,0:T(8,128)(2,1)} %bitcast.33, pred[]{:T(512)S(6)} %eq.37), kind=kLoop, calls=%fused_computation.4 | loop fusion | flops 4718592 | bytes 6291457 | tf_op jit(solution)/shard_map/jit(_where)/select_n | solution.py:240
  58.8 2.7 %copy.42 = bf16[8,64,4,3,128]{4,3,2,1,0:T(4,128)(2,1)} copy(bf16[8,64,4,3,128]{4,1,3,2,0:T(8,128)(2,1)S(1)} %bitcast.187) | data formatting | bytes 3145728 | tf_op jit(solution)/shard_map/transpose | solution.py:279
  61.5 5.1 %reshape.209.refs_5_ = bf16[512,1536]{1,0:T(8,128)(2,1)} reshape(bf16[8,64,4,3,128]{4,3,2,1,0:T(4,128)(2,1)} %copy.42) | data formatting | bytes 3145728 | tf_op jit(solution)/shard_map/reshape | solution.py:279
  66.6 2.2 %copy.43 = bf16[4,8,48,4,128]{4,3,2,1,0:T(4,128)(2,1)S(1)} copy(bf16[4,8,48,4,128]{4,2,3,0,1:T(8,128)(2,1)} %bitcast.189) | data formatting | bytes 3145728 | tf_op jit(solution)/shard_map/transpose | solution.py:280
  70.2 22.9 %collective-permute-done.1.refs_2_ = bf16[2,4,256,128]{3,2,1,0:T(8,128)(2,1)S(1)} collective-permute-done((bf16[2,4,256,128]{3,2,1,0:T(8,128)(2,1)}, bf16[2,4,256,128]{3,2,1,0:T(8,128)(2,1)S(1)}, u32[]{:S(2)}, u32[]{:S(2)}) %collective-permute-start.1) | collective-permute-done | bytes 524320 | tf_op jit(solution)/shard_map/ppermute | solution.py:206
  96.8 32.4 %block.1 = (bf16[2,4,256,128]{3,2,1,0:T(8,128)(2,1)S(1)}, bf16[2,4,256,128]{3,2,1,0:T(8,128)(2,1)S(1)}, bf16[2,4,256,128]{3,2,1,0:T(8,128)(2,1)S(1)}, bf16[2,4,2...) custom-call(s32[4]{0:T(128)S(1)} %and_select_fusion.1.order_ref, ...), custom_call_target="tpu_custom_call" | custom-call | flops 9663676416 | bytes 8388608 | tf_op jit(solution)/shard_map/block/pallas_call | solution.py:194
  139.5 2.0 collective-permute-start.15
  144.8 1.9 maximum_add_fusion
  147.2 1.8 collective-permute-start.18
  149.0 5.2 %collective-permute-done.13 = bf16[2,4,256,128]{3,2,1,0:T(8,128)(2,1)S(1)} collective-permute-done((bf16[2,4,256,128]{3,2,1,0:T(8,128)(2,1)S(1)}, bf16[2,4,256,128]{3,2,1,0:T(8,128)(2,1)S(1)}, u32[]{:S(2)}, u32[]{:S(2)}) %collective-permute-start.13) | collective-permute-done | bytes 524320 | tf_op jit(solution)/shard_map/ppermute | solution.py:206
  155.8 29.8 %collective-permute-done.14 = bf16[2,4,256,128]{3,2,1,0:T(8,128)(2,1)S(1)} collective-permute-done((bf16[2,4,256,128]{3,2,1,0:T(8,128)(2,1)S(1)}, bf16[2,4,256,128]{3,2,1,0:T(8,128)(2,1)S(1)}, u32[]{:S(2)}, u32[]{:S(2)}) %collective-permute-start.14) | collective-permute-done | bytes 524320 | tf_op jit(solution)/shard_map/ppermute | solution.py:206
  186.1 3.7 %collective-permute-start.22 = (bf16[416,128]{1,0:T(8,128)(2,1)S(1)}, bf16[416,128]{1,0:T(8,128)(2,1)S(1)}, u32[]{:S(2)}, u32[]{:S(2)}) collective-permute-start(bf16[416,128]{1,0:T(8,128)(2,1)S(1)} %get-tuple-element.70), channel_id=1, source_target_pairs={{0,3},{1,0},{2,1},{3,2},{4,7},{5,4},{6,5},{7,6},{8,11},{9,8},{10,9... | collective-permute-start | bytes 319496 | tf_op jit(solution)/shard_map/ppermute | solution.py:206
  189.8 3.8 %collective-permute-done.20 = bf16[416,128]{1,0:T(8,128)(2,1)S(1)} collective-permute-done((bf16[416,128]{1,0:T(8,128)(2,1)S(1)}, bf16[416,128]{1,0:T(8,128)(2,1)S(1)}, u32[]{:S(2)}, u32[]{:S(2)}) %collective-permute-start.20) | collective-permute-done | bytes 106528 | tf_op jit(solution)/shard_map/ppermute | solution.py:206
  193.6 3.4 %collective-permute-done.21 = bf16[416,128]{1,0:T(8,128)(2,1)S(1)} collective-permute-done((bf16[416,128]{1,0:T(8,128)(2,1)S(1)}, bf16[416,128]{1,0:T(8,128)(2,1)S(1)}, u32[]{:S(2)}, u32[]{:S(2)}) %collective-permute-start.21) | collective-permute-done | bytes 106528 | tf_op jit(solution)/shard_map/ppermute | solution.py:206
  197.5 1.9 collective-permute-start.24
  202.7 2.3 %collective-permute-done.25 = bf16[1,416,128]{2,1,0:T(8,128)(2,1)S(1)} collective-permute-done((bf16[1,416,128]{2,1,0:T(8,128)(2,1)S(1)}, bf16[1,416,128]{2,1,0:T(8,128)(2,1)S(1)}, u32[]{:S(2)}, u32[]{:S(2)}) %collective-permute-start.25) | collective-permute-done | bytes 106528 | tf_op jit(solution)/shard_map/ppermute | solution.py:210
  205.2 1.6 collective-permute-done.26
  (165 shorter events, 50.6 us)
Async XLA Ops:
  2.6 15.5 %collective-permute-start.6 = (bf16[384,128]{1,0:T(8,128)(2,1)S(1)}, bf16[384,128]{1,0:T(8,128)(2,1)S(1)}, u32[]{:S(2)}, u32[]{:S(2)}) collective-permute-start(bf16[384,128]{1,0:T(8,128)(2,1)S(1)} %pad_maximum_fusion.5), channel_id=1, source_target_pairs={{0,1},{1,2},{2,3},{3,0},{4,5},{5,6},{6,7},{7,4},{8,9},{9,10},{10,1... | collective-permute-start | bytes 294920 | tf_op jit(solution)/shard_map/ppermute | solution.py:206
  5.7 12.4 %collective-permute-start.7 = (bf16[384,128]{1,0:T(8,128)(2,1)S(1)}, bf16[384,128]{1,0:T(8,128)(2,1)S(1)}, u32[]{:S(2)}, u32[]{:S(2)}) collective-permute-start(bf16[384,128]{1,0:T(8,128)(2,1)S(1)} %pad_maximum_fusion.5), channel_id=1, source_target_pairs={{0,2},{1,3},{2,0},{3,1},{4,6},{5,7},{6,4},{7,5},{8,10},{9,11},{10,... | collective-permute-start | bytes 294920 | tf_op jit(solution)/shard_map/ppermute | solution.py:206
  8.3 9.9 %collective-permute-start.8 = (bf16[384,128]{1,0:T(8,128)(2,1)S(1)}, bf16[384,128]{1,0:T(8,128)(2,1)S(1)}, u32[]{:S(2)}, u32[]{:S(2)}) collective-permute-start(bf16[384,128]{1,0:T(8,128)(2,1)S(1)} %pad_maximum_fusion.5), channel_id=1, source_target_pairs={{0,3},{1,0},{2,1},{3,2},{4,7},{5,4},{6,5},{7,6},{8,11},{9,8},{10,9... | collective-permute-start | bytes 294920 | tf_op jit(solution)/shard_map/ppermute | solution.py:206
  18.2 12.1 %collective-permute-start.9 = (bf16[4,384,128]{2,1,0:T(8,128)(2,1)S(1)}, bf16[4,384,128]{2,1,0:T(8,128)(2,1)S(1)}, u32[]{:S(2)}, u32[]{:S(2)}) collective-permute-start(bf16[4,384,128]{2,1,0:T(8,128)(2,1)S(1)} %bitcast_dynamic-update-slice_fusion.9), channel_id=1, source_target_pairs={{0,8},{4,12},{8,0},{12,4},{16,24},{20,28},{24,16},{28,20},{1,9},{5... | collective-permute-start | bytes 1179656 | tf_op jit(solution)/shard_map/ppermute | solution.py:210
  19.9 18.2 %collective-permute-start.10 = (bf16[4,384,128]{2,1,0:T(8,128)(2,1)S(1)}, bf16[4,384,128]{2,1,0:T(8,128)(2,1)S(1)}, u32[]{:S(2)}, u32[]{:S(2)}) collective-permute-start(bf16[4,384,128]{2,1,0:T(8,128)(2,1)S(1)} %bitcast_dynamic-update-slice_fusion.9), channel_id=1, source_target_pairs={{0,16},{4,20},{8,24},{12,28},{16,0},{20,4},{24,8},{28,12},{1,17},{... | collective-permute-start | bytes 1179656 | tf_op jit(solution)/shard_map/ppermute | solution.py:210
  21.5 17.4 %collective-permute-start.11 = (bf16[4,384,128]{2,1,0:T(8,128)(2,1)S(1)}, bf16[4,384,128]{2,1,0:T(8,128)(2,1)S(1)}, u32[]{:S(2)}, u32[]{:S(2)}) collective-permute-start(bf16[4,384,128]{2,1,0:T(8,128)(2,1)S(1)} %bitcast_dynamic-update-slice_fusion.9), channel_id=1, source_target_pairs={{0,24},{4,28},{8,16},{12,20},{16,8},{20,12},{24,0},{28,4},{1,25},{... | collective-permute-start | bytes 1179656 | tf_op jit(solution)/shard_map/ppermute | solution.py:210
  39.7 14.1 %collective-permute-start.12 = (bf16[4,4,384,128]{3,2,1,0:T(8,128)(2,1)}, bf16[4,4,384,128]{3,2,1,0:T(8,128)(2,1)}, u32[]{:S(2)}, u32[]{:S(2)}) collective-permute-start(bf16[4,4,384,128]{3,2,1,0:T(8,128)(2,1)} %bitcast_dynamic-update-slice_fusion), channel_id=1, source_target_pairs={{0,4},{4,0},{8,12},{12,8},{16,20},{20,16},{24,28},{28,24},{1,5},{5... | collective-permute-start | bytes 4718600 | tf_op jit(solution)/shard_map/ppermute | solution.py:210
  40.3 9.8 %collective-permute-start.3 = (bf16[144,128]{1,0:T(8,128)(2,1)}, bf16[144,128]{1,0:T(8,128)(2,1)}, u32[]{:S(2)}, u32[]{:S(2)}) collective-permute-start(bf16[144,128]{1,0:T(8,128)(2,1)} %get-tuple-element.76), channel_id=1, source_target_pairs={{0,1},{1,2},{2,3},{3,0},{4,5},{5,6},{6,7},{7,4},{8,9},{9,10},{10,1... | collective-permute-start | bytes 110600 | tf_op jit(solution)/shard_map/ppermute | solution.py:206
  41.0 9.9 %collective-permute-start.4 = (bf16[144,128]{1,0:T(8,128)(2,1)}, bf16[144,128]{1,0:T(8,128)(2,1)}, u32[]{:S(2)}, u32[]{:S(2)}) collective-permute-start(bf16[144,128]{1,0:T(8,128)(2,1)} %get-tuple-element.76), channel_id=1, source_target_pairs={{0,2},{1,3},{2,0},{3,1},{4,6},{5,7},{6,4},{7,5},{8,10},{9,11},{10,... | collective-permute-start | bytes 110600 | tf_op jit(solution)/shard_map/ppermute | solution.py:206
  41.3 11.6 %collective-permute-start.5 = (bf16[144,128]{1,0:T(8,128)(2,1)}, bf16[144,128]{1,0:T(8,128)(2,1)}, u32[]{:S(2)}, u32[]{:S(2)}) collective-permute-start(bf16[144,128]{1,0:T(8,128)(2,1)} %get-tuple-element.76), channel_id=1, source_target_pairs={{0,3},{1,0},{2,1},{3,2},{4,7},{5,4},{6,5},{7,6},{8,11},{9,8},{10,9... | collective-permute-start | bytes 110600 | tf_op jit(solution)/shard_map/ppermute | solution.py:206
  45.2 25.0 %collective-permute-start.2 = (bf16[2,4,256,128]{3,2,1,0:T(8,128)(2,1)S(1)}, bf16[2,4,256,128]{3,2,1,0:T(8,128)(2,1)}, u32[]{:S(2)}, u32[]{:S(2)}) collective-permute-start(bf16[2,4,256,128]{3,2,1,0:T(8,128)(2,1)S(1)} %pad_maximum_fusion.4), channel_id=1, source_target_pairs={{0,3},{1,0},{2,1},{3,2},{4,7},{5,4},{6,5},{7,6},{8,11},{9,8},{10,9... | collective-permute-start | bytes 1572872 | tf_op jit(solution)/shard_map/ppermute | solution.py:206
  50.1 43.0 %collective-permute-start.1 = (bf16[2,4,256,128]{3,2,1,0:T(8,128)(2,1)}, bf16[2,4,256,128]{3,2,1,0:T(8,128)(2,1)S(1)}, u32[]{:S(2)}, u32[]{:S(2)}) collective-permute-start(bf16[2,4,256,128]{3,2,1,0:T(8,128)(2,1)} %pad_maximum_fusion.3), channel_id=1, source_target_pairs={{0,2},{1,3},{2,0},{3,1},{4,6},{5,7},{6,4},{7,5},{8,10},{9,11},{10,... | collective-permute-start | bytes 1572872 | tf_op jit(solution)/shard_map/ppermute | solution.py:206
  50.9 43.0 %collective-permute-start = (bf16[2,4,256,128]{3,2,1,0:T(8,128)(2,1)}, bf16[2,4,256,128]{3,2,1,0:T(8,128)(2,1)S(1)}, u32[]{:S(2)}, u32[]{:S(2)}) collective-permute-start(bf16[2,4,256,128]{3,2,1,0:T(8,128)(2,1)} %pad_maximum_fusion.2), channel_id=1, source_target_pairs={{0,1},{1,2},{2,3},{3,0},{4,5},{5,6},{6,7},{7,4},{8,9},{9,10},{10,1... | collective-permute-start | bytes 1572872 | tf_op jit(solution)/shard_map/ppermute | solution.py:206
  137.1 7.7 %collective-permute-start.16 = (bf16[4,4,416,128]{3,2,1,0:T(8,128)(2,1)}, bf16[4,4,416,128]{3,2,1,0:T(8,128)(2,1)}, u32[]{:S(2)}, u32[]{:S(2)}) collective-permute-start(bf16[4,4,416,128]{3,2,1,0:T(8,128)(2,1)} %pad_maximum_fusion), channel_id=1, source_target_pairs={{0,4},{4,0},{8,12},{12,8},{16,20},{20,16},{24,28},{28,24},{1,5},{5... | collective-permute-start | bytes 5111816 | tf_op jit(solution)/shard_map/ppermute | solution.py:210
  138.9 15.4 %collective-permute-start.13 = (bf16[2,4,256,128]{3,2,1,0:T(8,128)(2,1)S(1)}, bf16[2,4,256,128]{3,2,1,0:T(8,128)(2,1)S(1)}, u32[]{:S(2)}, u32[]{:S(2)}) collective-permute-start(bf16[2,4,256,128]{3,2,1,0:T(8,128)(2,1)S(1)} %get-tuple-element.21), channel_id=1, source_target_pairs={{0,3},{1,0},{2,1},{3,2},{4,7},{5,4},{6,5},{7,6},{8,11},{9,8},{10,9... | collective-permute-start | bytes 1572872 | tf_op jit(solution)/shard_map/ppermute | solution.py:206
  138.9 46.7 %collective-permute-start.14 = (bf16[2,4,256,128]{3,2,1,0:T(8,128)(2,1)S(1)}, bf16[2,4,256,128]{3,2,1,0:T(8,128)(2,1)S(1)}, u32[]{:S(2)}, u32[]{:S(2)}) collective-permute-start(bf16[2,4,256,128]{3,2,1,0:T(8,128)(2,1)S(1)} %get-tuple-element.22), channel_id=1, source_target_pairs={{0,2},{1,3},{2,0},{3,1},{4,6},{5,7},{6,4},{7,5},{8,10},{9,11},{10,... | collective-permute-start | bytes 1572872 | tf_op jit(solution)/shard_map/ppermute | solution.py:206
  139.5 65.5 %collective-permute-start.15 = (bf16[2,4,256,128]{3,2,1,0:T(8,128)(2,1)S(1)}, bf16[2,4,256,128]{3,2,1,0:T(8,128)(2,1)S(1)}, u32[]{:S(2)}, u32[]{:S(2)}) collective-permute-start(bf16[2,4,256,128]{3,2,1,0:T(8,128)(2,1)S(1)} %get-tuple-element.23), channel_id=1, source_target_pairs={{0,1},{1,2},{2,3},{3,0},{4,5},{5,6},{6,7},{7,4},{8,9},{9,10},{10,1... | collective-permute-start | bytes 1572872 | tf_op jit(solution)/shard_map/ppermute | solution.py:206
  146.9 38.8 %collective-permute-start.17 = (bf16[4,1,416,128]{3,2,1,0:T(8,128)(2,1)S(1)}, bf16[4,1,416,128]{3,2,1,0:T(8,128)(2,1)S(1)}, u32[]{:S(2)}, u32[]{:S(2)}) collective-permute-start(bf16[4,1,416,128]{3,2,1,0:T(8,128)(2,1)S(1)} %get-tuple-element.52), channel_id=1, source_target_pairs={{0,8},{4,12},{8,0},{12,4},{16,24},{20,28},{24,16},{28,20},{1,9},{5... | collective-permute-start | bytes 1277960 | tf_op jit(solution)/shard_map/ppermute | solution.py:210
  147.2 38.4 %collective-permute-start.18 = (bf16[4,1,416,128]{3,2,1,0:T(8,128)(2,1)S(1)}, bf16[4,1,416,128]{3,2,1,0:T(8,128)(2,1)S(1)}, u32[]{:S(2)}, u32[]{:S(2)}) collective-permute-start(bf16[4,1,416,128]{3,2,1,0:T(8,128)(2,1)S(1)} %get-tuple-element.54), channel_id=1, source_target_pairs={{0,16},{4,20},{8,24},{12,28},{16,0},{20,4},{24,8},{28,12},{1,17},{... | collective-permute-start | bytes 1277960 | tf_op jit(solution)/shard_map/ppermute | solution.py:210
  154.2 31.4 %collective-permute-start.19 = (bf16[4,1,416,128]{3,2,1,0:T(8,128)(2,1)S(1)}, bf16[4,1,416,128]{3,2,1,0:T(8,128)(2,1)S(1)}, u32[]{:S(2)}, u32[]{:S(2)}) collective-permute-start(bf16[4,1,416,128]{3,2,1,0:T(8,128)(2,1)S(1)} %get-tuple-element.53), channel_id=1, source_target_pairs={{0,24},{4,28},{8,16},{12,20},{16,8},{20,12},{24,0},{28,4},{1,25},{... | collective-permute-start | bytes 1277960 | tf_op jit(solution)/shard_map/ppermute | solution.py:210
  185.9 7.7 %collective-permute-start.20 = (bf16[416,128]{1,0:T(8,128)(2,1)S(1)}, bf16[416,128]{1,0:T(8,128)(2,1)S(1)}, u32[]{:S(2)}, u32[]{:S(2)}) collective-permute-start(bf16[416,128]{1,0:T(8,128)(2,1)S(1)} %get-tuple-element.69), channel_id=1, source_target_pairs={{0,1},{1,2},{2,3},{3,0},{4,5},{5,6},{6,7},{7,4},{8,9},{9,10},{10,1... | collective-permute-start | bytes 319496 | tf_op jit(solution)/shard_map/ppermute | solution.py:206
  186.0 11.0 %collective-permute-start.21 = (bf16[416,128]{1,0:T(8,128)(2,1)S(1)}, bf16[416,128]{1,0:T(8,128)(2,1)S(1)}, u32[]{:S(2)}, u32[]{:S(2)}) collective-permute-start(bf16[416,128]{1,0:T(8,128)(2,1)S(1)} %get-tuple-element.71), channel_id=1, source_target_pairs={{0,2},{1,3},{2,0},{3,1},{4,6},{5,7},{6,4},{7,5},{8,10},{9,11},{10,... | collective-permute-start | bytes 319496 | tf_op jit(solution)/shard_map/ppermute | solution.py:206
  186.1 10.9 %collective-permute-start.22 = (bf16[416,128]{1,0:T(8,128)(2,1)S(1)}, bf16[416,128]{1,0:T(8,128)(2,1)S(1)}, u32[]{:S(2)}, u32[]{:S(2)}) collective-permute-start(bf16[416,128]{1,0:T(8,128)(2,1)S(1)} %get-tuple-element.70), channel_id=1, source_target_pairs={{0,3},{1,0},{2,1},{3,2},{4,7},{5,4},{6,5},{7,6},{8,11},{9,8},{10,9... | collective-permute-start | bytes 319496 | tf_op jit(solution)/shard_map/ppermute | solution.py:206
  199.4 5.6 %collective-permute-start.25 = (bf16[1,416,128]{2,1,0:T(8,128)(2,1)S(1)}, bf16[1,416,128]{2,1,0:T(8,128)(2,1)S(1)}, u32[]{:S(2)}, u32[]{:S(2)}) collective-permute-start(bf16[1,416,128]{2,1,0:T(8,128)(2,1)S(1)} %bitcast.214), channel_id=1, source_target_pairs={{0,24},{4,28},{8,16},{12,20},{16,8},{20,12},{24,0},{28,4},{1,25},{... | collective-permute-start | bytes 319496 | tf_op jit(solution)/shard_map/ppermute | solution.py:210
  (27 other events, 228.7 us)

commit v2 on v1

v2 whole, which is shorter than its diff:
```python
import functools

import jax
import jax.numpy as jnp
from jax import lax
from jax.experimental import pallas as pl
from jax.experimental.pallas import tpu as pltpu
from jax.sharding import PartitionSpec as P

SPLIT = (2, 2)
GROUP = 8

EPS = 1e-06
ROOT_TWO_PI = 2.5066282746310002
F32 = jnp.float32
BF16 = jnp.bfloat16
PAD = 8
HINT = 1 << 36


def gelu_pair(v):
    z = jnp.abs(v)
    t = 1.0 / (1.0 + (0.3275911 * 0.7071067811865476) * z)
    e = jnp.exp(v * v * -0.5)
    poly = t * (0.5 * 0.254829592 + t * (0.5 * -0.284496736 + t * (0.5 * 1.421413741 + t * (0.5 * -1.453152027 + t * (0.5 * 1.061405429)))))
    tail = poly * e
    cdf = jnp.where(v >= 0.0, 1.0 - tail, tail)
    return v * cdf, cdf + v * (e * (1.0 / ROOT_TWO_PI))


def dot(a, b, ca, cb):
    return lax.dot_general(a, b, (((ca,), (cb,)), ((), ())), preferred_element_type=F32)


def body(n_blocks, taps, speakers, small_rows, first, last,
         order_ref, spk_ref, live_ref, meta_ref, *refs):
    nb = n_blocks
    x0, g0 = refs[:2]
    p = refs[2:nb + 1]
    prm, w_in, w_out = refs[nb + 1:nb + 4]
    k = nb + 4
    if not first:
        got = refs[k:k + 3]
        k += 3
    o = refs[k:k + nb]
    k += nb
    if last:
        keep, send = refs[k:k + 2]
        gwi, gwo, gsm = refs[-3:]
        k += 2
    else:
        gwi, gwo, gsm = refs[k:k + 3]
        k += 3
    (xpad, gpad, normed, nlow, blow, act, slope, plow, wide, b_in) = refs[k:k + 10]
    i = pl.program_id(0)
    length, lanes = normed.shape[1], normed.shape[2]
    width = nb * lanes
    ff = act.shape[1]
    per = ff // nb
    tiles = per // lanes
    margin = taps // 2
    r_conv, r_cb = 2 * speakers, 2 * speakers + taps
    r_bo, r_ls, r_bi = r_cb + 1, r_cb + 2, r_cb + 3
    cols = [pl.multiple_of(order_ref[d] * lanes, lanes) for d in range(nb)]
    xs = [x0] + [q.at[0] for q in p]
    gs = [g0] + [q.at[1] for q in p]

    @pl.when(i == 0)
    def _():
        for d in range(nb):
            zero = jnp.zeros((PAD, lanes), F32)
            xpad[d, 0:PAD, :] = zero
            xpad[d, PAD + length:, :] = zero
            gpad[d, 0:PAD, :] = zero
            gpad[d, PAD + length:, :] = zero
            for r in range(tiles):
                at = pl.multiple_of(order_ref[d] * per + r * lanes, lanes)
                b_in[:, pl.ds(at, lanes)] = prm[d, r_bi + r:r_bi + r + 1, :]
        if first:
            gwi[...] = jnp.zeros_like(gwi)
            gwo[...] = jnp.zeros_like(gwo)
            gsm[...] = jnp.zeros_like(gsm)
        else:
            gwi[...] = got[0][...]
            gwo[...] = got[1][...]
            gsm[...] = got[2][...]

    spk = spk_ref[i]
    live = live_ref[i].astype(F32)
    total = jnp.zeros((length, 1), F32)
    for d in range(nb):
        xpad[d, PAD:PAD + length, :] = xs[d][0].astype(F32)
        acc = jnp.broadcast_to(prm[d, r_cb:r_cb + 1, :], (length, lanes))
        for t in range(taps):
            s = PAD - margin + t
            acc = acc + prm[d, r_conv + t:r_conv + t + 1, :] * xpad[d, s:s + length, :]
        normed[d] = acc
        total = total + jnp.sum(acc, 1, keepdims=True)
    mean = total / width
    square = jnp.zeros((length, 1), F32)
    for d in range(nb):
        c = normed[d] - mean
        normed[d] = c
        square = square + jnp.sum(c * c, 1, keepdims=True)
    inv = lax.rsqrt(square / width + EPS)
    for d in range(nb):
        v = normed[d] * inv
        normed[d] = v
        sc = prm[d, pl.ds(spk, 1), :]
        sh = prm[d, pl.ds(speakers + spk, 1), :]
        nlow[:, pl.ds(cols[d], lanes)] = (v * sc + sh).astype(BF16)

    step = 256
    for f in range(0, ff, step):
        pre = dot(nlow[...], w_in[:, f:f + step], 1, 0) + b_in[:, f:f + step]
        a, s = gelu_pair(pre)
        act[:, f:f + step] = a.astype(BF16)
        slope[:, f:f + step] = s
    wide[...] = dot(act[...], w_out[...], 1, 0)
    for d in range(nb):
        b = wide[:, pl.ds(cols[d], lanes)] + prm[d, r_bo:r_bo + 1, :]
        ls = prm[d, r_ls:r_ls + 1, :] * live
        x = xs[d][0].astype(F32)
        g = gs[d][0].astype(F32)
        o[d][0, 0] = (x + b * ls).astype(BF16)
        gb = g * ls
        gsm[d, r_bo:r_bo + 1, :] += jnp.sum(gb, 0, keepdims=True)
        gsm[d, r_ls:r_ls + 1, :] += jnp.sum(g * b, 0, keepdims=True) * live
        blow[:, pl.ds(cols[d], lanes)] = gb.astype(BF16)
    for f in range(0, ff, step):
        gp = dot(blow[...], w_out[f:f + step, :], 1, 1) * slope[:, f:f + step]
        low = gp.astype(BF16)
        plow[:, f:f + step] = low
        at = f // lanes
        gsum = jnp.sum(gp, 0, keepdims=True)
        for r in range(step // lanes):
            q = at + r
            gsm[nb, q:q + 1, :] += gsum[:, r * lanes:(r + 1) * lanes]
        da = dot(nlow[...], low, 0, 0)
        for r in range(step // lanes):
            gwi[at + r] += da[:, r * lanes:(r + 1) * lanes]
        gwo[f:f + step, :] += dot(act[:, f:f + step], blow[...], 0, 0)
    wide[...] = dot(plow[...], w_in[...], 1, 1)
    m1 = jnp.zeros((length, 1), F32)
    m2 = jnp.zeros((length, 1), F32)
    for d in range(nb):
        gn = wide[:, pl.ds(cols[d], lanes)]
        v = normed[d]
        gv = gn * v
        gsm[d, pl.ds(spk, 1), :] += jnp.sum(gv, 0, keepdims=True)
        gsm[d, pl.ds(speakers + spk, 1), :] += jnp.sum(gn, 0, keepdims=True)
        sc = prm[d, pl.ds(spk, 1), :]
        m1 = m1 + jnp.sum(gn * sc, 1, keepdims=True)
        m2 = m2 + jnp.sum(gv * sc, 1, keepdims=True)
    m1 = m1 / width
    m2 = m2 / width
    for d in range(nb):
        sc = prm[d, pl.ds(spk, 1), :]
        gc = (wide[:, pl.ds(cols[d], lanes)] * sc - m1 - normed[d] * m2) * inv
        gpad[d, PAD:PAD + length, :] = gc
        gsm[d, r_cb:r_cb + 1, :] += jnp.sum(gc, 0, keepdims=True)
        acc = jnp.zeros((length, lanes), F32)
        for t in range(taps):
            s = PAD - margin + t
            gsm[d, r_conv + t:r_conv + t + 1, :] += jnp.sum(xpad[d, s:s + length, :] * gc, 0, keepdims=True)
            s = PAD + margin - t
            acc = acc + prm[d, r_conv + t:r_conv + t + 1, :] * gpad[d, s:s + length, :]
        o[d][1, 0] = acc.astype(BF16)

    if last:
        @pl.when(i == pl.num_programs(0) - 1)
        def _():
            place = meta_ref[1]
            ra, rb, rs = width // GROUP, per // GROUP, small_rows // GROUP
            for d in range(nb):
                c = order_ref[d]
                for r in range(tiles):
                    gsm[d, r_bi + r:r_bi + r + 1, :] = gsm[nb, pl.ds(c * tiles + r, 1), :]

            def emit(m, carry):
                for e in range(nb):
                    d = -e % nb
                    c = order_ref[d]
                    for out, part in ((keep, place ^ (2 * m)), (send, place ^ (2 * m) ^ 1)):
                        for r in range(tiles):
                            v = gwi[c * tiles + r, pl.ds(pl.multiple_of(part * ra, ra), ra), :]
                            out[m, e, r * ra:(r + 1) * ra, :] = v.astype(out.dtype)
                        base = tiles * ra
                        for r in range(nb):
                            v = gwo[pl.ds(pl.multiple_of(c * per + part * rb, 16), rb), r * lanes:(r + 1) * lanes]
                            out[m, e, base + r * rb:base + (r + 1) * rb, :] = v.astype(out.dtype)
                        base += nb * rb
                        v = gsm[d, pl.ds(pl.multiple_of(part * rs, rs), rs), :]
                        out[m, e, base:base + rs, :] = v.astype(out.dtype)
                return carry
            lax.fori_loop(0, GROUP // 2, emit, 0)


def block_call(order, spk, live, meta, clips, grads, packed, prm, w_in, w_out, taps, speakers, small_rows, carried, last):
    nb = len(packed) + 1
    _, n, length, lanes = packed[0].shape
    width = nb * lanes
    ff = w_in.shape[1]
    per = ff // nb
    first = carried is None
    full = lambda shape: pl.BlockSpec(shape, lambda i, *_: (0,) * len(shape), pipeline_mode=pl.Buffered(1))
    fullo = lambda shape: pl.BlockSpec(shape, lambda i, *_: (0,) * len(shape))
    pspec = pl.BlockSpec((2, 1, length, lanes), lambda i, *_: (0, i, 0, 0))
    own = pl.BlockSpec((1, length, lanes), lambda i, order, spk, live, meta: (meta[0] + i, 0, 0))
    in_specs = [own, own] + [pspec] * (nb - 1) + [full(prm.shape), full(w_in.shape), full(w_out.shape)]
    sums = [(ff // lanes, width, lanes), (ff, width), (nb + 1, small_rows, lanes)]
    rows = (width // GROUP) * (per // lanes) + (per // GROUP) * nb + small_rows // GROUP
    out_shape = [jax.ShapeDtypeStruct(packed[0].shape, BF16)] * nb
    out_specs = [pspec] * nb
    if last:
        out_shape += [jax.ShapeDtypeStruct((GROUP // 2, nb, rows, lanes), t) for t in (F32, BF16)]
        out_specs += [fullo((GROUP // 2, nb, rows, lanes))] * 2
    else:
        out_shape += [jax.ShapeDtypeStruct(s, F32) for s in sums]
        out_specs += [fullo(s) for s in sums]
    args = [clips, grads] + list(packed) + [prm, w_in, w_out]
    if not first:
        args += list(carried)
        in_specs += [full(v.shape) for v in carried]
    scratch = [
        pltpu.VMEM((nb, length + 2 * PAD, lanes), F32),
        pltpu.VMEM((nb, length + 2 * PAD, lanes), F32),
        pltpu.VMEM((nb, length, lanes), F32),
        pltpu.VMEM((length, width), BF16),
        pltpu.VMEM((length, width), BF16),
        pltpu.VMEM((length, ff), BF16),
        pltpu.VMEM((length, ff), F32),
        pltpu.VMEM((length, ff), BF16),
        pltpu.VMEM((length, width), F32),
        pltpu.VMEM((1, ff), F32),
    ]
    if last:
        scratch += [pltpu.VMEM(s, F32) for s in sums]
    return pl.pallas_call(
        functools.partial(body, nb, taps, speakers, small_rows, first, last),
        out_shape=out_shape,
        grid_spec=pltpu.PrefetchScalarGridSpec(
            num_scalar_prefetch=4, grid=(n,), in_specs=in_specs, out_specs=out_specs, scratch_shapes=scratch),
        cost_estimate=pl.CostEstimate(flops=(HINT if last else 0), transcendentals=0, bytes_accessed=0),
        compiler_params=pltpu.CompilerParams(dimension_semantics=("arbitrary",), vmem_limit_bytes=56 << 20),
        name="block",
    )(order, spk, live, meta, *args)


def stack_body(count, rows, *refs):
    ins, (w, prm) = refs[:count], refs[count:]
    for d in range(count):
        w[d] = ins[d][0:rows, :]
        prm[d] = ins[d][rows:, :].astype(F32)


def stack_call(parts, rows, hint):
    total, lanes = parts[0].shape
    return pl.pallas_call(
        functools.partial(stack_body, len(parts), rows),
        out_shape=[jax.ShapeDtypeStruct((len(parts), rows, lanes), BF16),
                   jax.ShapeDtypeStruct((len(parts), total - rows, lanes), F32)],
        cost_estimate=pl.CostEstimate(flops=hint, transcendentals=0, bytes_accessed=0),
        name="gathered",
    )(*parts)


def whole_body(nb, ra, rb, tiles, lanes, order_ref, meta_ref, *refs):
    ins, (w_in, w_out) = [refs[s % 2].at[s // 2] for s in range(GROUP)], refs[2:]
    per = tiles * lanes
    for s in range(GROUP):
        part = meta_ref[1] ^ s

        def go(d, carry):
            c = order_ref[d]
            for r in range(tiles):
                w_in[pl.ds(pl.multiple_of(part * ra, ra), ra), pl.ds(pl.multiple_of(c * per + r * lanes, lanes), lanes)] = ins[s][d, r * ra:(r + 1) * ra, :]
            base = tiles * ra
            for r in range(nb):
                w_out[pl.ds(pl.multiple_of(c * per + part * rb, 16), rb), r * lanes:(r + 1) * lanes] = ins[s][d, base + r * rb:base + (r + 1) * rb, :]
            return carry
        lax.fori_loop(0, nb, go, 0)


def whole_call(order, meta, parts, ra, rb, tiles):
    _, nb, rows, lanes = parts[0].shape
    width, ff = nb * lanes, nb * tiles * lanes
    vm = pl.BlockSpec(memory_space=pltpu.VMEM)
    sm = pl.BlockSpec(memory_space=pltpu.SMEM)
    return pl.pallas_call(
        functools.partial(whole_body, nb, ra, rb, tiles, lanes),
        in_specs=[sm, sm] + [vm] * 2,
        out_specs=[vm, vm],
        out_shape=[jax.ShapeDtypeStruct((width, ff), BF16), jax.ShapeDtypeStruct((ff, width), BF16)],
        name="weights",
    )(order, meta, *parts)


def finish_body(nb, ra, rb, rs, tiles, lanes, taps, speakers, meta_ref, *refs):
    ins = [refs[s % 2].at[s // 2] for s in range(GROUP)]
    g_in, g_out, scale, shift, conv, cb, bo, ls, bi, small = refs[2:]
    for s in range(GROUP):
        part = meta_ref[1] ^ s
        for r in range(tiles):
            g_in[pl.ds(pl.multiple_of(part * ra, ra), ra), r * lanes:(r + 1) * lanes] = ins[s][r * ra:(r + 1) * ra, :].astype(F32)
        base = tiles * ra
        for r in range(nb):
            g_out[pl.ds(pl.multiple_of(part * rb, 16), rb), r * lanes:(r + 1) * lanes] = ins[s][base + r * rb:base + (r + 1) * rb, :].astype(F32)
        base += nb * rb
        small[pl.ds(pl.multiple_of(part * rs, rs), rs), :] = ins[s][base:base + rs, :].astype(F32)
    scale[...] = small[0:speakers, :]
    shift[...] = small[speakers:2 * speakers, :]
    at = 2 * speakers
    conv[...] = small[at:at + taps, :]
    at += taps
    cb[...] = small[at:at + 1, :]
    bo[...] = small[at + 1:at + 2, :]
    ls[...] = small[at + 2:at + 3, :]
    for r in range(tiles):
        bi[:, r * lanes:(r + 1) * lanes] = small[at + 3 + r:at + 4 + r, :]


def finish_call(meta, parts, nb, ra, rb, rs, tiles, taps, speakers):
    lanes = parts[0].shape[2]
    vm = pl.BlockSpec(memory_space=pltpu.VMEM)
    sm = pl.BlockSpec(memory_space=pltpu.SMEM)
    shapes = [(nb * lanes, tiles * lanes), (tiles * lanes, nb * lanes), (speakers, lanes), (speakers, lanes), (taps, lanes),
              (1, lanes), (1, lanes), (1, lanes), (1, tiles * lanes)]
    return pl.pallas_call(
        functools.partial(finish_body, nb, ra, rb, rs, tiles, lanes, taps, speakers),
        in_specs=[sm] + [vm] * 2,
        out_specs=[vm] * len(shapes),
        out_shape=[jax.ShapeDtypeStruct(s, F32) for s in shapes],
        scratch_shapes=[pltpu.VMEM((rs * GROUP, lanes), F32)],
        name="finish",
    )(meta, *parts)


def ring(axis, size, shift):
    return lambda v: lax.ppermute(v, axis, [(i, (i + shift) % size) for i in range(size)])


def flip(axis, size, mask):
    return lambda v: lax.ppermute(v, axis, [(i, i ^ mask) for i in range(size)])


def gather_group(v, dp_count, after=()):
    a, b = flip("dp", dp_count, 2)(v), flip("dp", dp_count, 4)(v)
    near = jnp.stack([v, a, b, flip("dp", dp_count, 4)(a)])
    near, *after = lax.optimization_barrier((near, *after))
    return [near, flip("dp", dp_count, 1)(near)], after


def per_device(clips_in, speaker, counts, conv_weight, conv_bias, scale_table, shift_table,
               w_in, b_in, w_out, b_out, layer_scale, grad_out):
    clip_num, length, lanes = clips_in.shape
    nb = lax.axis_size("chan")
    dp_count = lax.axis_size("dp")
    me = lax.axis_index("chan")
    dp = lax.axis_index("dp")
    speakers = scale_table.shape[0]
    taps = conv_weight.shape[0]
    per = w_in.shape[1]
    tiles = per // lanes
    width = nb * lanes
    order = (me - jnp.arange(nb, dtype=jnp.int32)) % nb
    place = dp % GROUP
    slots = clip_num // nb
    sizes = [slots * c // sum(SPLIT) for c in SPLIT]
    starts = [nb * sum(sizes[:k]) for k in range(len(sizes))]

    ra, rb = width // GROUP, per // GROUP
    wa = lax.dynamic_slice_in_dim(w_in, place * ra, ra).reshape(ra, tiles, lanes).transpose(1, 0, 2).reshape(-1, lanes)
    wb = lax.dynamic_slice_in_dim(w_out, place * rb, rb).reshape(rb, nb, lanes).transpose(1, 0, 2).reshape(-1, lanes)
    rows = [wa, wb, scale_table, shift_table, conv_weight, conv_bias[None], b_out[None], layer_scale[None], b_in.reshape(-1, lanes)]
    used = sum(r.shape[0] for r in rows[2:])
    small_rows = -(-used // (GROUP * 16)) * GROUP * 16
    share = jnp.pad(jnp.concatenate(rows), ((0, -used % 16), (0, 0)))
    shares = [share] + [ring("chan", nb, d)(share) for d in range(1, nb)]

    packed = []
    for k, n in enumerate(sizes):
        part = []
        for d in range(1, nb):
            at = starts[k] + (me + d) % nb * n
            block = jnp.stack([lax.dynamic_slice_in_dim(clips_in, at, n), lax.dynamic_slice_in_dim(grad_out, at, n)])
            part.append(ring("chan", nb, d)(block))
        packed.append(part)

    stacked, prm = stack_call(shares, wa.shape[0] + wb.shape[0], 0)
    meta = jnp.stack([me, place]).astype(jnp.int32)
    gathered, packed[0] = gather_group(stacked, dp_count, packed[0])
    w_in_all, w_out_all = whole_call(order, meta, gathered, ra, rb, tiles)

    carried = None
    back = []
    for k, n in enumerate(sizes):
        base = starts[k] + me * n
        spk = lax.dynamic_slice_in_dim(speaker, base, n)
        live = (base + jnp.arange(n) < counts[0]).astype(jnp.int32)
        last = k == len(sizes) - 1
        out = block_call(order, spk, live, jnp.stack([base, place]).astype(jnp.int32), clips_in, grad_out, packed[k],
                         prm, w_in_all, w_out_all, taps, speakers, small_rows, carried, last)
        carried = out[nb:]
        back.append([out[0]] + [ring("chan", nb, -d)(out[d]) for d in range(1, nb)])

    keep, send = carried
    send, *back[0] = lax.optimization_barrier((send, *back[0]))
    got = flip("dp", dp_count, 1)(send)
    total = keep[0] + got[0].astype(F32)
    for m in range(1, GROUP // 2):
        total = total + flip("dp", dp_count, 2 * m)((keep[m] + got[m].astype(F32)).astype(BF16)).astype(F32)
    step = GROUP
    while step < dp_count:
        low = total.astype(BF16)
        total = low.astype(F32) + flip("dp", dp_count, step)(low).astype(F32)
        step *= 2
    mine = total[0]
    for d in range(1, nb):
        mine = mine + ring("chan", nb, d)(total[d].astype(BF16)).astype(F32)
    g_in, g_out, g_scale, g_shift, g_conv, g_cb, g_bo, g_ls, g_bi = finish_call(
        meta, gather_group(mine.astype(BF16), dp_count)[0], nb, ra, rb, small_rows // GROUP, tiles, taps, speakers)

    clips_out = jnp.zeros(clips_in.shape, BF16)
    grad_clips = grad_out.astype(F32)
    for k, n in enumerate(sizes):
        for d in range(nb):
            at = starts[k] + (me + d) % nb * n
            clips_out = lax.dynamic_update_slice_in_dim(clips_out, back[k][d][0], at, 0)
            g = lax.dynamic_slice_in_dim(grad_out, at, n).astype(F32) + back[k][d][1].astype(F32)
            grad_clips = lax.dynamic_update_slice_in_dim(grad_clips, g, at, 0)

    return (clips_out, grad_clips, g_conv, g_cb.reshape(lanes), g_scale, g_shift, g_in, g_bi.reshape(per), g_out,
            g_bo.reshape(lanes), g_ls.reshape(lanes))


def solution(mesh):
    act = P("dp", None, "chan")
    col, vec, row = P(None, "chan"), P("chan"), P("chan", None)
    in_specs = (act, P("dp"), P("dp"), col, vec, col, col, col, vec, row, vec, vec, act)
    out_specs = (act, act, col, vec, col, col, col, vec, row, vec, vec)
    return jax.shard_map(per_device, mesh=mesh, in_specs=in_specs, out_specs=out_specs, check_vma=False)
```

time: 213 us -> 180 us (0.85)
  local copies, waits for them, and re-layouts: 39.8 us -> 10.1 us
  waiting for transfers between devices: 84 us -> 63.1 us
  Pallas kernels: 32.4 us -> 47.1 us
  starting transfers between devices: 32.5 us -> 46.8 us
  between operations: 9.75 us -> 1.75 us
  other arithmetic: 13.1 us -> 10.7 us
    ppermute x15 -> x18, waiting for transfers between devices: 65.1 us -> 40 us  [ring(): lax.ppermute(v, axis, [(i, (i + shift) % size) for i in range(size)])]
    ppermute x15 -> x18, starting transfers between devices: 21.5 us -> 36.4 us  [ring(): lax.ppermute(v, axis, [(i, (i + shift) % size) for i in range(size)])]
    pallas_call x1 -> x5, Pallas kernels: 32.4 us -> 47.1 us  [the longest x2 38.5 us: block_call(): pl.pallas_call(functools.partial(body, nb, taps, speakers, small_rows, fi...]
    transpose x6 -> x2, local copies, waits for them, and re-layouts: 6.3 us -> 0.02 us  [the longest x1 0.01 us: per_device(): lax.dynamic_slice_in_dim(w_out, place * rb, rb).reshape(rb, nb, lanes)]
    reshape x4 -> x2, local copies, waits for them, and re-layouts: 5.71 us -> 0.04 us  [the longest x1 0.02 us: per_device(): lax.dynamic_slice_in_dim(w_in, place * ra, ra).reshape(ra, tiles, lanes)]
    unnamed x50 -> x44, local copies, waits for them, and re-layouts: 9.44 us -> 4.03 us
    squeeze x7 -> x0, local copies, waits for them, and re-layouts: 5.34 us -> none  [the longest x6 4.82 us: pick(): return lax.dynamic_index_in_dim(v, index, axis, keepdims=False)]
    ppermute x12, waiting for transfers between devices: 18.9 us -> 23.1 us  [flip(): return lambda v: lax.ppermute(v, axis, [(i, i ^ mask) for i in range(size)])]
  transfers between devices with their start and end apart: 27 -> 30, of which waited for: 11 -> 14; matrix products, arithmetic and copies ran while one was open for 15% -> 7% of each run, Pallas kernels for 0% -> 24%
where the time goes in v2:
time: 180 us
  waiting for transfers between devices  63.1 us (35%)
  Pallas kernels  47.1 us (26%)
  starting transfers between devices  46.8 us (26%)
  other arithmetic  10.7 us (6%)
  local copies, waits for them, and re-layouts  10.1 us (6%)
    ppermute x18, waiting for transfers between devices, ring(): lax.ppermute(v, axis, [(i, (i + shift) % size) for i in range(size)])  40 us
    pallas_call x2, Pallas kernels, block_call(): pl.pallas_call(functools.partial(body, nb, taps, speakers, small_rows, fi...  38.5 us
    ppermute x18, starting transfers between devices, ring(): lax.ppermute(v, axis, [(i, (i + shift) % size) for i in range(size)])  36.4 us
    ppermute x12, waiting for transfers between devices, flip(): return lambda v: lax.ppermute(v, axis, [(i, i ^ mask) for i in range(size)])  23.1 us
    ppermute x12, starting transfers between devices, flip(): return lambda v: lax.ppermute(v, axis, [(i, i ^ mask) for i in range(size)])  10.4 us
    pallas_call x1, Pallas kernels, whole_call(): pl.pallas_call(functools.partial(whole_body, nb, ra, rb, tiles, lanes), i...  4.29 us
    unnamed x44, local copies, waits for them, and re-layouts  4.03 us
  transfers between devices with their start and end apart: 30, of which 14 were waited for; matrix products, arithmetic and copies ran while one was open for 7% of the time, Pallas kernels for 24%

profile of v2, /device:TPU:0, one launch (start us, length us, event | category | flops | bytes accessed | tf_op | source)
XLA Modules:
  0.0 179.6 jit_solution(14027954509133439698)
XLA Ops:
  2.5 2.9 %concatenate.3 = bf16[525,128]{1,0:T(8,128)(2,1)S(1)} concatenate(bf16[192,128]{1,0:T(8,128)(2,1)S(1)} %bitcast.138, bf16[192,128]{1,0:T(8,128)(2,1)S(1)} %bitcast.139, bf16[64,128]{1,0:T(8,128)(2,1)} %param.18, bf16[64,128]{1,0:T(8,128)(2,1)} %param.19, bf16[7,128]{1,0:T(8,128)(2,1)} %param.16, bf16[1,128]{1,0:T(2,128)(2,1)} %bitcast.144, bf16[1,128]{1,0:T(2,128)(2,1)} %bitcast.145, ...), dimensions={0} | concatenate | bytes 268800 | tf_op jit(solution)/shard_map/concatenate | solution.py:378
  5.5 3.1 %collective-permute-start.3 = (bf16[528,128]{1,0:T(8,128)(2,1)S(1)}, bf16[528,128]{1,0:T(8,128)(2,1)S(1)}, u32[]{:S(2)}, u32[]{:S(2)}) collective-permute-start(bf16[528,128]{1,0:T(8,128)(2,1)S(1)} %pad.4.refs_0_), channel_id=1, source_target_pairs={{0,1},{1,2},{2,3},{3,0},{4,5},{5,6},{6,7},{7,4},{8,9},{9,10},{10,1... | collective-permute-start | bytes 405512 | tf_op jit(solution)/shard_map/ppermute | solution.py:340
  8.6 2.6 %collective-permute-start.4 = (bf16[528,128]{1,0:T(8,128)(2,1)S(1)}, bf16[528,128]{1,0:T(8,128)(2,1)S(1)}, u32[]{:S(2)}, u32[]{:S(2)}) collective-permute-start(bf16[528,128]{1,0:T(8,128)(2,1)S(1)} %pad.4.refs_0_), channel_id=1, source_target_pairs={{0,2},{1,3},{2,0},{3,1},{4,6},{5,7},{6,4},{7,5},{8,10},{9,11},{10,... | collective-permute-start | bytes 405512 | tf_op jit(solution)/shard_map/ppermute | solution.py:340
  12.5 2.6 %collective-permute-done.3.refs_1_ = bf16[528,128]{1,0:T(8,128)(2,1)S(1)} collective-permute-done((bf16[528,128]{1,0:T(8,128)(2,1)S(1)}, bf16[528,128]{1,0:T(8,128)(2,1)S(1)}, u32[]{:S(2)}, u32[]{:S(2)}) %collective-permute-start.3) | collective-permute-done | bytes 135200 | tf_op jit(solution)/shard_map/ppermute | solution.py:340
  15.2 4.9 %collective-permute-done.4.refs_2_ = bf16[528,128]{1,0:T(8,128)(2,1)S(1)} collective-permute-done((bf16[528,128]{1,0:T(8,128)(2,1)S(1)}, bf16[528,128]{1,0:T(8,128)(2,1)S(1)}, u32[]{:S(2)}, u32[]{:S(2)}) %collective-permute-start.4) | collective-permute-done | bytes 135200 | tf_op jit(solution)/shard_map/ppermute | solution.py:340
  27.8 6.8 %collective-permute-done.6 = bf16[4,384,128]{2,1,0:T(8,128)(2,1)S(1)} collective-permute-done((bf16[4,384,128]{2,1,0:T(8,128)(2,1)}, bf16[4,384,128]{2,1,0:T(8,128)(2,1)S(1)}, u32[]{:S(2)}, u32[]{:S(2)}) %collective-permute-start.6) | collective-permute-done | bytes 393248 | tf_op jit(solution)/shard_map/ppermute | solution.py:344
  38.0 3.4 %collective-permute-start.11 = (bf16[2,2,256,128]{3,2,1,0:T(8,128)(2,1)S(1)}, bf16[2,2,256,128]{3,2,1,0:T(8,128)(2,1)S(1)}, u32[]{:S(2)}, u32[]{:S(2)}) collective-permute-start(bf16[2,2,256,128]{3,2,1,0:T(8,128)(2,1)S(1)} %pad_maximum_fusion.7), channel_id=1, source_target_pairs={{0,3},{1,0},{2,1},{3,2},{4,7},{5,4},{6,5},{7,6},{8,11},{9,8},{10,9... | collective-permute-start | bytes 786440 | tf_op jit(solution)/shard_map/ppermute | solution.py:340
  41.5 3.8 %collective-permute-done.8 = bf16[4,384,128]{2,1,0:T(8,128)(2,1)S(1)} collective-permute-done((bf16[4,384,128]{2,1,0:T(8,128)(2,1)S(1)}, bf16[4,384,128]{2,1,0:T(8,128)(2,1)S(1)}, u32[]{:S(2)}, u32[]{:S(2)}) %collective-permute-start.8) | collective-permute-done | bytes 393248 | tf_op jit(solution)/shard_map/ppermute | solution.py:344
  46.6 7.1 %collective-permute-done.10.refs_3_ = bf16[2,2,256,128]{3,2,1,0:T(8,128)(2,1)S(1)} collective-permute-done((bf16[2,2,256,128]{3,2,1,0:T(8,128)(2,1)S(1)}, bf16[2,2,256,128]{3,2,1,0:T(8,128)(2,1)S(1)}, u32[]{:S(2)}, u32[]{:S(2)}) %collective-permute-start.10) | collective-permute-done | bytes 262176 | tf_op jit(solution)/shard_map/ppermute | solution.py:340
  53.7 4.1 %collective-permute-done.9.refs_2_ = bf16[2,2,256,128]{3,2,1,0:T(8,128)(2,1)S(1)} collective-permute-done((bf16[2,2,256,128]{3,2,1,0:T(8,128)(2,1)S(1)}, bf16[2,2,256,128]{3,2,1,0:T(8,128)(2,1)S(1)}, u32[]{:S(2)}, u32[]{:S(2)}) %collective-permute-start.9) | collective-permute-done | bytes 262176 | tf_op jit(solution)/shard_map/ppermute | solution.py:340
  60.9 3.6 %collective-permute-start.1 = (bf16[2,2,256,128]{3,2,1,0:T(8,128)(2,1)}, bf16[2,2,256,128]{3,2,1,0:T(8,128)(2,1)}, u32[]{:S(2)}, u32[]{:S(2)}) collective-permute-start(bf16[2,2,256,128]{3,2,1,0:T(8,128)(2,1)} %pad_maximum_fusion.3), channel_id=1, source_target_pairs={{0,2},{1,3},{2,0},{3,1},{4,6},{5,7},{6,4},{7,5},{8,10},{9,11},{10,... | collective-permute-start | bytes 786440 | tf_op jit(solution)/shard_map/ppermute | solution.py:340
  73.3 4.3 %weights.1 = (bf16[512,1536]{1,0:T(8,128)(2,1)}, bf16[1536,512]{1,0:T(8,128)(2,1)}) custom-call(s32[4]{0:T(128)} %and_select_fusion.order_ref, s32[2]{0:T(128)} %pad_add_fusion.1.meta_ref, bf16[4,4,384,128]{3,2,1,0:T(8,128)(2,1)} %copy-done.3, bf16[4,4,384,128]{3,2,1,0:T(8,128)(2,1)} %collective-permute-done.12.refs_1_), custom_call_target="tpu_custom_call" | custom-call | tf_op jit(solution)/shard_map/weights/pallas_call | solution.py:290
  77.5 18.2 %block.2 = (bf16[2,2,256,128]{3,2,1,0:T(8,128)(2,1)}, bf16[2,2,256,128]{3,2,1,0:T(8,128)(2,1)}, bf16[2,2,256,128]{3,2,1,0:T(8,128)(2,1)}, bf16[2,2,256,128]{3,2,...) custom-call(s32[4]{0:T(128)} %and_select_fusion.order_ref, ...), custom_call_target="tpu_custom_call" | custom-call | tf_op jit(solution)/shard_map/block/pallas_call | solution.py:239
  98.6 20.3 %block.3 = (bf16[2,2,256,128]{3,2,1,0:T(8,128)(2,1)}, bf16[2,2,256,128]{3,2,1,0:T(8,128)(2,1)}, bf16[2,2,256,128]{3,2,1,0:T(8,128)(2,1)}, bf16[2,2,256,128]{3,2,...) custom-call(s32[4]{0:T(128)} %and_select_fusion.order_ref, s32[2]{0:T(128)} %get-tuple-element.102.spk_ref, ...), custom_call_target="tpu_custom_call" | custom-call | flops 68719476736 | tf_op jit(solution)/shard_map/block/pallas_call | solution.py:239
  118.9 3.2 %collective-permute-start.16 = (bf16[2,2,256,128]{3,2,1,0:T(8,128)(2,1)}, bf16[2,2,256,128]{3,2,1,0:T(8,128)(2,1)S(1)}, u32[]{:S(2)}, u32[]{:S(2)}) collective-permute-start(bf16[2,2,256,128]{3,2,1,0:T(8,128)(2,1)} %get-tuple-element.67), channel_id=1, source_target_pairs={{0,3},{1,0},{2,1},{3,2},{4,7},{5,4},{6,5},{7,6},{8,11},{9,8},{10,9... | collective-permute-start | bytes 786440 | tf_op jit(solution)/shard_map/ppermute | solution.py:340
  123.9 5.3 %collective-permute-done.16 = bf16[2,2,256,128]{3,2,1,0:T(8,128)(2,1)S(1)} collective-permute-done((bf16[2,2,256,128]{3,2,1,0:T(8,128)(2,1)}, bf16[2,2,256,128]{3,2,1,0:T(8,128)(2,1)S(1)}, u32[]{:S(2)}, u32[]{:S(2)}) %collective-permute-start.16) | collective-permute-done | bytes 262176 | tf_op jit(solution)/shard_map/ppermute | solution.py:340
  133.1 12.2 %collective-permute-done.17 = bf16[2,2,256,128]{3,2,1,0:T(8,128)(2,1)S(1)} collective-permute-done((bf16[2,2,256,128]{3,2,1,0:T(8,128)(2,1)}, bf16[2,2,256,128]{3,2,1,0:T(8,128)(2,1)S(1)}, u32[]{:S(2)}, u32[]{:S(2)}) %collective-permute-start.17) | collective-permute-done | bytes 262176 | tf_op jit(solution)/shard_map/ppermute | solution.py:340
  145.3 4.4 %collective-permute-done.21 = bf16[4,416,128]{2,1,0:T(8,128)(2,1)S(1)} collective-permute-done((bf16[4,416,128]{2,1,0:T(8,128)(2,1)S(1)}, bf16[4,416,128]{2,1,0:T(8,128)(2,1)S(1)}, u32[]{:S(2)}, u32[]{:S(2)}) %collective-permute-start.21) | collective-permute-done | bytes 426016 | tf_op jit(solution)/shard_map/ppermute | solution.py:344
  150.1 7.4 %collective-permute-start.23 = (bf16[416,128]{1,0:T(8,128)(2,1)S(1)}, bf16[416,128]{1,0:T(8,128)(2,1)S(1)}, u32[]{:S(2)}, u32[]{:S(2)}) collective-permute-start(bf16[416,128]{1,0:T(8,128)(2,1)S(1)} %get-tuple-element.98), channel_id=1, source_target_pairs={{0,1},{1,2},{2,3},{3,0},{4,5},{5,6},{6,7},{7,4},{8,9},{9,10},{10,1... | collective-permute-start | bytes 319496 | tf_op jit(solution)/shard_map/ppermute | solution.py:340
  157.4 2.4 %collective-permute-start.25 = (bf16[416,128]{1,0:T(8,128)(2,1)S(1)}, bf16[416,128]{1,0:T(8,128)(2,1)S(1)}, u32[]{:S(2)}, u32[]{:S(2)}) collective-permute-start(bf16[416,128]{1,0:T(8,128)(2,1)S(1)} %get-tuple-element.99), channel_id=1, source_target_pairs={{0,3},{1,0},{2,1},{3,2},{4,7},{5,4},{6,5},{7,6},{8,11},{9,8},{10,9... | collective-permute-start | bytes 319496 | tf_op jit(solution)/shard_map/ppermute | solution.py:340
  159.9 3.8 %collective-permute-done.24 = bf16[416,128]{1,0:T(8,128)(2,1)S(1)} collective-permute-done((bf16[416,128]{1,0:T(8,128)(2,1)S(1)}, bf16[416,128]{1,0:T(8,128)(2,1)S(1)}, u32[]{:S(2)}, u32[]{:S(2)}) %collective-permute-start.24) | collective-permute-done | bytes 106528 | tf_op jit(solution)/shard_map/ppermute | solution.py:340
  165.3 3.2 %collective-permute-done.26 = bf16[416,128]{1,0:T(8,128)(2,1)S(1)} collective-permute-done((bf16[416,128]{1,0:T(8,128)(2,1)S(1)}, bf16[416,128]{1,0:T(8,128)(2,1)S(1)}, u32[]{:S(2)}, u32[]{:S(2)}) %collective-permute-start.26) | collective-permute-done | bytes 106528 | tf_op jit(solution)/shard_map/ppermute | solution.py:344
  169.1 4.1 %collective-permute-done.28 = bf16[416,128]{1,0:T(8,128)(2,1)S(1)} collective-permute-done((bf16[416,128]{1,0:T(8,128)(2,1)S(1)}, bf16[416,128]{1,0:T(8,128)(2,1)S(1)}, u32[]{:S(2)}, u32[]{:S(2)}) %collective-permute-start.28) | collective-permute-done | bytes 106528 | tf_op jit(solution)/shard_map/ppermute | solution.py:344
  175.9 2.4 %finish.1 = (f32[512,384]{1,0:T(8,128)}, f32[384,512]{1,0:T(8,128)}, f32[64,128]{1,0:T(8,128)}, f32[64,128]{1,0:T(8,128)}, f32[7,128]{1,0:T(8,128)}, /*index=5*/...) custom-call(s32[2]{0:T(128)} %pad_add_fusion.1.meta_ref, bf16[4,416,128]{2,1,0:T(8,128)(2,1)} %copy-done.7, ...), custom_call_target="tpu_custom_call" | custom-call | tf_op jit(solution)/shard_map/finish/pallas_call | solution.py:329
  (132 shorter events, 41.8 us)
Async XLA Ops:
  5.5 9.7 %collective-permute-start.3 = (bf16[528,128]{1,0:T(8,128)(2,1)S(1)}, bf16[528,128]{1,0:T(8,128)(2,1)S(1)}, u32[]{:S(2)}, u32[]{:S(2)}) collective-permute-start(bf16[528,128]{1,0:T(8,128)(2,1)S(1)} %pad.4.refs_0_), channel_id=1, source_target_pairs={{0,1},{1,2},{2,3},{3,0},{4,5},{5,6},{6,7},{7,4},{8,9},{9,10},{10,1... | collective-permute-start | bytes 405512 | tf_op jit(solution)/shard_map/ppermute | solution.py:340
  8.6 11.5 %collective-permute-start.4 = (bf16[528,128]{1,0:T(8,128)(2,1)S(1)}, bf16[528,128]{1,0:T(8,128)(2,1)S(1)}, u32[]{:S(2)}, u32[]{:S(2)}) collective-permute-start(bf16[528,128]{1,0:T(8,128)(2,1)S(1)} %pad.4.refs_0_), channel_id=1, source_target_pairs={{0,2},{1,3},{2,0},{3,1},{4,6},{5,7},{6,4},{7,5},{8,10},{9,11},{10,... | collective-permute-start | bytes 405512 | tf_op jit(solution)/shard_map/ppermute | solution.py:340
  11.2 8.9 %collective-permute-start.5 = (bf16[528,128]{1,0:T(8,128)(2,1)S(1)}, bf16[528,128]{1,0:T(8,128)(2,1)S(1)}, u32[]{:S(2)}, u32[]{:S(2)}) collective-permute-start(bf16[528,128]{1,0:T(8,128)(2,1)S(1)} %pad.4.refs_0_), channel_id=1, source_target_pairs={{0,3},{1,0},{2,1},{3,2},{4,7},{5,4},{6,5},{7,6},{8,11},{9,8},{10,9... | collective-permute-start | bytes 405512 | tf_op jit(solution)/shard_map/ppermute | solution.py:340
  23.4 11.2 %collective-permute-start.6 = (bf16[4,384,128]{2,1,0:T(8,128)(2,1)}, bf16[4,384,128]{2,1,0:T(8,128)(2,1)S(1)}, u32[]{:S(2)}, u32[]{:S(2)}) collective-permute-start(bf16[4,384,128]{2,1,0:T(8,128)(2,1)} %get-tuple-element.47), channel_id=1, source_target_pairs={{0,8},{4,12},{8,0},{12,4},{16,24},{20,28},{24,16},{28,20},{1,9},{5... | collective-permute-start | bytes 1179656 | tf_op jit(solution)/shard_map/ppermute | solution.py:344
  26.2 15.3 %collective-permute-start.7 = (bf16[4,384,128]{2,1,0:T(8,128)(2,1)S(1)}, bf16[4,384,128]{2,1,0:T(8,128)(2,1)S(1)}, u32[]{:S(2)}, u32[]{:S(2)}) collective-permute-start(bf16[4,384,128]{2,1,0:T(8,128)(2,1)S(1)} %copy-done.11), channel_id=1, source_target_pairs={{0,16},{4,20},{8,24},{12,28},{16,0},{20,4},{24,8},{28,12},{1,17},{... | collective-permute-start | bytes 1179656 | tf_op jit(solution)/shard_map/ppermute | solution.py:344
  34.5 10.8 %collective-permute-start.8 = (bf16[4,384,128]{2,1,0:T(8,128)(2,1)S(1)}, bf16[4,384,128]{2,1,0:T(8,128)(2,1)S(1)}, u32[]{:S(2)}, u32[]{:S(2)}) collective-permute-start(bf16[4,384,128]{2,1,0:T(8,128)(2,1)S(1)} %collective-permute-done.6), channel_id=1, source_target_pairs={{0,16},{4,20},{8,24},{12,28},{16,0},{20,4},{24,8},{28,12},{1,17},{... | collective-permute-start | bytes 1179656 | tf_op jit(solution)/shard_map/ppermute | solution.py:344
  36.1 17.6 %collective-permute-start.10 = (bf16[2,2,256,128]{3,2,1,0:T(8,128)(2,1)S(1)}, bf16[2,2,256,128]{3,2,1,0:T(8,128)(2,1)S(1)}, u32[]{:S(2)}, u32[]{:S(2)}) collective-permute-start(bf16[2,2,256,128]{3,2,1,0:T(8,128)(2,1)S(1)} %pad_maximum_fusion.6), channel_id=1, source_target_pairs={{0,2},{1,3},{2,0},{3,1},{4,6},{5,7},{6,4},{7,5},{8,10},{9,11},{10,... | collective-permute-start | bytes 786440 | tf_op jit(solution)/shard_map/ppermute | solution.py:340
  38.0 15.7 %collective-permute-start.11 = (bf16[2,2,256,128]{3,2,1,0:T(8,128)(2,1)S(1)}, bf16[2,2,256,128]{3,2,1,0:T(8,128)(2,1)S(1)}, u32[]{:S(2)}, u32[]{:S(2)}) collective-permute-start(bf16[2,2,256,128]{3,2,1,0:T(8,128)(2,1)S(1)} %pad_maximum_fusion.7), channel_id=1, source_target_pairs={{0,3},{1,0},{2,1},{3,2},{4,7},{5,4},{6,5},{7,6},{8,11},{9,8},{10,9... | collective-permute-start | bytes 786440 | tf_op jit(solution)/shard_map/ppermute | solution.py:340
  41.4 16.3 %collective-permute-start.9 = (bf16[2,2,256,128]{3,2,1,0:T(8,128)(2,1)S(1)}, bf16[2,2,256,128]{3,2,1,0:T(8,128)(2,1)S(1)}, u32[]{:S(2)}, u32[]{:S(2)}) collective-permute-start(bf16[2,2,256,128]{3,2,1,0:T(8,128)(2,1)S(1)} %pad_maximum_fusion.5), channel_id=1, source_target_pairs={{0,1},{1,2},{2,3},{3,0},{4,5},{5,6},{6,7},{7,4},{8,9},{9,10},{10,1... | collective-permute-start | bytes 786440 | tf_op jit(solution)/shard_map/ppermute | solution.py:340
  57.8 15.5 %collective-permute-start.12 = (bf16[4,4,384,128]{3,2,1,0:T(8,128)(2,1)S(1)}, bf16[4,4,384,128]{3,2,1,0:T(8,128)(2,1)}, u32[]{:S(2)}, u32[]{:S(2)}) collective-permute-start(bf16[4,4,384,128]{3,2,1,0:T(8,128)(2,1)S(1)} %pad_maximum_fusion.refs_0_), channel_id=1, source_target_pairs={{0,4},{4,0},{8,12},{12,8},{16,20},{20,16},{24,28},{28,24},{1,5},{5... | collective-permute-start | bytes 4718600 | tf_op jit(solution)/shard_map/ppermute | solution.py:344
  58.6 39.4 %collective-permute-start.2 = (bf16[2,2,256,128]{3,2,1,0:T(8,128)(2,1)}, bf16[2,2,256,128]{3,2,1,0:T(8,128)(2,1)}, u32[]{:S(2)}, u32[]{:S(2)}) collective-permute-start(bf16[2,2,256,128]{3,2,1,0:T(8,128)(2,1)} %pad_maximum_fusion.4), channel_id=1, source_target_pairs={{0,3},{1,0},{2,1},{3,2},{4,7},{5,4},{6,5},{7,6},{8,11},{9,8},{10,9... | collective-permute-start | bytes 786440 | tf_op jit(solution)/shard_map/ppermute | solution.py:340
  60.9 37.6 %collective-permute-start.1 = (bf16[2,2,256,128]{3,2,1,0:T(8,128)(2,1)}, bf16[2,2,256,128]{3,2,1,0:T(8,128)(2,1)}, u32[]{:S(2)}, u32[]{:S(2)}) collective-permute-start(bf16[2,2,256,128]{3,2,1,0:T(8,128)(2,1)} %pad_maximum_fusion.3), channel_id=1, source_target_pairs={{0,2},{1,3},{2,0},{3,1},{4,6},{5,7},{6,4},{7,5},{8,10},{9,11},{10,... | collective-permute-start | bytes 786440 | tf_op jit(solution)/shard_map/ppermute | solution.py:340
  65.3 33.3 %collective-permute-start = (bf16[2,2,256,128]{3,2,1,0:T(8,128)(2,1)}, bf16[2,2,256,128]{3,2,1,0:T(8,128)(2,1)}, u32[]{:S(2)}, u32[]{:S(2)}) collective-permute-start(bf16[2,2,256,128]{3,2,1,0:T(8,128)(2,1)} %pad_maximum_fusion.2), channel_id=1, source_target_pairs={{0,1},{1,2},{2,3},{3,0},{4,5},{5,6},{6,7},{7,4},{8,9},{9,10},{10,1... | collective-permute-start | bytes 786440 | tf_op jit(solution)/shard_map/ppermute | solution.py:340
  95.7 27.6 %collective-permute-start.13 = (bf16[2,2,256,128]{3,2,1,0:T(8,128)(2,1)}, bf16[2,2,256,128]{3,2,1,0:T(8,128)(2,1)S(1)}, u32[]{:S(2)}, u32[]{:S(2)}) collective-permute-start(bf16[2,2,256,128]{3,2,1,0:T(8,128)(2,1)} %get-tuple-element.59), channel_id=1, source_target_pairs={{0,3},{1,0},{2,1},{3,2},{4,7},{5,4},{6,5},{7,6},{8,11},{9,8},{10,9... | collective-permute-start | bytes 786440 | tf_op jit(solution)/shard_map/ppermute | solution.py:340
  97.9 25.4 %collective-permute-start.14 = (bf16[2,2,256,128]{3,2,1,0:T(8,128)(2,1)}, bf16[2,2,256,128]{3,2,1,0:T(8,128)(2,1)S(1)}, u32[]{:S(2)}, u32[]{:S(2)}) collective-permute-start(bf16[2,2,256,128]{3,2,1,0:T(8,128)(2,1)} %get-tuple-element.60), channel_id=1, source_target_pairs={{0,2},{1,3},{2,0},{3,1},{4,6},{5,7},{6,4},{7,5},{8,10},{9,11},{10,... | collective-permute-start | bytes 786440 | tf_op jit(solution)/shard_map/ppermute | solution.py:340
  97.9 25.4 %collective-permute-start.15 = (bf16[2,2,256,128]{3,2,1,0:T(8,128)(2,1)}, bf16[2,2,256,128]{3,2,1,0:T(8,128)(2,1)S(1)}, u32[]{:S(2)}, u32[]{:S(2)}) collective-permute-start(bf16[2,2,256,128]{3,2,1,0:T(8,128)(2,1)} %get-tuple-element.61), channel_id=1, source_target_pairs={{0,1},{1,2},{2,3},{3,0},{4,5},{5,6},{6,7},{7,4},{8,9},{9,10},{10,1... | collective-permute-start | bytes 786440 | tf_op jit(solution)/shard_map/ppermute | solution.py:340
  118.9 10.3 %collective-permute-start.16 = (bf16[2,2,256,128]{3,2,1,0:T(8,128)(2,1)}, bf16[2,2,256,128]{3,2,1,0:T(8,128)(2,1)S(1)}, u32[]{:S(2)}, u32[]{:S(2)}) collective-permute-start(bf16[2,2,256,128]{3,2,1,0:T(8,128)(2,1)} %get-tuple-element.67), channel_id=1, source_target_pairs={{0,3},{1,0},{2,1},{3,2},{4,7},{5,4},{6,5},{7,6},{8,11},{9,8},{10,9... | collective-permute-start | bytes 786440 | tf_op jit(solution)/shard_map/ppermute | solution.py:340
  122.1 23.1 %collective-permute-start.17 = (bf16[2,2,256,128]{3,2,1,0:T(8,128)(2,1)}, bf16[2,2,256,128]{3,2,1,0:T(8,128)(2,1)S(1)}, u32[]{:S(2)}, u32[]{:S(2)}) collective-permute-start(bf16[2,2,256,128]{3,2,1,0:T(8,128)(2,1)} %get-tuple-element.68), channel_id=1, source_target_pairs={{0,2},{1,3},{2,0},{3,1},{4,6},{5,7},{6,4},{7,5},{8,10},{9,11},{10,... | collective-permute-start | bytes 786440 | tf_op jit(solution)/shard_map/ppermute | solution.py:340
  123.3 50.1 %collective-permute-start.18 = (bf16[2,2,256,128]{3,2,1,0:T(8,128)(2,1)}, bf16[2,2,256,128]{3,2,1,0:T(8,128)(2,1)S(1)}, u32[]{:S(2)}, u32[]{:S(2)}) collective-permute-start(bf16[2,2,256,128]{3,2,1,0:T(8,128)(2,1)} %get-tuple-element.69), channel_id=1, source_target_pairs={{0,1},{1,2},{2,3},{3,0},{4,5},{5,6},{6,7},{7,4},{8,9},{9,10},{10,1... | collective-permute-start | bytes 786440 | tf_op jit(solution)/shard_map/ppermute | solution.py:340
  129.6 15.8 %collective-permute-start.20 = (bf16[4,416,128]{2,1,0:T(8,128)(2,1)S(1)}, bf16[4,416,128]{2,1,0:T(8,128)(2,1)S(1)}, u32[]{:S(2)}, u32[]{:S(2)}) collective-permute-start(bf16[4,416,128]{2,1,0:T(8,128)(2,1)S(1)} %get-tuple-element.83), channel_id=1, source_target_pairs={{0,8},{4,12},{8,0},{12,4},{16,24},{20,28},{24,16},{28,20},{1,9},{5... | collective-permute-start | bytes 1277960 | tf_op jit(solution)/shard_map/ppermute | solution.py:344
  131.1 18.6 %collective-permute-start.21 = (bf16[4,416,128]{2,1,0:T(8,128)(2,1)S(1)}, bf16[4,416,128]{2,1,0:T(8,128)(2,1)S(1)}, u32[]{:S(2)}, u32[]{:S(2)}) collective-permute-start(bf16[4,416,128]{2,1,0:T(8,128)(2,1)S(1)} %get-tuple-element.85), channel_id=1, source_target_pairs={{0,16},{4,20},{8,24},{12,28},{16,0},{20,4},{24,8},{28,12},{1,17},{... | collective-permute-start | bytes 1277960 | tf_op jit(solution)/shard_map/ppermute | solution.py:344
  131.6 18.1 %collective-permute-start.22 = (bf16[4,416,128]{2,1,0:T(8,128)(2,1)S(1)}, bf16[4,416,128]{2,1,0:T(8,128)(2,1)S(1)}, u32[]{:S(2)}, u32[]{:S(2)}) collective-permute-start(bf16[4,416,128]{2,1,0:T(8,128)(2,1)S(1)} %get-tuple-element.84), channel_id=1, source_target_pairs={{0,24},{4,28},{8,16},{12,20},{16,8},{20,12},{24,0},{28,4},{1,25},{... | collective-permute-start | bytes 1277960 | tf_op jit(solution)/shard_map/ppermute | solution.py:344
  150.1 9.8 %collective-permute-start.23 = (bf16[416,128]{1,0:T(8,128)(2,1)S(1)}, bf16[416,128]{1,0:T(8,128)(2,1)S(1)}, u32[]{:S(2)}, u32[]{:S(2)}) collective-permute-start(bf16[416,128]{1,0:T(8,128)(2,1)S(1)} %get-tuple-element.98), channel_id=1, source_target_pairs={{0,1},{1,2},{2,3},{3,0},{4,5},{5,6},{6,7},{7,4},{8,9},{9,10},{10,1... | collective-permute-start | bytes 319496 | tf_op jit(solution)/shard_map/ppermute | solution.py:340
  157.4 6.3 %collective-permute-start.24 = (bf16[416,128]{1,0:T(8,128)(2,1)S(1)}, bf16[416,128]{1,0:T(8,128)(2,1)S(1)}, u32[]{:S(2)}, u32[]{:S(2)}) collective-permute-start(bf16[416,128]{1,0:T(8,128)(2,1)S(1)} %get-tuple-element.100), channel_id=1, source_target_pairs={{0,2},{1,3},{2,0},{3,1},{4,6},{5,7},{6,4},{7,5},{8,10},{9,11},{10,... | collective-permute-start | bytes 319496 | tf_op jit(solution)/shard_map/ppermute | solution.py:340
  (28 other events, 251.4 us)

commit v3 on v2

v3 whole, which is shorter than its diff:
```python
import functools

import jax
import jax.numpy as jnp
from jax import lax
from jax.experimental import pallas as pl
from jax.experimental.pallas import tpu as pltpu
from jax.sharding import PartitionSpec as P

RUNS = ((1, 1), (2,))
GROUP = 8

EPS = 1e-06
ROOT_TWO_PI = 2.5066282746310002
F32 = jnp.float32
BF16 = jnp.bfloat16
PAD = 8
HINT = 1 << 36


def gelu_pair(v):
    z = jnp.abs(v)
    t = 1.0 / (1.0 + (0.3275911 * 0.7071067811865476) * z)
    e = jnp.exp(v * v * -0.5)
    poly = t * (0.5 * 0.254829592 + t * (0.5 * -0.284496736 + t * (0.5 * 1.421413741 + t * (0.5 * -1.453152027 + t * (0.5 * 1.061405429)))))
    tail = poly * e
    cdf = jnp.where(v >= 0.0, 1.0 - tail, tail)
    return v * cdf, cdf + v * (e * (1.0 / ROOT_TWO_PI))


def dot(a, b, ca, cb):
    return lax.dot_general(a, b, (((ca,), (cb,)), ((), ())), preferred_element_type=F32)


def body(n_blocks, taps, speakers, runs, first,
         order_ref, spk_ref, live_ref, slot_ref, meta_ref, *refs):
    nb = n_blocks
    x0, g0 = refs[:2]
    k = 2
    p = []
    for _ in runs:
        p.append(refs[k:k + nb - 1])
        k += nb - 1
    prm = refs[k]
    shares = refs[k + 1:k + 1 + GROUP]
    k += 1 + GROUP
    if not first:
        got = refs[k]
        k += 1
    o = refs[k:k + nb]
    k += nb
    (nlow, blow, act, plow, gsm, xpad, gpad, normed, gin, slope, wide, b_in, w_in, w_out) = refs[k:k + 14]
    i = pl.program_id(0)
    length, lanes = normed.shape[1], normed.shape[2]
    width = nb * lanes
    ff = act.shape[2]
    per = ff // nb
    tiles = per // lanes
    margin = taps // 2
    r_conv, r_cb = 2 * speakers, 2 * speakers + taps
    r_bo, r_ls, r_bi = r_cb + 1, r_cb + 2, r_cb + 3
    cols = [pl.multiple_of(order_ref[d] * lanes, lanes) for d in range(nb)]

    @pl.when(i == 0)
    def _():
        for d in range(nb):
            zero = jnp.zeros((PAD, lanes), F32)
            xpad[d, 0:PAD, :] = zero
            xpad[d, PAD + length:, :] = zero
            gpad[d, 0:PAD, :] = zero
            gpad[d, PAD + length:, :] = zero
            for r in range(tiles):
                at = pl.multiple_of(order_ref[d] * per + r * lanes, lanes)
                b_in[:, pl.ds(at, lanes)] = prm[d, r_bi + r:r_bi + r + 1, :]
        gsm[...] = jnp.zeros_like(gsm) if first else got[...]
        ra, rb = width // GROUP, per // GROUP
        for s in range(GROUP):
            part = meta_ref[1] ^ s

            def unpack(d, carry):
                c = order_ref[d]
                for r in range(tiles):
                    w_in[pl.ds(pl.multiple_of(part * ra, ra), ra), pl.ds(pl.multiple_of(c * per + r * lanes, lanes), lanes)] = shares[s][d, r * ra:(r + 1) * ra, :]
                base = tiles * ra
                for r in range(nb):
                    w_out[pl.ds(pl.multiple_of(c * per + part * rb, 16), rb), r * lanes:(r + 1) * lanes] = shares[s][d, base + r * rb:base + (r + 1) * rb, :]
                return carry
            lax.fori_loop(0, nb, unpack, 0)

    xpad[0, PAD:PAD + length, :] = x0[0].astype(F32)
    gin[0] = g0[0]
    low = 0
    for run, part in zip(runs, p):
        @pl.when((i >= low) & (i < low + run))
        def _(low=low, run=run, part=part):
            at = i - low if run > 1 else 0
            for d in range(1, nb):
                xpad[d, PAD:PAD + length, :] = part[d - 1][0, at].astype(F32)
                gin[d] = part[d - 1][1, at]
        low += run

    spk = spk_ref[i]
    live = live_ref[i].astype(F32)
    total = jnp.zeros((length, 1), F32)
    for d in range(nb):
        acc = jnp.broadcast_to(prm[d, r_cb:r_cb + 1, :], (length, lanes))
        for t in range(taps):
            s = PAD - margin + t
            acc = acc + prm[d, r_conv + t:r_conv + t + 1, :] * xpad[d, s:s + length, :]
        normed[d] = acc
        total = total + jnp.sum(acc, 1, keepdims=True)
    mean = total / width
    square = jnp.zeros((length, 1), F32)
    for d in range(nb):
        c = normed[d] - mean
        normed[d] = c
        square = square + jnp.sum(c * c, 1, keepdims=True)
    inv = lax.rsqrt(square / width + EPS)
    for d in range(nb):
        v = normed[d] * inv
        normed[d] = v
        sc = prm[d, pl.ds(spk, 1), :]
        sh = prm[d, pl.ds(speakers + spk, 1), :]
        nlow[0, :, pl.ds(cols[d], lanes)] = (v * sc + sh).astype(BF16)

    step = 256
    for f in range(0, ff, step):
        pre = dot(nlow[0], w_in[:, f:f + step], 1, 0) + b_in[:, f:f + step]
        a, s = gelu_pair(pre)
        act[0, :, f:f + step] = a.astype(BF16)
        slope[:, f:f + step] = s
    wide[...] = dot(act[0], w_out[...], 1, 0)
    for d in range(nb):
        b = wide[:, pl.ds(cols[d], lanes)] + prm[d, r_bo:r_bo + 1, :]
        ls = prm[d, r_ls:r_ls + 1, :] * live
        x = xpad[d, PAD:PAD + length, :]
        g = gin[d].astype(F32)
        o[d][0, 0] = (x + b * ls).astype(BF16)
        gb = g * ls
        gsm[d, r_bo:r_bo + 1, :] += jnp.sum(gb, 0, keepdims=True)
        gsm[d, r_ls:r_ls + 1, :] += jnp.sum(g * b, 0, keepdims=True) * live
        blow[0, :, pl.ds(cols[d], lanes)] = gb.astype(BF16)
    for f in range(0, ff, step):
        gp = dot(blow[0], w_out[f:f + step, :], 1, 1) * slope[:, f:f + step]
        plow[0, :, f:f + step] = gp.astype(BF16)
        gsum = jnp.sum(gp, 0, keepdims=True)
        for r in range(step // lanes):
            q = f // lanes + r
            gsm[nb, q:q + 1, :] += gsum[:, r * lanes:(r + 1) * lanes]
    wide[...] = dot(plow[0], w_in[...], 1, 1)
    m1 = jnp.zeros((length, 1), F32)
    m2 = jnp.zeros((length, 1), F32)
    for d in range(nb):
        gn = wide[:, pl.ds(cols[d], lanes)]
        v = normed[d]
        gv = gn * v
        gsm[d, pl.ds(spk, 1), :] += jnp.sum(gv, 0, keepdims=True)
        gsm[d, pl.ds(speakers + spk, 1), :] += jnp.sum(gn, 0, keepdims=True)
        sc = prm[d, pl.ds(spk, 1), :]
        m1 = m1 + jnp.sum(gn * sc, 1, keepdims=True)
        m2 = m2 + jnp.sum(gv * sc, 1, keepdims=True)
    m1 = m1 / width
    m2 = m2 / width
    for d in range(nb):
        sc = prm[d, pl.ds(spk, 1), :]
        gc = (wide[:, pl.ds(cols[d], lanes)] * sc - m1 - normed[d] * m2) * inv
        gpad[d, PAD:PAD + length, :] = gc
        gsm[d, r_cb:r_cb + 1, :] += jnp.sum(gc, 0, keepdims=True)
        acc = jnp.zeros((length, lanes), F32)
        for t in range(taps):
            s = PAD - margin + t
            gsm[d, r_conv + t:r_conv + t + 1, :] += jnp.sum(xpad[d, s:s + length, :] * gc, 0, keepdims=True)
            s = PAD + margin - t
            acc = acc + prm[d, r_conv + t:r_conv + t + 1, :] * gpad[d, s:s + length, :]
        o[d][1, 0] = acc.astype(BF16)


def block_call(order, spk, live, slot, meta, clips, grads, packed, prm, shares, ff, taps, speakers, small_rows, carried, hint):
    nb = len(packed[0]) + 1
    runs = [part[0].shape[1] for part in packed]
    n = sum(runs)
    _, _, length, lanes = packed[0][0].shape
    width = nb * lanes
    first = carried is None
    full = lambda shape: pl.BlockSpec(shape, lambda i, *_: (0,) * len(shape), pipeline_mode=pl.Buffered(1))
    step = lambda *shape: pl.BlockSpec((1,) + shape, lambda i, *_: (i,) + (0,) * len(shape))
    own = pl.BlockSpec((1, length, lanes), lambda i, order, spk, live, slot, meta: (slot[i], 0, 0))
    sums = (nb + 1, small_rows, lanes)
    args = [clips, grads] + [v for part in packed for v in part] + [prm] + list(shares)
    in_specs = [own, own] + [full(v.shape) for v in args[2:]]
    out_shape = [jax.ShapeDtypeStruct((2, n, length, lanes), BF16)] * nb + [
        jax.ShapeDtypeStruct((n, length, w), BF16) for w in (width, width, ff, ff)] + [jax.ShapeDtypeStruct(sums, F32)]
    out_specs = [pl.BlockSpec((2, 1, length, lanes), lambda i, *_: (0, i, 0, 0))] * nb + [step(length, w) for w in (width, width, ff, ff)] + [
        pl.BlockSpec(sums, lambda i, *_: (0, 0, 0))]
    if not first:
        args.append(carried)
        in_specs.append(full(sums))
    scratch = [
        pltpu.VMEM((nb, length + 2 * PAD, lanes), F32),
        pltpu.VMEM((nb, length + 2 * PAD, lanes), F32),
        pltpu.VMEM((nb, length, lanes), F32),
        pltpu.VMEM((nb, length, lanes), BF16),
        pltpu.VMEM((length, ff), F32),
        pltpu.VMEM((length, width), F32),
        pltpu.VMEM((1, ff), F32),
        pltpu.VMEM((width, ff), BF16),
        pltpu.VMEM((ff, width), BF16),
    ]
    return pl.pallas_call(
        functools.partial(body, nb, taps, speakers, runs, first),
        out_shape=out_shape,
        grid_spec=pltpu.PrefetchScalarGridSpec(
            num_scalar_prefetch=5, grid=(n,), in_specs=in_specs, out_specs=out_specs, scratch_shapes=scratch),
        cost_estimate=pl.CostEstimate(flops=hint, transcendentals=0, bytes_accessed=0),
        compiler_params=pltpu.CompilerParams(dimension_semantics=("arbitrary",), vmem_limit_bytes=40 << 20),
        name="block",
    )(order, spk, live, slot, meta, *args)


def grads_body(nb, count, bi_row, order_ref, meta_ref, *refs):
    nlow, blow, act, plow = (refs[j * count:(j + 1) * count] for j in range(4))
    sums, keep, send, gwi, gwo, gsm = refs[4 * count:]
    tiles_all, width, lanes = gwi.shape
    ff = gwo.shape[0]
    tiles = tiles_all // nb
    per = ff // nb
    step = 256
    for f in range(0, ff, step):
        da = sum(dot(a[...], v[:, f:f + step], 0, 0) for a, v in zip(nlow, plow))
        for r in range(step // lanes):
            gwi[f // lanes + r] = da[:, r * lanes:(r + 1) * lanes]
        gwo[f:f + step, :] = sum(dot(v[:, f:f + step], b[...], 0, 0) for v, b in zip(act, blow))
    gsm[...] = sums[0:nb]
    for d in range(nb):
        for r in range(tiles):
            gsm[d, bi_row + r:bi_row + r + 1, :] = sums[nb, pl.ds(order_ref[d] * tiles + r, 1), :]
    place = meta_ref[1]
    ra, rb, rs = width // GROUP, per // GROUP, gsm.shape[1] // GROUP

    def emit(m, carry):
        for e in range(nb):
            d = -e % nb
            c = order_ref[d]
            for out, part in ((keep, place ^ (2 * m)), (send, place ^ (2 * m) ^ 1)):
                for r in range(tiles):
                    v = gwi[c * tiles + r, pl.ds(pl.multiple_of(part * ra, ra), ra), :]
                    out[m, e, r * ra:(r + 1) * ra, :] = v.astype(out.dtype)
                base = tiles * ra
                for r in range(nb):
                    v = gwo[pl.ds(pl.multiple_of(c * per + part * rb, 16), rb), r * lanes:(r + 1) * lanes]
                    out[m, e, base + r * rb:base + (r + 1) * rb, :] = v.astype(out.dtype)
                base += nb * rb
                v = gsm[d, pl.ds(pl.multiple_of(part * rs, rs), rs), :]
                out[m, e, base:base + rs, :] = v.astype(out.dtype)
        return carry
    lax.fori_loop(0, GROUP // 2, emit, 0)


def grads_call(order, meta, nlow, blow, act, plow, sums, bi_row):
    nb = sums.shape[0] - 1
    small_rows, lanes = sums.shape[1:]
    ff = act[0].shape[-1]
    width = nb * lanes
    per = ff // nb
    rows = (width // GROUP) * (per // lanes) + (per // GROUP) * nb + small_rows // GROUP
    flat = [v.reshape(-1, v.shape[-1]) for v in (*nlow, *blow, *act, *plow)]
    vm = pl.BlockSpec(memory_space=pltpu.VMEM)
    sm = pl.BlockSpec(memory_space=pltpu.SMEM)
    return pl.pallas_call(
        functools.partial(grads_body, nb, len(nlow), bi_row),
        in_specs=[sm, sm] + [vm] * (len(flat) + 1),
        out_specs=[vm, vm],
        out_shape=[jax.ShapeDtypeStruct((GROUP // 2, nb, rows, lanes), t) for t in (F32, BF16)],
        scratch_shapes=[pltpu.VMEM((ff // lanes, width, lanes), F32), pltpu.VMEM((ff, width), F32), pltpu.VMEM((nb, small_rows, lanes), F32)],
        cost_estimate=pl.CostEstimate(flops=HINT, transcendentals=0, bytes_accessed=0),
        compiler_params=pltpu.CompilerParams(vmem_limit_bytes=40 << 20),
        name="weight_grads",
    )(order, meta, *flat, sums)


def stack_body(count, rows, *refs):
    ins, (w, prm) = refs[:count], refs[count:]
    for d in range(count):
        w[d] = ins[d][0:rows, :]
        prm[d] = ins[d][rows:, :].astype(F32)


def stack_call(parts, rows, hint):
    total, lanes = parts[0].shape
    return pl.pallas_call(
        functools.partial(stack_body, len(parts), rows),
        out_shape=[jax.ShapeDtypeStruct((len(parts), rows, lanes), BF16),
                   jax.ShapeDtypeStruct((len(parts), total - rows, lanes), F32)],
        cost_estimate=pl.CostEstimate(flops=hint, transcendentals=0, bytes_accessed=0),
        name="gathered",
    )(*parts)


def finish_body(nb, ra, rb, rs, tiles, lanes, taps, speakers, meta_ref, *refs):
    ins = [refs[s % 2].at[s // 2] for s in range(GROUP)]
    g_in, g_out, scale, shift, conv, cb, bo, ls, bi, small = refs[2:]
    for s in range(GROUP):
        part = meta_ref[1] ^ s
        for r in range(tiles):
            g_in[pl.ds(pl.multiple_of(part * ra, ra), ra), r * lanes:(r + 1) * lanes] = ins[s][r * ra:(r + 1) * ra, :].astype(F32)
        base = tiles * ra
        for r in range(nb):
            g_out[pl.ds(pl.multiple_of(part * rb, 16), rb), r * lanes:(r + 1) * lanes] = ins[s][base + r * rb:base + (r + 1) * rb, :].astype(F32)
        base += nb * rb
        small[pl.ds(pl.multiple_of(part * rs, rs), rs), :] = ins[s][base:base + rs, :].astype(F32)
    scale[...] = small[0:speakers, :]
    shift[...] = small[speakers:2 * speakers, :]
    at = 2 * speakers
    conv[...] = small[at:at + taps, :]
    at += taps
    cb[...] = small[at:at + 1, :]
    bo[...] = small[at + 1:at + 2, :]
    ls[...] = small[at + 2:at + 3, :]
    for r in range(tiles):
        bi[pl.ds(r * lanes, lanes)] = small[at + 3 + r, :]


def finish_call(meta, parts, nb, ra, rb, rs, tiles, taps, speakers):
    lanes = parts[0].shape[2]
    vm = pl.BlockSpec(memory_space=pltpu.VMEM)
    sm = pl.BlockSpec(memory_space=pltpu.SMEM)
    shapes = [(nb * lanes, tiles * lanes), (tiles * lanes, nb * lanes), (speakers, lanes), (speakers, lanes), (taps, lanes),
              (1, lanes), (1, lanes), (1, lanes), (tiles * lanes,)]
    return pl.pallas_call(
        functools.partial(finish_body, nb, ra, rb, rs, tiles, lanes, taps, speakers),
        in_specs=[sm] + [vm] * 2,
        out_specs=[vm] * len(shapes),
        out_shape=[jax.ShapeDtypeStruct(s, F32) for s in shapes],
        scratch_shapes=[pltpu.VMEM((rs * GROUP, lanes), F32)],
        name="finish",
    )(meta, *parts)


def ring(axis, size, shift):
    return lambda v: lax.ppermute(v, axis, [(i, (i + shift) % size) for i in range(size)])


def flip(axis, size, mask):
    return lambda v: lax.ppermute(v, axis, [(i, i ^ mask) for i in range(size)])


def gather_group(v, dp_count, gates):
    core = flip("dp", dp_count, 1)
    a, b = flip("dp", dp_count, 2)(v), flip("dp", dp_count, 4)(v)
    a, *one = lax.optimization_barrier((a, *gates[0]))
    c = flip("dp", dp_count, 4)(a)
    c, *two = lax.optimization_barrier((c, *gates[1]))
    return [v, core(v), a, core(a), b, core(b), c, core(c)], (one, two)


def gather_small(v, dp_count):
    near = jnp.stack([v] + [flip("dp", dp_count, 2 * m)(v) for m in range(1, GROUP // 2)])
    return [near, flip("dp", dp_count, 1)(near)]


def per_device(clips_in, speaker, counts, conv_weight, conv_bias, scale_table, shift_table,
               w_in, b_in, w_out, b_out, layer_scale, grad_out):
    clip_num, length, lanes = clips_in.shape
    nb = lax.axis_size("chan")
    dp_count = lax.axis_size("dp")
    me = lax.axis_index("chan")
    dp = lax.axis_index("dp")
    speakers = scale_table.shape[0]
    taps = conv_weight.shape[0]
    per = w_in.shape[1]
    tiles = per // lanes
    width = nb * lanes
    order = (me - jnp.arange(nb, dtype=jnp.int32)) % nb
    place = dp % GROUP
    sizes = [sum(r) for r in RUNS]
    starts = [nb * sum(sizes[:k]) for k in range(len(sizes))]
    assert clip_num == nb * sum(sizes)
    ra, rb = width // GROUP, per // GROUP
    wa = lax.dynamic_slice_in_dim(w_in, place * ra, ra).reshape(ra, tiles, lanes).transpose(1, 0, 2).reshape(-1, lanes)
    wb = lax.dynamic_slice_in_dim(w_out, place * rb, rb).reshape(rb, nb, lanes).transpose(1, 0, 2).reshape(-1, lanes)
    rows = [wa, wb, scale_table, shift_table, conv_weight, conv_bias[None], b_out[None], layer_scale[None], b_in.reshape(-1, lanes)]
    used = sum(r.shape[0] for r in rows[2:])
    small_rows = -(-used // (GROUP * 16)) * GROUP * 16
    share = jnp.pad(jnp.concatenate(rows), ((0, -used % 16), (0, 0)))
    shares = [share] + [ring("chan", nb, d)(share) for d in range(1, nb)]

    packed = []
    for start, n, runs in zip(starts, sizes, RUNS):
        low, parts = 0, []
        for run in runs:
            part = []
            for d in range(1, nb):
                at = start + (me + d) % nb * n + low
                block = jnp.stack([lax.dynamic_slice_in_dim(clips_in, at, run), lax.dynamic_slice_in_dim(grad_out, at, run)])
                part.append(ring("chan", nb, d)(block))
            parts.append(part)
            low += run
        packed.append(parts)

    stacked, prm = stack_call(shares, wa.shape[0] + wb.shape[0], 0)
    meta = jnp.stack([me, place]).astype(jnp.int32)
    gathered, packed[0] = gather_group(stacked, dp_count, packed[0])

    sums = None
    kept, back = [], []
    for k, (start, n) in enumerate(zip(starts, sizes)):
        base = start + me * n
        slot = (base + jnp.arange(n)).astype(jnp.int32)
        spk = lax.dynamic_slice_in_dim(speaker, base, n)
        live = (slot < counts[0]).astype(jnp.int32)
        out = block_call(order, spk, live, slot, meta, clips_in, grad_out, packed[k], prm, gathered, nb * per,
                         taps, speakers, small_rows, sums, HINT if k else 0)
        kept.append(out[nb:nb + 4])
        sums = out[nb + 4]
        sent = out[:nb]
        if k:
            *sent, back[0] = lax.optimization_barrier((*sent, back[0]))
        back.append([sent[0]] + [ring("chan", nb, -d)(sent[d]) for d in range(1, nb)])
    keep, send = grads_call(order, meta, *zip(*kept), sums, 2 * speakers + taps + 3)

    send, *back[0] = lax.optimization_barrier((send, *back[0]))
    got = flip("dp", dp_count, 1)(send)
    total = keep[0] + got[0].astype(F32)
    for m in range(1, GROUP // 2):
        total = total + flip("dp", dp_count, 2 * m)((keep[m] + got[m].astype(F32)).astype(BF16)).astype(F32)
    step = GROUP
    while step < dp_count:
        low = total.astype(BF16)
        total = low.astype(F32) + flip("dp", dp_count, step)(low).astype(F32)
        step *= 2
    total, back[-1] = lax.optimization_barrier((total, back[-1]))
    mine = total[0]
    for d in range(1, nb):
        mine = mine + ring("chan", nb, d)(total[d].astype(BF16)).astype(F32)
    g_in, g_out, g_scale, g_shift, g_conv, g_cb, g_bo, g_ls, g_bi = finish_call(
        meta, gather_small(mine.astype(BF16), dp_count), nb, ra, rb, small_rows // GROUP, tiles, taps, speakers)

    clips_out = jnp.zeros(clips_in.shape, BF16)
    grad_clips = grad_out.astype(F32)
    for k, n in enumerate(sizes):
        for d in range(nb):
            at = starts[k] + (me + d) % nb * n
            clips_out = lax.dynamic_update_slice_in_dim(clips_out, back[k][d][0], at, 0)
            g = lax.dynamic_slice_in_dim(grad_out, at, n).astype(F32) + back[k][d][1].astype(F32)
            grad_clips = lax.dynamic_update_slice_in_dim(grad_clips, g, at, 0)

    return (clips_out, grad_clips, g_conv, g_cb.reshape(lanes), g_scale, g_shift, g_in, g_bi, g_out,
            g_bo.reshape(lanes), g_ls.reshape(lanes))


def solution(mesh):
    act = P("dp", None, "chan")
    col, vec, row = P(None, "chan"), P("chan"), P("chan", None)
    in_specs = (act, P("dp"), P("dp"), col, vec, col, col, col, vec, row, vec, vec, act)
    out_specs = (act, act, col, vec, col, col, col, vec, row, vec, vec)
    return jax.shard_map(per_device, mesh=mesh, in_specs=in_specs, out_specs=out_specs, check_vma=False)
```

time: 180 us -> 161 us (0.89)
  waiting for transfers between devices: 63.1 us -> 36.2 us
  other arithmetic: 10.7 us -> 22.5 us
  Pallas kernels: 47.1 us -> 36.6 us
  local copies, waits for them, and re-layouts: 10.1 us -> 15.4 us
    ppermute x18 -> x21, waiting for transfers between devices: 40 us -> 11 us  [ring(): lax.ppermute(v, axis, [(i, (i + shift) % size) for i in range(size)])]
    pallas_call x3, Pallas kernels: 42.8 us -> 32.2 us  [the longest x2 26.6 us: block_call(): pl.pallas_call(functools.partial(body, nb, taps, speakers, runs, first),...]
    another operation x11, other arithmetic: 5.11 us -> 10.9 us  [the longest x9 10.8 us: per_device(): jnp.stack([lax.dynamic_slice_in_dim(clips_in, at, run), lax.dynamic_slice...]
    dynamic_update_slice x8, other arithmetic: 0.27 us -> 5.97 us  [per_device(): grad_clips = lax.dynamic_update_slice_in_dim(grad_clips, g, at, 0)]
    unnamed x44 -> x66, local copies, waits for them, and re-layouts: 4.03 us -> 8.3 us
    ppermute x12 -> x15, waiting for transfers between devices: 23.1 us -> 25.2 us  [flip(): return lambda v: lax.ppermute(v, axis, [(i, i ^ mask) for i in range(size)])]
    ppermute x12 -> x15, starting transfers between devices: 10.4 us -> 11.5 us  [flip(): return lambda v: lax.ppermute(v, axis, [(i, i ^ mask) for i in range(size)])]
    ppermute x18 -> x21, starting transfers between devices: 36.4 us -> 36.5 us  [ring(): lax.ppermute(v, axis, [(i, (i + shift) % size) for i in range(size)])]
  transfers between devices with their start and end apart: 30 -> 36, of which waited for: 14 -> 11; matrix products, arithmetic and copies ran while one was open for 7% -> 16% of each run, Pallas kernels for 24% -> 21%
where the time goes in v3:
time: 161 us; the launch traced here: 160 us
  starting transfers between devices  47.9 us (30%)
  Pallas kernels  36.6 us (23%)
  waiting for transfers between devices  36.2 us (22%)
  other arithmetic  22.5 us (14%)
  local copies, waits for them, and re-layouts  15.4 us (10%)
  between operations  1.73 us (1%)
    ppermute x21, starting transfers between devices, ring(): lax.ppermute(v, axis, [(i, (i + shift) % size) for i in range(size)])  36.5 us
    pallas_call x2, Pallas kernels, block_call(): pl.pallas_call(functools.partial(body, nb, taps, speakers, runs, first),...  26.6 us
    ppermute x15, waiting for transfers between devices, flip(): return lambda v: lax.ppermute(v, axis, [(i, i ^ mask) for i in range(size)])  25.2 us
    ppermute x15, starting transfers between devices, flip(): return lambda v: lax.ppermute(v, axis, [(i, i ^ mask) for i in range(size)])  11.5 us
    ppermute x21, waiting for transfers between devices, ring(): lax.ppermute(v, axis, [(i, (i + shift) % size) for i in range(size)])  11 us
    another operation x9, other arithmetic, per_device(): jnp.stack([lax.dynamic_slice_in_dim(clips_in, at, run), lax.dynamic_slice...  10.8 us
    unnamed x66, local copies, waits for them, and re-layouts  8.3 us
    dynamic_update_slice x8, other arithmetic, per_device(): grad_clips = lax.dynamic_update_slice_in_dim(grad_clips, g, at, 0)  5.97 us
  transfers between devices with their start and end apart: 36, of which 11 were waited for; matrix products, arithmetic and copies ran while one was open for 16% of the time, Pallas kernels for 21%

profile of v3, /device:TPU:0, one launch (start us, length us, event | category | flops | bytes accessed | tf_op | source)
XLA Modules:
  0.0 160.3 jit_solution(9874414748826614643)
XLA Ops:
  2.5 2.9 %concatenate.3 = bf16[525,128]{1,0:T(8,128)(2,1)S(1)} concatenate(bf16[192,128]{1,0:T(8,128)(2,1)S(1)} %bitcast.141, bf16[192,128]{1,0:T(8,128)(2,1)S(1)} %bitcast.142, bf16[64,128]{1,0:T(8,128)(2,1)} %param.18, bf16[64,128]{1,0:T(8,128)(2,1)} %param.19, bf16[7,128]{1,0:T(8,128)(2,1)} %param.16, bf16[1,128]{1,0:T(2,128)(2,1)} %bitcast.147, bf16[1,128]{1,0:T(2,128)(2,1)} %bitcast.148, ...), dimensions={0} | concatenate | bytes 268800 | tf_op jit(solution)/shard_map/concatenate | solution.py:384
  5.5 3.1 %collective-permute-start = (bf16[528,128]{1,0:T(8,128)(2,1)S(1)}, bf16[528,128]{1,0:T(8,128)(2,1)S(1)}, u32[]{:S(2)}, u32[]{:S(2)}) collective-permute-start(bf16[528,128]{1,0:T(8,128)(2,1)S(1)} %pad.4.refs_0_), channel_id=1, source_target_pairs={{0,1},{1,2},{2,3},{3,0},{4,5},{5,6},{6,7},{7,4},{8,9},{9,10},{10,1... | collective-permute-start | bytes 405512 | tf_op jit(solution)/shard_map/ppermute | solution.py:340
  8.6 2.6 %collective-permute-start.1 = (bf16[528,128]{1,0:T(8,128)(2,1)S(1)}, bf16[528,128]{1,0:T(8,128)(2,1)S(1)}, u32[]{:S(2)}, u32[]{:S(2)}) collective-permute-start(bf16[528,128]{1,0:T(8,128)(2,1)S(1)} %pad.4.refs_0_), channel_id=1, source_target_pairs={{0,2},{1,3},{2,0},{3,1},{4,6},{5,7},{6,4},{7,5},{8,10},{9,11},{10,... | collective-permute-start | bytes 405512 | tf_op jit(solution)/shard_map/ppermute | solution.py:340
  12.5 1.9 %dynamic-slice_bitcast_fusion.6 = (bf16[1,1,256,128]{3,2,1,0:T(8,128)(2,1)S(1)}, bf16[1,1,256,128]{3,2,1,0:T(8,128)(2,1)}, bf16[1,1,256,128]{3,2,1,0:T(8,128)(2,...) fusion(bf16[16,256,128]{2,1,0:T(8,128)(2,1)} %refs_1_.3, ...), kind=kLoop, calls=%fused_computation.56 | loop fusion | bytes 1572888 | tf_op jit(solution)/shard_map/stack | solution.py:394
  20.2 5.2 %collective-permute-start.4 = (bf16[2,1,256,128]{3,2,1,0:T(8,128)(2,1)}, bf16[2,1,256,128]{3,2,1,0:T(8,128)(2,1)}, u32[]{:S(2)}, u32[]{:S(2)}) collective-permute-start(bf16[2,1,256,128]{3,2,1,0:T(8,128)(2,1)} %pad_maximum_fusion.4), channel_id=1, source_target_pairs={{0,1},{1,2},{2,3},{3,0},{4,5},{5,6},{6,7},{7,4},{8,9},{9,10},{10,1... | collective-permute-start | bytes 393224 | tf_op jit(solution)/shard_map/ppermute | solution.py:340
  25.4 5.9 %collective-permute-start.10 = (bf16[2,1,256,128]{3,2,1,0:T(8,128)(2,1)}, bf16[2,1,256,128]{3,2,1,0:T(8,128)(2,1)}, u32[]{:S(2)}, u32[]{:S(2)}) collective-permute-start(bf16[2,1,256,128]{3,2,1,0:T(8,128)(2,1)} %pad_maximum_fusion.9), channel_id=1, source_target_pairs={{0,3},{1,0},{2,1},{3,2},{4,7},{5,4},{6,5},{7,6},{8,11},{9,8},{10,9... | collective-permute-start | bytes 393224 | tf_op jit(solution)/shard_map/ppermute | solution.py:340
  32.0 2.0 %gathered.1 = (bf16[4,384,128]{2,1,0:T(8,128)(2,1)}, f32[4,144,128]{2,1,0:T(8,128)}) custom-call(bf16[528,128]{1,0:T(8,128)(2,1)} %copy-done.21, bf16[528,128]{1,0:T(8,128)(2,1)} %copy-done.29, bf16[528,128]{1,0:T(8,128)(2,1)} %copy-done.30, bf16[528,128]{1,0:T(8,128)(2,1)} %copy-done.31), custom_call_target="tpu_custom_call" | custom-call | tf_op jit(solution)/shard_map/gathered/pallas_call | solution.py:290
  45.4 3.6 %collective-permute-done.8.refs_5_ = bf16[2,1,256,128]{3,2,1,0:T(8,128)(2,1)} collective-permute-done((bf16[2,1,256,128]{3,2,1,0:T(8,128)(2,1)}, bf16[2,1,256,128]{3,2,1,0:T(8,128)(2,1)}, u32[]{:S(2)}, u32[]{:S(2)}) %collective-permute-start.8) | collective-permute-done | bytes 131104 | tf_op jit(solution)/shard_map/ppermute | solution.py:340
  50.7 4.5 %collective-permute-done.9.refs_6_ = bf16[2,1,256,128]{3,2,1,0:T(8,128)(2,1)} collective-permute-done((bf16[2,1,256,128]{3,2,1,0:T(8,128)(2,1)}, bf16[2,1,256,128]{3,2,1,0:T(8,128)(2,1)}, u32[]{:S(2)}, u32[]{:S(2)}) %collective-permute-start.9) | collective-permute-done | bytes 131104 | tf_op jit(solution)/shard_map/ppermute | solution.py:340
  55.2 3.8 %collective-permute-done.7.refs_15_.refs_12_ = bf16[4,384,128]{2,1,0:T(8,128)(2,1)} collective-permute-done((bf16[4,384,128]{2,1,0:T(8,128)(2,1)S(1)}, bf16[4,384,128]{2,1,0:T(8,128)(2,1)}, u32[]{:S(2)}, u32[]{:S(2)}) %collective-permute-start.7) | collective-permute-done | bytes 393248 | tf_op jit(solution)/shard_map/ppermute | solution.py:344
  60.7 2.4 %collective-permute-start.18 = (bf16[2,2,256,128]{3,2,1,0:T(8,128)(2,1)}, bf16[2,2,256,128]{3,2,1,0:T(8,128)(2,1)}, u32[]{:S(2)}, u32[]{:S(2)}) collective-permute-start(bf16[2,2,256,128]{3,2,1,0:T(8,128)(2,1)} %pad_maximum_fusion.3), channel_id=1, source_target_pairs={{0,3},{1,0},{2,1},{3,2},{4,7},{5,4},{6,5},{7,6},{8,11},{9,8},{10,9... | collective-permute-start | bytes 786440 | tf_op jit(solution)/shard_map/ppermute | solution.py:340
  64.7 13.3 %block.2 = (bf16[2,2,256,128]{3,2,1,0:T(8,128)(2,1)S(1)}, bf16[2,2,256,128]{3,2,1,0:T(8,128)(2,1)S(1)}, bf16[2,2,256,128]{3,2,1,0:T(8,128)(2,1)S(1)}, bf16[2,2,2...) custom-call(s32[4]{0:T(128)S(1)} %and_select_fusion.order_ref, ...), custom_call_target="tpu_custom_call" | custom-call | tf_op jit(solution)/shard_map/block/pallas_call | solution.py:209
  80.7 2.0 %collective-permute-start.21 = (bf16[2,2,256,128]{3,2,1,0:T(8,128)(2,1)S(1)}, bf16[2,2,256,128]{3,2,1,0:T(8,128)(2,1)S(1)}, u32[]{:S(2)}, u32[]{:S(2)}) collective-permute-start(bf16[2,2,256,128]{3,2,1,0:T(8,128)(2,1)S(1)} %get-tuple-element.96), channel_id=1, source_target_pairs={{0,1},{1,2},{2,3},{3,0},{4,5},{5,6},{6,7},{7,4},{8,9},{9,10},{10,1... | collective-permute-start | bytes 786440 | tf_op jit(solution)/shard_map/ppermute | solution.py:340
  82.8 13.3 %block.3 = (bf16[2,2,256,128]{3,2,1,0:T(8,128)(2,1)S(1)}, bf16[2,2,256,128]{3,2,1,0:T(8,128)(2,1)S(1)}, bf16[2,2,256,128]{3,2,1,0:T(8,128)(2,1)S(1)}, bf16[2,2,2...) custom-call(s32[4]{0:T(128)S(1)} %and_select_fusion.order_ref, ...), custom_call_target="tpu_custom_call" | custom-call | flops 68719476736 | tf_op jit(solution)/shard_map/block/pallas_call | solution.py:209
  97.5 5.6 %weight_grads.1 = (f32[4,4,416,128]{3,2,1,0:T(8,128)S(1)}, bf16[4,4,416,128]{3,2,1,0:T(8,128)(2,1)}) custom-call(s32[4]{0:T(128)S(1)} %and_select_fusion.order_ref, s32[2]{0:T(128)S(1)} %pad_add_fusion.meta_ref, bf16[512,512]{1,0:T(8,128)(2,1)S(1)} %bitcast.132, bf16[512,512]{1,0:T(8,128)(2,1)S(1)} %bitcast.136, bf16[512,512]{1,0:T(8,128)(2,1)S(1)} %bitcast.133, ...), custom_call_target="tpu_custom_call" | custom-call | flops 68719476736 | tf_op jit(solution)/shard_map/weight_grads/pallas_call | solution.py:269
  103.2 1.7 %copy-done.2 = f32[4,4,416,128]{3,2,1,0:T(8,128)} copy-done((f32[4,4,416,128]{3,2,1,0:T(8,128)}, f32[4,4,416,128]{3,2,1,0:T(8,128)S(1)}, u32[]{:S(2)}) %copy-start.2) | copy-done | bytes 3407896
  107.3 1.8 %collective-permute-start.26 = (bf16[2,2,256,128]{3,2,1,0:T(8,128)(2,1)S(1)}, bf16[2,2,256,128]{3,2,1,0:T(8,128)(2,1)S(1)}, u32[]{:S(2)}, u32[]{:S(2)}) collective-permute-start(bf16[2,2,256,128]{3,2,1,0:T(8,128)(2,1)S(1)} %copy-done.16), channel_id=1, source_target_pairs={{0,3},{1,0},{2,1},{3,2},{4,7},{5,4},{6,5},{7,6},{8,11},{9,8},{10,9... | collective-permute-start | bytes 786440 | tf_op jit(solution)/shard_map/ppermute | solution.py:340
  117.6 8.4 %collective-permute-done.23 = bf16[4,416,128]{2,1,0:T(8,128)(2,1)S(1)} collective-permute-done((bf16[4,416,128]{2,1,0:T(8,128)(2,1)S(1)}, bf16[4,416,128]{2,1,0:T(8,128)(2,1)S(1)}, u32[]{:S(2)}, u32[]{:S(2)}) %collective-permute-start.23) | collective-permute-done | bytes 426016 | tf_op jit(solution)/shard_map/ppermute | solution.py:344
  127.2 6.5 %collective-permute-done.24 = bf16[4,416,128]{2,1,0:T(8,128)(2,1)S(1)} collective-permute-done((bf16[4,416,128]{2,1,0:T(8,128)(2,1)S(1)}, bf16[4,416,128]{2,1,0:T(8,128)(2,1)S(1)}, u32[]{:S(2)}, u32[]{:S(2)}) %collective-permute-start.24) | collective-permute-done | bytes 426016 | tf_op jit(solution)/shard_map/ppermute | solution.py:344
  137.7 2.0 %collective-permute-start.30 = (bf16[416,128]{1,0:T(8,128)(2,1)S(1)}, bf16[416,128]{1,0:T(8,128)(2,1)S(1)}, u32[]{:S(2)}, u32[]{:S(2)}) collective-permute-start(bf16[416,128]{1,0:T(8,128)(2,1)S(1)} %get-tuple-element.148), channel_id=1, source_target_pairs={{0,2},{1,3},{2,0},{3,1},{4,6},{5,7},{6,4},{7,5},{8,10},{9,11},{10,... | collective-permute-start | bytes 319496 | tf_op jit(solution)/shard_map/ppermute | solution.py:340
  139.6 2.7 %collective-permute-start.31 = (bf16[416,128]{1,0:T(8,128)(2,1)S(1)}, bf16[416,128]{1,0:T(8,128)(2,1)S(1)}, u32[]{:S(2)}, u32[]{:S(2)}) collective-permute-start(bf16[416,128]{1,0:T(8,128)(2,1)S(1)} %get-tuple-element.147), channel_id=1, source_target_pairs={{0,3},{1,0},{2,1},{3,2},{4,7},{5,4},{6,5},{7,6},{8,11},{9,8},{10,9... | collective-permute-start | bytes 319496 | tf_op jit(solution)/shard_map/ppermute | solution.py:340
  144.6 2.9 %collective-permute-done.30 = bf16[416,128]{1,0:T(8,128)(2,1)S(1)} collective-permute-done((bf16[416,128]{1,0:T(8,128)(2,1)S(1)}, bf16[416,128]{1,0:T(8,128)(2,1)S(1)}, u32[]{:S(2)}, u32[]{:S(2)}) %collective-permute-start.30) | collective-permute-done | bytes 106528 | tf_op jit(solution)/shard_map/ppermute | solution.py:340
  152.9 2.3 %collective-permute-done.34 = bf16[416,128]{1,0:T(8,128)(2,1)S(1)} collective-permute-done((bf16[416,128]{1,0:T(8,128)(2,1)S(1)}, bf16[416,128]{1,0:T(8,128)(2,1)S(1)}, u32[]{:S(2)}, u32[]{:S(2)}) %collective-permute-start.34) | collective-permute-done | bytes 106528 | tf_op jit(solution)/shard_map/ppermute | solution.py:344
  157.9 2.4 %finish.1 = (f32[512,384]{1,0:T(8,128)}, f32[384,512]{1,0:T(8,128)}, f32[64,128]{1,0:T(8,128)}, f32[64,128]{1,0:T(8,128)}, f32[7,128]{1,0:T(8,128)}, /*index=5*/...) custom-call(s32[2]{0:T(128)} %copy-done.10, bf16[4,416,128]{2,1,0:T(8,128)(2,1)} %copy-done.19, ...), custom_call_target="tpu_custom_call" | custom-call | tf_op jit(solution)/shard_map/finish/pallas_call | solution.py:329
  (169 shorter events, 55.7 us)
Async XLA Ops:
  5.5 14.7 %collective-permute-start = (bf16[528,128]{1,0:T(8,128)(2,1)S(1)}, bf16[528,128]{1,0:T(8,128)(2,1)S(1)}, u32[]{:S(2)}, u32[]{:S(2)}) collective-permute-start(bf16[528,128]{1,0:T(8,128)(2,1)S(1)} %pad.4.refs_0_), channel_id=1, source_target_pairs={{0,1},{1,2},{2,3},{3,0},{4,5},{5,6},{6,7},{7,4},{8,9},{9,10},{10,1... | collective-permute-start | bytes 405512 | tf_op jit(solution)/shard_map/ppermute | solution.py:340
  8.6 16.8 %collective-permute-start.1 = (bf16[528,128]{1,0:T(8,128)(2,1)S(1)}, bf16[528,128]{1,0:T(8,128)(2,1)S(1)}, u32[]{:S(2)}, u32[]{:S(2)}) collective-permute-start(bf16[528,128]{1,0:T(8,128)(2,1)S(1)} %pad.4.refs_0_), channel_id=1, source_target_pairs={{0,2},{1,3},{2,0},{3,1},{4,6},{5,7},{6,4},{7,5},{8,10},{9,11},{10,... | collective-permute-start | bytes 405512 | tf_op jit(solution)/shard_map/ppermute | solution.py:340
  11.2 20.1 %collective-permute-start.2 = (bf16[528,128]{1,0:T(8,128)(2,1)S(1)}, bf16[528,128]{1,0:T(8,128)(2,1)S(1)}, u32[]{:S(2)}, u32[]{:S(2)}) collective-permute-start(bf16[528,128]{1,0:T(8,128)(2,1)S(1)} %pad.4.refs_0_), channel_id=1, source_target_pairs={{0,3},{1,0},{2,1},{3,2},{4,7},{5,4},{6,5},{7,6},{8,11},{9,8},{10,9... | collective-permute-start | bytes 405512 | tf_op jit(solution)/shard_map/ppermute | solution.py:340
  15.1 26.9 %collective-permute-start.6 = (bf16[2,1,256,128]{3,2,1,0:T(8,128)(2,1)}, bf16[2,1,256,128]{3,2,1,0:T(8,128)(2,1)S(1)}, u32[]{:S(2)}, u32[]{:S(2)}) collective-permute-start(bf16[2,1,256,128]{3,2,1,0:T(8,128)(2,1)} %pad_maximum_fusion.6), channel_id=1, source_target_pairs={{0,3},{1,0},{2,1},{3,2},{4,7},{5,4},{6,5},{7,6},{8,11},{9,8},{10,9... | collective-permute-start | bytes 393224 | tf_op jit(solution)/shard_map/ppermute | solution.py:340
  16.2 25.7 %collective-permute-start.5 = (bf16[2,1,256,128]{3,2,1,0:T(8,128)(2,1)}, bf16[2,1,256,128]{3,2,1,0:T(8,128)(2,1)S(1)}, u32[]{:S(2)}, u32[]{:S(2)}) collective-permute-start(bf16[2,1,256,128]{3,2,1,0:T(8,128)(2,1)} %pad_maximum_fusion.5), channel_id=1, source_target_pairs={{0,2},{1,3},{2,0},{3,1},{4,6},{5,7},{6,4},{7,5},{8,10},{9,11},{10,... | collective-permute-start | bytes 393224 | tf_op jit(solution)/shard_map/ppermute | solution.py:340
  20.2 23.4 %collective-permute-start.4 = (bf16[2,1,256,128]{3,2,1,0:T(8,128)(2,1)}, bf16[2,1,256,128]{3,2,1,0:T(8,128)(2,1)}, u32[]{:S(2)}, u32[]{:S(2)}) collective-permute-start(bf16[2,1,256,128]{3,2,1,0:T(8,128)(2,1)} %pad_maximum_fusion.4), channel_id=1, source_target_pairs={{0,1},{1,2},{2,3},{3,0},{4,5},{5,6},{6,7},{7,4},{8,9},{9,10},{10,1... | collective-permute-start | bytes 393224 | tf_op jit(solution)/shard_map/ppermute | solution.py:340
  25.4 18.8 %collective-permute-start.10 = (bf16[2,1,256,128]{3,2,1,0:T(8,128)(2,1)}, bf16[2,1,256,128]{3,2,1,0:T(8,128)(2,1)}, u32[]{:S(2)}, u32[]{:S(2)}) collective-permute-start(bf16[2,1,256,128]{3,2,1,0:T(8,128)(2,1)} %pad_maximum_fusion.9), channel_id=1, source_target_pairs={{0,3},{1,0},{2,1},{3,2},{4,7},{5,4},{6,5},{7,6},{8,11},{9,8},{10,9... | collective-permute-start | bytes 393224 | tf_op jit(solution)/shard_map/ppermute | solution.py:340
  42.0 13.3 %collective-permute-start.13 = (bf16[4,384,128]{2,1,0:T(8,128)(2,1)}, bf16[4,384,128]{2,1,0:T(8,128)(2,1)}, u32[]{:S(2)}, u32[]{:S(2)}) collective-permute-start(bf16[4,384,128]{2,1,0:T(8,128)(2,1)} %get-tuple-element.68.refs_9_.refs_6_), channel_id=1, source_target_pairs={{0,16},{4,20},{8,24},{12,28},{16,0},{20,4},{24,8},{28,12},{1,17},{... | collective-permute-start | bytes 1179656 | tf_op jit(solution)/shard_map/ppermute | solution.py:344
  43.5 15.5 %collective-permute-start.7 = (bf16[4,384,128]{2,1,0:T(8,128)(2,1)S(1)}, bf16[4,384,128]{2,1,0:T(8,128)(2,1)}, u32[]{:S(2)}, u32[]{:S(2)}) collective-permute-start(bf16[4,384,128]{2,1,0:T(8,128)(2,1)S(1)} %collective-permute-done.3.refs_11_.refs_8_), channel_id=1, source_target_pairs={{0,16},{4,20},{8,24},{12,28},{16,0},{20,4},{24,8},{28,12},{1,17},{... | collective-permute-start | bytes 1179656 | tf_op jit(solution)/shard_map/ppermute | solution.py:344
  44.3 15.3 %collective-permute-start.11 = (bf16[4,384,128]{2,1,0:T(8,128)(2,1)}, bf16[4,384,128]{2,1,0:T(8,128)(2,1)}, u32[]{:S(2)}, u32[]{:S(2)}) collective-permute-start(bf16[4,384,128]{2,1,0:T(8,128)(2,1)} %get-tuple-element.68.refs_9_.refs_6_), channel_id=1, source_target_pairs={{0,4},{4,0},{8,12},{12,8},{16,20},{20,16},{24,28},{28,24},{1,5},{5... | collective-permute-start | bytes 1179656 | tf_op jit(solution)/shard_map/ppermute | solution.py:344
  44.3 16.4 %collective-permute-start.12 = (bf16[4,384,128]{2,1,0:T(8,128)(2,1)S(1)}, bf16[4,384,128]{2,1,0:T(8,128)(2,1)}, u32[]{:S(2)}, u32[]{:S(2)}) collective-permute-start(bf16[4,384,128]{2,1,0:T(8,128)(2,1)S(1)} %collective-permute-done.3.refs_11_.refs_8_), channel_id=1, source_target_pairs={{0,4},{4,0},{8,12},{12,8},{16,20},{20,16},{24,28},{28,24},{1,5},{5... | collective-permute-start | bytes 1179656 | tf_op jit(solution)/shard_map/ppermute | solution.py:344
  55.2 25.5 %collective-permute-start.16 = (bf16[2,2,256,128]{3,2,1,0:T(8,128)(2,1)}, bf16[2,2,256,128]{3,2,1,0:T(8,128)(2,1)}, u32[]{:S(2)}, u32[]{:S(2)}) collective-permute-start(bf16[2,2,256,128]{3,2,1,0:T(8,128)(2,1)} %pad_maximum_fusion.1), channel_id=1, source_target_pairs={{0,1},{1,2},{2,3},{3,0},{4,5},{5,6},{6,7},{7,4},{8,9},{9,10},{10,1... | collective-permute-start | bytes 786440 | tf_op jit(solution)/shard_map/ppermute | solution.py:340
  59.5 23.2 %collective-permute-start.17 = (bf16[2,2,256,128]{3,2,1,0:T(8,128)(2,1)}, bf16[2,2,256,128]{3,2,1,0:T(8,128)(2,1)}, u32[]{:S(2)}, u32[]{:S(2)}) collective-permute-start(bf16[2,2,256,128]{3,2,1,0:T(8,128)(2,1)} %pad_maximum_fusion.2), channel_id=1, source_target_pairs={{0,2},{1,3},{2,0},{3,1},{4,6},{5,7},{6,4},{7,5},{8,10},{9,11},{10,... | collective-permute-start | bytes 786440 | tf_op jit(solution)/shard_map/ppermute | solution.py:340
  60.7 22.1 %collective-permute-start.18 = (bf16[2,2,256,128]{3,2,1,0:T(8,128)(2,1)}, bf16[2,2,256,128]{3,2,1,0:T(8,128)(2,1)}, u32[]{:S(2)}, u32[]{:S(2)}) collective-permute-start(bf16[2,2,256,128]{3,2,1,0:T(8,128)(2,1)} %pad_maximum_fusion.3), channel_id=1, source_target_pairs={{0,3},{1,0},{2,1},{3,2},{4,7},{5,4},{6,5},{7,6},{8,11},{9,8},{10,9... | collective-permute-start | bytes 786440 | tf_op jit(solution)/shard_map/ppermute | solution.py:340
  78.8 26.1 %collective-permute-start.19 = (bf16[2,2,256,128]{3,2,1,0:T(8,128)(2,1)S(1)}, bf16[2,2,256,128]{3,2,1,0:T(8,128)(2,1)S(1)}, u32[]{:S(2)}, u32[]{:S(2)}) collective-permute-start(bf16[2,2,256,128]{3,2,1,0:T(8,128)(2,1)S(1)} %get-tuple-element.94), channel_id=1, source_target_pairs={{0,3},{1,0},{2,1},{3,2},{4,7},{5,4},{6,5},{7,6},{8,11},{9,8},{10,9... | collective-permute-start | bytes 786440 | tf_op jit(solution)/shard_map/ppermute | solution.py:340
  79.6 25.3 %collective-permute-start.20 = (bf16[2,2,256,128]{3,2,1,0:T(8,128)(2,1)S(1)}, bf16[2,2,256,128]{3,2,1,0:T(8,128)(2,1)S(1)}, u32[]{:S(2)}, u32[]{:S(2)}) collective-permute-start(bf16[2,2,256,128]{3,2,1,0:T(8,128)(2,1)S(1)} %get-tuple-element.95), channel_id=1, source_target_pairs={{0,2},{1,3},{2,0},{3,1},{4,6},{5,7},{6,4},{7,5},{8,10},{9,11},{10,... | collective-permute-start | bytes 786440 | tf_op jit(solution)/shard_map/ppermute | solution.py:340
  80.7 24.2 %collective-permute-start.21 = (bf16[2,2,256,128]{3,2,1,0:T(8,128)(2,1)S(1)}, bf16[2,2,256,128]{3,2,1,0:T(8,128)(2,1)S(1)}, u32[]{:S(2)}, u32[]{:S(2)}) collective-permute-start(bf16[2,2,256,128]{3,2,1,0:T(8,128)(2,1)S(1)} %get-tuple-element.96), channel_id=1, source_target_pairs={{0,1},{1,2},{2,3},{3,0},{4,5},{5,6},{6,7},{7,4},{8,9},{9,10},{10,1... | collective-permute-start | bytes 786440 | tf_op jit(solution)/shard_map/ppermute | solution.py:340
  107.3 29.3 %collective-permute-start.26 = (bf16[2,2,256,128]{3,2,1,0:T(8,128)(2,1)S(1)}, bf16[2,2,256,128]{3,2,1,0:T(8,128)(2,1)S(1)}, u32[]{:S(2)}, u32[]{:S(2)}) collective-permute-start(bf16[2,2,256,128]{3,2,1,0:T(8,128)(2,1)S(1)} %copy-done.16), channel_id=1, source_target_pairs={{0,3},{1,0},{2,1},{3,2},{4,7},{5,4},{6,5},{7,6},{8,11},{9,8},{10,9... | collective-permute-start | bytes 786440 | tf_op jit(solution)/shard_map/ppermute | solution.py:340
  109.1 27.5 %collective-permute-start.27 = (bf16[2,2,256,128]{3,2,1,0:T(8,128)(2,1)S(1)}, bf16[2,2,256,128]{3,2,1,0:T(8,128)(2,1)S(1)}, u32[]{:S(2)}, u32[]{:S(2)}) collective-permute-start(bf16[2,2,256,128]{3,2,1,0:T(8,128)(2,1)S(1)} %copy-done.14), channel_id=1, source_target_pairs={{0,2},{1,3},{2,0},{3,1},{4,6},{5,7},{6,4},{7,5},{8,10},{9,11},{10,... | collective-permute-start | bytes 786440 | tf_op jit(solution)/shard_map/ppermute | solution.py:340
  113.3 12.8 %collective-permute-start.23 = (bf16[4,416,128]{2,1,0:T(8,128)(2,1)S(1)}, bf16[4,416,128]{2,1,0:T(8,128)(2,1)S(1)}, u32[]{:S(2)}, u32[]{:S(2)}) collective-permute-start(bf16[4,416,128]{2,1,0:T(8,128)(2,1)S(1)} %get-tuple-element.125), channel_id=1, source_target_pairs={{0,8},{4,12},{8,0},{12,4},{16,24},{20,28},{24,16},{28,20},{1,9},{5... | collective-permute-start | bytes 1277960 | tf_op jit(solution)/shard_map/ppermute | solution.py:344
  113.9 19.8 %collective-permute-start.24 = (bf16[4,416,128]{2,1,0:T(8,128)(2,1)S(1)}, bf16[4,416,128]{2,1,0:T(8,128)(2,1)S(1)}, u32[]{:S(2)}, u32[]{:S(2)}) collective-permute-start(bf16[4,416,128]{2,1,0:T(8,128)(2,1)S(1)} %get-tuple-element.127), channel_id=1, source_target_pairs={{0,16},{4,20},{8,24},{12,28},{16,0},{20,4},{24,8},{28,12},{1,17},{... | collective-permute-start | bytes 1277960 | tf_op jit(solution)/shard_map/ppermute | solution.py:344
  115.4 20.0 %collective-permute-start.25 = (bf16[4,416,128]{2,1,0:T(8,128)(2,1)S(1)}, bf16[4,416,128]{2,1,0:T(8,128)(2,1)S(1)}, u32[]{:S(2)}, u32[]{:S(2)}) collective-permute-start(bf16[4,416,128]{2,1,0:T(8,128)(2,1)S(1)} %get-tuple-element.126), channel_id=1, source_target_pairs={{0,24},{4,28},{8,16},{12,20},{16,8},{20,12},{24,0},{28,4},{1,25},{... | collective-permute-start | bytes 1277960 | tf_op jit(solution)/shard_map/ppermute | solution.py:344
  126.0 10.6 %collective-permute-start.28 = (bf16[2,2,256,128]{3,2,1,0:T(8,128)(2,1)S(1)}, bf16[2,2,256,128]{3,2,1,0:T(8,128)(2,1)S(1)}, u32[]{:S(2)}, u32[]{:S(2)}) collective-permute-start(bf16[2,2,256,128]{3,2,1,0:T(8,128)(2,1)S(1)} %copy-done.12), channel_id=1, source_target_pairs={{0,1},{1,2},{2,3},{3,0},{4,5},{5,6},{6,7},{7,4},{8,9},{9,10},{10,1... | collective-permute-start | bytes 786440 | tf_op jit(solution)/shard_map/ppermute | solution.py:340
  137.7 9.8 %collective-permute-start.30 = (bf16[416,128]{1,0:T(8,128)(2,1)S(1)}, bf16[416,128]{1,0:T(8,128)(2,1)S(1)}, u32[]{:S(2)}, u32[]{:S(2)}) collective-permute-start(bf16[416,128]{1,0:T(8,128)(2,1)S(1)} %get-tuple-element.148), channel_id=1, source_target_pairs={{0,2},{1,3},{2,0},{3,1},{4,6},{5,7},{6,4},{7,5},{8,10},{9,11},{10,... | collective-permute-start | bytes 319496 | tf_op jit(solution)/shard_map/ppermute | solution.py:340
  (45 other events, 365.2 us)

commit v4 on v3

v4 whole, which is shorter than its diff:
```python
import functools

import jax
import jax.numpy as jnp
from jax import lax
from jax.experimental import pallas as pl
from jax.experimental.pallas import tpu as pltpu
from jax.sharding import PartitionSpec as P

RUNS = ((1, 1), (2,))
GROUP = 8

EPS = 1e-06
ROOT_TWO_PI = 2.5066282746310002
F32 = jnp.float32
BF16 = jnp.bfloat16
PAD = 8
HINT = 1 << 36


def gelu_pair(v):
    z = jnp.abs(v)
    t = 1.0 / (1.0 + (0.3275911 * 0.7071067811865476) * z)
    e = jnp.exp(v * v * -0.5)
    poly = t * (0.5 * 0.254829592 + t * (0.5 * -0.284496736 + t * (0.5 * 1.421413741 + t * (0.5 * -1.453152027 + t * (0.5 * 1.061405429)))))
    tail = poly * e
    cdf = jnp.where(v >= 0.0, 1.0 - tail, tail)
    return v * cdf, cdf + v * (e * (1.0 / ROOT_TWO_PI))


def dot(a, b, ca, cb):
    return lax.dot_general(a, b, (((ca,), (cb,)), ((), ())), preferred_element_type=F32)


def body(n_blocks, taps, speakers, runs, first, last,
         order_ref, spk_ref, live_ref, slot_ref, meta_ref, *refs):
    nb = n_blocks
    x0, g0 = refs[:2]
    k = 2
    p = []
    for _ in runs:
        p.append(refs[k:k + nb - 1])
        k += nb - 1
    shares = refs[k:k + GROUP]
    k += GROUP
    if not first:
        got = refs[k]
        k += 1
    if last:
        before = refs[k:k + 4]
        k += 4
    o = refs[k:k + nb]
    k += nb
    if last:
        keep, send = refs[k:k + 2]
        k += 2
        (gwi, gwo, *held, sems) = refs[-7:]
    (nlow_all, blow_all, act_all, plow_all, gsm, xpad, gpad, normed, gin, slope, wide, b_in, w_in, w_out, prm) = refs[k:k + 15]
    i = pl.program_id(0)
    length, lanes = normed.shape[1], normed.shape[2]
    width = nb * lanes
    ff = act_all.shape[2]
    per = ff // nb
    tiles = per // lanes
    margin = taps // 2
    r_conv, r_cb = 2 * speakers, 2 * speakers + taps
    r_bo, r_ls, r_bi = r_cb + 1, r_cb + 2, r_cb + 3
    cols = [pl.multiple_of(order_ref[d] * lanes, lanes) for d in range(nb)]

    @pl.when(i == 0)
    def _():
        for d in range(nb):
            zero = jnp.zeros((PAD, lanes), F32)
            xpad[d, 0:PAD, :] = zero
            xpad[d, PAD + length:, :] = zero
            gpad[d, 0:PAD, :] = zero
            gpad[d, PAD + length:, :] = zero
        gsm[...] = jnp.zeros_like(gsm) if first else got[...]
        ra, rb, rs = width // GROUP, per // GROUP, prm.shape[1] // GROUP
        for s in range(GROUP):
            part = meta_ref[1] ^ s

            def unpack(d, carry):
                c = order_ref[d]
                for r in range(tiles):
                    w_in[pl.ds(pl.multiple_of(part * ra, ra), ra), pl.ds(pl.multiple_of(c * per + r * lanes, lanes), lanes)] = shares[s][d, r * ra:(r + 1) * ra, :]
                base = tiles * ra
                for r in range(nb):
                    w_out[pl.ds(pl.multiple_of(c * per + part * rb, 16), rb), r * lanes:(r + 1) * lanes] = shares[s][d, base + r * rb:base + (r + 1) * rb, :]
                base += nb * rb
                prm[d, pl.ds(pl.multiple_of(part * rs, rs), rs), :] = shares[s][d, base:base + rs, :].astype(F32)
                return carry
            lax.fori_loop(0, nb, unpack, 0)
        for d in range(nb):
            for r in range(tiles):
                at = pl.multiple_of(order_ref[d] * per + r * lanes, lanes)
                b_in[:, pl.ds(at, lanes)] = prm[d, r_bi + r:r_bi + r + 1, :]

        if last:
            for j in range(4):
                pltpu.make_async_copy(before[j], held[j], sems.at[j]).start()

    row = i if last else 0
    nlow, blow, act, plow = (v.at[row] for v in (nlow_all, blow_all, act_all, plow_all))
    xpad[0, PAD:PAD + length, :] = x0[0].astype(F32)
    gin[0] = g0[0]
    low = 0
    for run, part in zip(runs, p):
        @pl.when((i >= low) & (i < low + run))
        def _(low=low, run=run, part=part):
            at = i - low if run > 1 else 0
            for d in range(1, nb):
                xpad[d, PAD:PAD + length, :] = part[d - 1][0, at].astype(F32)
                gin[d] = part[d - 1][1, at]
        low += run

    spk = spk_ref[i]
    live = live_ref[i].astype(F32)
    total = jnp.zeros((length, 1), F32)
    for d in range(nb):
        acc = jnp.broadcast_to(prm[d, r_cb:r_cb + 1, :], (length, lanes))
        for t in range(taps):
            s = PAD - margin + t
            acc = acc + prm[d, r_conv + t:r_conv + t + 1, :] * xpad[d, s:s + length, :]
        normed[d] = acc
        total = total + jnp.sum(acc, 1, keepdims=True)
    mean = total / width
    square = jnp.zeros((length, 1), F32)
    for d in range(nb):
        c = normed[d] - mean
        normed[d] = c
        square = square + jnp.sum(c * c, 1, keepdims=True)
    inv = lax.rsqrt(square / width + EPS)
    for d in range(nb):
        v = normed[d] * inv
        normed[d] = v
        sc = prm[d, pl.ds(spk, 1), :]
        sh = prm[d, pl.ds(speakers + spk, 1), :]
        nlow[:, pl.ds(cols[d], lanes)] = (v * sc + sh).astype(BF16)

    step = 256
    for f in range(0, ff, step):
        pre = dot(nlow[...], w_in[:, f:f + step], 1, 0) + b_in[:, f:f + step]
        a, s = gelu_pair(pre)
        act[:, f:f + step] = a.astype(BF16)
        slope[:, f:f + step] = s
    wide[...] = dot(act[...], w_out[...], 1, 0)
    for d in range(nb):
        b = wide[:, pl.ds(cols[d], lanes)] + prm[d, r_bo:r_bo + 1, :]
        ls = prm[d, r_ls:r_ls + 1, :] * live
        x = xpad[d, PAD:PAD + length, :]
        g = gin[d].astype(F32)
        o[d][0, 0] = (x + b * ls).astype(BF16)
        gb = g * ls
        gsm[d, r_bo:r_bo + 1, :] += jnp.sum(gb, 0, keepdims=True)
        gsm[d, r_ls:r_ls + 1, :] += jnp.sum(g * b, 0, keepdims=True) * live
        blow[:, pl.ds(cols[d], lanes)] = gb.astype(BF16)
    for f in range(0, ff, step):
        gp = dot(blow[...], w_out[f:f + step, :], 1, 1) * slope[:, f:f + step]
        plow[:, f:f + step] = gp.astype(BF16)
        gsum = jnp.sum(gp, 0, keepdims=True)
        for r in range(step // lanes):
            q = f // lanes + r
            gsm[nb, q:q + 1, :] += gsum[:, r * lanes:(r + 1) * lanes]
    wide[...] = dot(plow[...], w_in[...], 1, 1)
    m1 = jnp.zeros((length, 1), F32)
    m2 = jnp.zeros((length, 1), F32)
    for d in range(nb):
        gn = wide[:, pl.ds(cols[d], lanes)]
        v = normed[d]
        gv = gn * v
        gsm[d, pl.ds(spk, 1), :] += jnp.sum(gv, 0, keepdims=True)
        gsm[d, pl.ds(speakers + spk, 1), :] += jnp.sum(gn, 0, keepdims=True)
        sc = prm[d, pl.ds(spk, 1), :]
        m1 = m1 + jnp.sum(gn * sc, 1, keepdims=True)
        m2 = m2 + jnp.sum(gv * sc, 1, keepdims=True)
    m1 = m1 / width
    m2 = m2 / width
    for d in range(nb):
        sc = prm[d, pl.ds(spk, 1), :]
        gc = (wide[:, pl.ds(cols[d], lanes)] * sc - m1 - normed[d] * m2) * inv
        gpad[d, PAD:PAD + length, :] = gc
        gsm[d, r_cb:r_cb + 1, :] += jnp.sum(gc, 0, keepdims=True)
        acc = jnp.zeros((length, lanes), F32)
        for t in range(taps):
            s = PAD - margin + t
            gsm[d, r_conv + t:r_conv + t + 1, :] += jnp.sum(xpad[d, s:s + length, :] * gc, 0, keepdims=True)
            s = PAD + margin - t
            acc = acc + prm[d, r_conv + t:r_conv + t + 1, :] * gpad[d, s:s + length, :]
        o[d][1, 0] = acc.astype(BF16)

    if last:
        @pl.when(i == pl.num_programs(0) - 1)
        def _():
            for j in range(4):
                pltpu.make_async_copy(before[j], held[j], sems.at[j]).wait()
            flat = [v[...].reshape(-1, v.shape[2]) for v in (nlow_all, blow_all)]
            heads = [v[...].reshape(-1, v.shape[2]) for v in held[:2]]
            for f in range(0, ff, step):
                cut = lambda v: v[:, :, f:f + step].reshape(-1, step)
                da = dot(flat[0], cut(plow_all), 0, 0) + dot(heads[0], cut(held[3]), 0, 0)
                for r in range(step // lanes):
                    gwi[f // lanes + r] = da[:, r * lanes:(r + 1) * lanes]
                gwo[f:f + step, :] = dot(cut(act_all), flat[1], 0, 0) + dot(cut(held[2]), heads[1], 0, 0)
            for d in range(nb):
                for r in range(tiles):
                    gsm[d, r_bi + r:r_bi + r + 1, :] = gsm[nb, pl.ds(order_ref[d] * tiles + r, 1), :]
            place = meta_ref[1]
            ra, rb, rs = width // GROUP, per // GROUP, gsm.shape[1] // GROUP

            def emit(m, carry):
                for e in range(nb):
                    d = -e % nb
                    c = order_ref[d]
                    for out, part in ((keep, place ^ (2 * m)), (send, place ^ (2 * m) ^ 1)):
                        for r in range(tiles):
                            v = gwi[c * tiles + r, pl.ds(pl.multiple_of(part * ra, ra), ra), :]
                            out[m, e, r * ra:(r + 1) * ra, :] = v.astype(out.dtype)
                        base = tiles * ra
                        for r in range(nb):
                            v = gwo[pl.ds(pl.multiple_of(c * per + part * rb, 16), rb), r * lanes:(r + 1) * lanes]
                            out[m, e, base + r * rb:base + (r + 1) * rb, :] = v.astype(out.dtype)
                        base += nb * rb
                        v = gsm[d, pl.ds(pl.multiple_of(part * rs, rs), rs), :]
                        out[m, e, base:base + rs, :] = v.astype(out.dtype)
                return carry
            lax.fori_loop(0, GROUP // 2, emit, 0)


def block_call(order, spk, live, slot, meta, clips, grads, packed, shares, ff, taps, speakers, small_rows, carried, before):
    nb = len(packed[0]) + 1
    runs = [part[0].shape[1] for part in packed]
    n = sum(runs)
    _, _, length, lanes = packed[0][0].shape
    width = nb * lanes
    first, last = carried is None, before is not None
    per = ff // nb
    rows = (width // GROUP) * (per // lanes) + (per // GROUP) * nb + small_rows // GROUP
    widths = (width, width, ff, ff)
    full = lambda shape: pl.BlockSpec(shape, lambda i, *_: (0,) * len(shape), pipeline_mode=pl.Buffered(1))
    step = lambda *shape: pl.BlockSpec((1,) + shape, lambda i, *_: (i,) + (0,) * len(shape))
    own = pl.BlockSpec((1, length, lanes), lambda i, order, spk, live, slot, meta: (slot[i], 0, 0))
    sums = (nb + 1, small_rows, lanes)
    args = [clips, grads] + [v for part in packed for v in part] + list(shares)
    in_specs = [own, own] + [full(v.shape) for v in args[2:]]
    out_shape = [jax.ShapeDtypeStruct((2, n, length, lanes), BF16)] * nb
    out_specs = [pl.BlockSpec((2, 1, length, lanes), lambda i, *_: (0, i, 0, 0))] * nb
    if not first:
        args.append(carried)
        in_specs.append(full(sums))
    if last:
        args += list(before)
        in_specs += [pl.BlockSpec(memory_space=pl.ANY)] * 4
        out_shape += [jax.ShapeDtypeStruct((GROUP // 2, nb, rows, lanes), BF16)] * 2
        out_specs += [pl.BlockSpec((GROUP // 2, nb, rows, lanes), lambda i, *_: (0, 0, 0, 0))] * 2
    else:
        out_shape += [jax.ShapeDtypeStruct((n, length, w), BF16) for w in widths] + [jax.ShapeDtypeStruct(sums, F32)]
        out_specs += [step(length, w) for w in widths] + [pl.BlockSpec(sums, lambda i, *_: (0, 0, 0))]
    scratch = [
        pltpu.VMEM((nb, length + 2 * PAD, lanes), F32),
        pltpu.VMEM((nb, length + 2 * PAD, lanes), F32),
        pltpu.VMEM((nb, length, lanes), F32),
        pltpu.VMEM((nb, length, lanes), BF16),
        pltpu.VMEM((length, ff), F32),
        pltpu.VMEM((length, width), F32),
        pltpu.VMEM((1, ff), F32),
        pltpu.VMEM((width, ff), BF16),
        pltpu.VMEM((ff, width), BF16),
        pltpu.VMEM((nb, small_rows, lanes), F32),
    ]
    if last:
        scratch = [pltpu.VMEM((n, length, w), BF16) for w in widths] + [pltpu.VMEM(sums, F32)] + scratch
        scratch += [pltpu.VMEM((ff // lanes, width, lanes), F32), pltpu.VMEM((ff, width), F32)]
        scratch += [pltpu.VMEM(v.shape, BF16) for v in before] + [pltpu.SemaphoreType.DMA((4,))]
    return pl.pallas_call(
        functools.partial(body, nb, taps, speakers, runs, first, last),
        out_shape=out_shape,
        grid_spec=pltpu.PrefetchScalarGridSpec(
            num_scalar_prefetch=5, grid=(n,), in_specs=in_specs, out_specs=out_specs, scratch_shapes=scratch),
        cost_estimate=pl.CostEstimate(flops=HINT if last else 0, transcendentals=0, bytes_accessed=0),
        compiler_params=pltpu.CompilerParams(dimension_semantics=("arbitrary",), vmem_limit_bytes=60 << 20),
        name="block",
    )(order, spk, live, slot, meta, *args)


def pack_body(moves, slot_ref, clips, grads, *refs):
    blocks, sems = refs[:-1], refs[-1]
    copies = []
    for j, (at, r, source) in enumerate(moves):
        for q, array in enumerate((clips, grads)):
            copies.append(pltpu.make_async_copy(array.at[slot_ref[source]], blocks[at].at[q, r], sems.at[2 * j + q]))
    for copy in copies:
        copy.start()
    for copy in copies:
        copy.wait()


def pack_call(slots, blocks, clips, grads):
    length, lanes = clips.shape[1:]
    moves, source = [], 0
    for at, run in enumerate(blocks):
        for r in range(run):
            moves.append((at, r, source))
            source += 1
    hbm = pl.BlockSpec(memory_space=pl.ANY)
    sm = pl.BlockSpec(memory_space=pltpu.SMEM)
    vm = pl.BlockSpec(memory_space=pltpu.VMEM)
    return pl.pallas_call(
        functools.partial(pack_body, moves),
        out_shape=[jax.ShapeDtypeStruct((2, run, length, lanes), BF16) for run in blocks],
        in_specs=[sm, hbm, hbm],
        out_specs=[vm] * len(blocks),
        scratch_shapes=[pltpu.SemaphoreType.DMA((2 * len(moves),))],
        name="pack",
    )(slots, clips, grads)


def share_body(taps, speakers, place_ref, w_in, w_out, scale, shift, conv, cb, bo, ls, bi, share, small):
    lanes = share.shape[1]
    small[0:speakers, :] = scale[...].astype(F32)
    small[speakers:2 * speakers, :] = shift[...].astype(F32)
    at = 2 * speakers
    small[at:at + taps, :] = conv[...].astype(F32)
    at += taps
    for v in (cb, bo, ls):
        small[at, :] = v[...].astype(F32)
        at += 1
    tiles = bi.shape[0] // lanes
    for r in range(tiles):
        small[at + r, :] = bi[pl.ds(r * lanes, lanes)].astype(F32)
    at += tiles
    small[at:, :] = jnp.zeros((small.shape[0] - at, lanes), F32)
    ra, rb, rs = w_in.shape[0], w_out.shape[0], small.shape[0] // GROUP
    for r in range(tiles):
        share[r * ra:(r + 1) * ra, :] = w_in[:, r * lanes:(r + 1) * lanes]
    base = tiles * ra
    for r in range(w_out.shape[1] // lanes):
        share[base + r * rb:base + (r + 1) * rb, :] = w_out[:, r * lanes:(r + 1) * lanes]
    base += w_out.shape[1] // lanes * rb
    share[base:base + rs, :] = small[pl.ds(pl.multiple_of(place_ref[0] * rs, rs), rs), :].astype(BF16)


def share_call(place, w_in, w_out, small, small_rows):
    lanes = small[0].shape[1]
    speakers, taps = small[0].shape[0], small[2].shape[0]
    ra, rb = w_in.shape[0] // GROUP, w_out.shape[0] // GROUP
    rows = w_in.shape[1] // lanes * ra + w_out.shape[1] // lanes * rb + small_rows // GROUP
    full = lambda shape: pl.BlockSpec(shape, lambda i, *_: (0,) * len(shape))
    share_row = lambda shape: pl.BlockSpec(shape, lambda i, place: (place[0], 0))
    return pl.pallas_call(
        functools.partial(share_body, taps, speakers),
        out_shape=jax.ShapeDtypeStruct((rows, lanes), BF16),
        grid_spec=pltpu.PrefetchScalarGridSpec(
            num_scalar_prefetch=1, grid=(1,),
            in_specs=[share_row((ra, w_in.shape[1])), share_row((rb, w_out.shape[1]))] + [full(v.shape) for v in small],
            out_specs=full((rows, lanes)),
            scratch_shapes=[pltpu.VMEM((small_rows, lanes), F32)]),
        compiler_params=pltpu.CompilerParams(dimension_semantics=("arbitrary",)),
        name="share",
    )(place, w_in, w_out, *small)


def stack_body(*refs):
    for d, v in enumerate(refs[:-1]):
        refs[-1][d] = v[...]


def stack_call(parts):
    return pl.pallas_call(
        stack_body,
        out_shape=jax.ShapeDtypeStruct((len(parts),) + parts[0].shape, BF16),
        name="gathered",
    )(*parts)


def finish_body(nb, ra, rb, rs, tiles, lanes, taps, speakers, meta_ref, *refs):
    ins = [refs[s % 2].at[s // 2] for s in range(GROUP)]
    g_in, g_out, scale, shift, conv, cb, bo, ls, bi, small = refs[2:]
    for s in range(GROUP):
        part = meta_ref[1] ^ s
        for r in range(tiles):
            g_in[pl.ds(pl.multiple_of(part * ra, ra), ra), r * lanes:(r + 1) * lanes] = ins[s][r * ra:(r + 1) * ra, :].astype(F32)
        base = tiles * ra
        for r in range(nb):
            g_out[pl.ds(pl.multiple_of(part * rb, 16), rb), r * lanes:(r + 1) * lanes] = ins[s][base + r * rb:base + (r + 1) * rb, :].astype(F32)
        base += nb * rb
        small[pl.ds(pl.multiple_of(part * rs, rs), rs), :] = ins[s][base:base + rs, :].astype(F32)
    scale[...] = small[0:speakers, :]
    shift[...] = small[speakers:2 * speakers, :]
    at = 2 * speakers
    conv[...] = small[at:at + taps, :]
    at += taps
    cb[...] = small[at:at + 1, :]
    bo[...] = small[at + 1:at + 2, :]
    ls[...] = small[at + 2:at + 3, :]
    for r in range(tiles):
        bi[pl.ds(r * lanes, lanes)] = small[at + 3 + r, :]


def finish_call(meta, parts, nb, ra, rb, rs, tiles, taps, speakers):
    lanes = parts[0].shape[2]
    vm = pl.BlockSpec(memory_space=pltpu.VMEM)
    sm = pl.BlockSpec(memory_space=pltpu.SMEM)
    shapes = [(nb * lanes, tiles * lanes), (tiles * lanes, nb * lanes), (speakers, lanes), (speakers, lanes), (taps, lanes),
              (1, lanes), (1, lanes), (1, lanes), (tiles * lanes,)]
    return pl.pallas_call(
        functools.partial(finish_body, nb, ra, rb, rs, tiles, lanes, taps, speakers),
        in_specs=[sm] + [vm] * 2,
        out_specs=[vm] * len(shapes),
        out_shape=[jax.ShapeDtypeStruct(s, F32) for s in shapes],
        scratch_shapes=[pltpu.VMEM((rs * GROUP, lanes), F32)],
        name="finish",
    )(meta, *parts)


def ring(axis, size, shift):
    return lambda v: lax.ppermute(v, axis, [(i, (i + shift) % size) for i in range(size)])


def flip(axis, size, mask):
    return lambda v: lax.ppermute(v, axis, [(i, i ^ mask) for i in range(size)])


def gather_group(v, dp_count, gates):
    core = flip("dp", dp_count, 1)
    a, b = flip("dp", dp_count, 2)(v), flip("dp", dp_count, 4)(v)
    a, *one = lax.optimization_barrier((a, *gates[0]))
    c = flip("dp", dp_count, 4)(a)
    c, *two = lax.optimization_barrier((c, *gates[1]))
    return [v, core(v), a, core(a), b, core(b), c, core(c)], (one, two)


def gather_small(v, dp_count):
    near = jnp.stack([v] + [flip("dp", dp_count, 2 * m)(v) for m in range(1, GROUP // 2)])
    return [near, flip("dp", dp_count, 1)(near)]


def per_device(clips_in, speaker, counts, conv_weight, conv_bias, scale_table, shift_table,
               w_in, b_in, w_out, b_out, layer_scale, grad_out):
    clip_num, length, lanes = clips_in.shape
    nb = lax.axis_size("chan")
    dp_count = lax.axis_size("dp")
    me = lax.axis_index("chan")
    dp = lax.axis_index("dp")
    speakers = scale_table.shape[0]
    taps = conv_weight.shape[0]
    per = w_in.shape[1]
    tiles = per // lanes
    width = nb * lanes
    order = (me - jnp.arange(nb, dtype=jnp.int32)) % nb
    place = dp % GROUP
    sizes = [sum(r) for r in RUNS]
    starts = [nb * sum(sizes[:k]) for k in range(len(sizes))]
    assert clip_num == nb * sum(sizes)
    ra, rb = width // GROUP, per // GROUP
    small = [scale_table, shift_table, conv_weight, conv_bias, b_out, layer_scale, b_in]
    used = 2 * speakers + taps + 3 + tiles
    small_rows = -(-used // (GROUP * 16)) * GROUP * 16
    slots, blocks = [], []
    for start, n, runs in zip(starts, sizes, RUNS):
        low = 0
        for run in runs:
            for d in range(1, nb):
                blocks.append(run)
                slots.append(start + (me + d) % nb * n + low + jnp.arange(run))
            low += run
    share = share_call(place.astype(jnp.int32)[None], w_in, w_out, small, small_rows)
    packed = pack_call(jnp.concatenate(slots).astype(jnp.int32), blocks, clips_in, grad_out)

    shares = [share] + [ring("chan", nb, d)(share) for d in range(1, nb)]
    stacked = stack_call(shares)
    stacked, *packed = lax.optimization_barrier((stacked, *packed))
    came = [ring("chan", nb, 1 + j % (nb - 1))(v) for j, v in enumerate(packed)]
    packed = []
    for runs in RUNS:
        packed.append([])
        for _ in runs:
            packed[-1].append(came[:nb - 1])
            came = came[nb - 1:]
    meta = jnp.stack([me, place]).astype(jnp.int32)
    gathered, packed[0] = gather_group(stacked, dp_count, packed[0])

    sums, kept, back = None, None, []
    for k, (start, n) in enumerate(zip(starts, sizes)):
        base = start + me * n
        slot = (base + jnp.arange(n)).astype(jnp.int32)
        spk = lax.dynamic_slice_in_dim(speaker, base, n)
        live = (slot < counts[0]).astype(jnp.int32)
        out = block_call(order, spk, live, slot, meta, clips_in, grad_out, packed[k], gathered, nb * per,
                         taps, speakers, small_rows, sums, kept)
        if k:
            keep, send = out[nb:]
        else:
            kept, sums = out[nb:nb + 4], out[nb + 4]
        sent = out[:nb]
        if k:
            sent, back[0] = lax.optimization_barrier((sent, back[0]))
        else:
            sent, packed[1] = lax.optimization_barrier((sent, packed[1]))
        back.append([sent[0]] + [ring("chan", nb, -d)(sent[d]) for d in range(1, nb)])

    send, *back[0] = lax.optimization_barrier((send, *back[0]))
    got = flip("dp", dp_count, 1)(send)
    total = keep[0].astype(F32) + got[0].astype(F32)
    outward = [(keep[m].astype(F32) + got[m].astype(F32)).astype(BF16) for m in range(1, GROUP // 2)]
    outward, back[0] = lax.optimization_barrier((outward, back[0]))
    for m in range(1, GROUP // 2):
        total = total + flip("dp", dp_count, 2 * m)(outward[m - 1]).astype(F32)
    step = GROUP
    while step < dp_count:
        low = total.astype(BF16)
        total = low.astype(F32) + flip("dp", dp_count, step)(low).astype(F32)
        step *= 2
    total, back[-1] = lax.optimization_barrier((total, back[-1]))
    mine = total[0]
    for d in range(1, nb):
        mine = mine + ring("chan", nb, d)(total[d].astype(BF16)).astype(F32)
    clips_out = jnp.zeros(clips_in.shape, BF16)
    grad_clips = grad_out.astype(F32)
    for k, n in enumerate(sizes):
        for d in range(nb):
            at = starts[k] + (me + d) % nb * n
            clips_out = lax.dynamic_update_slice_in_dim(clips_out, back[k][d][0], at, 0)
            g = lax.dynamic_slice_in_dim(grad_out, at, n).astype(F32) + back[k][d][1].astype(F32)
            grad_clips = lax.dynamic_update_slice_in_dim(grad_clips, g, at, 0)
    mine, clips_out, grad_clips = lax.optimization_barrier((mine, clips_out, grad_clips))

    g_in, g_out, g_scale, g_shift, g_conv, g_cb, g_bo, g_ls, g_bi = finish_call(
        meta, gather_small(mine.astype(BF16), dp_count), nb, ra, rb, small_rows // GROUP, tiles, taps, speakers)

    return (clips_out, grad_clips, g_conv, g_cb.reshape(lanes), g_scale, g_shift, g_in, g_bi, g_out,
            g_bo.reshape(lanes), g_ls.reshape(lanes))


def solution(mesh):
    act = P("dp", None, "chan")
    col, vec, row = P(None, "chan"), P("chan"), P("chan", None)
    in_specs = (act, P("dp"), P("dp"), col, vec, col, col, col, vec, row, vec, vec, act)
    out_specs = (act, act, col, vec, col, col, col, vec, row, vec, vec)
    return jax.shard_map(per_device, mesh=mesh, in_specs=in_specs, out_specs=out_specs, check_vma=False)
```

time: 161 us -> 157 us (0.975)
  other arithmetic: 22.5 us -> 9.45 us
  waiting for transfers between devices: 36.2 us -> 48.3 us
  Pallas kernels: 36.6 us -> 44.5 us
  local copies, waits for them, and re-layouts: 15.4 us -> 8 us
  starting transfers between devices: 47.9 us -> 43.8 us
    ppermute x21, waiting for transfers between devices: 11 us -> 27.8 us  [ring(): lax.ppermute(v, axis, [(i, (i + shift) % size) for i in range(size)])]
    another operation x10 -> x1, other arithmetic: 10.9 us -> 0.06 us  [the longest x9 10.8 us: per_device(): jnp.stack([lax.dynamic_slice_in_dim(clips_in, at, run), lax.dynamic_slice...]
    pallas_call x4 -> x5, Pallas kernels: 34.2 us -> 42.2 us  [the longest x2 35.4 us: block_call(): pl.pallas_call(functools.partial(body, nb, taps, speakers, runs, first, l...]
    ppermute x21, starting transfers between devices: 36.5 us -> 31.4 us  [ring(): lax.ppermute(v, axis, [(i, (i + shift) % size) for i in range(size)])]
    ppermute x15, waiting for transfers between devices: 25.2 us -> 20.5 us  [flip(): return lambda v: lax.ppermute(v, axis, [(i, i ^ mask) for i in range(size)])]
    unnamed x66 -> x50, local copies, waits for them, and re-layouts: 8.3 us -> 3.63 us
    dynamic_update_slice x8, other arithmetic: 5.97 us -> 2.98 us  [per_device(): grad_clips = lax.dynamic_update_slice_in_dim(grad_clips, g, at, 0)]
    another operation x2 -> x0, local copies, waits for them, and re-layouts: 2.82 us -> none  [per_device(): jnp.stack([lax.dynamic_slice_in_dim(clips_in, at, run), lax.dynamic_slice...]
  transfers between devices with their start and end apart: 36 -> 36, of which waited for: 11 -> 16; matrix products, arithmetic and copies ran while one was open for 16% -> 9% of each run, Pallas kernels for 21% -> 25%
where the time goes in v4:
time: 157 us; the launch traced here: 156 us
  waiting for transfers between devices  48.3 us (31%)
  Pallas kernels  44.5 us (28%)
  starting transfers between devices  43.8 us (28%)
  other arithmetic  9.45 us (6%)
  local copies, waits for them, and re-layouts  8 us (5%)
  between operations  1.99 us (1%)
    pallas_call x2, Pallas kernels, block_call(): pl.pallas_call(functools.partial(body, nb, taps, speakers, runs, first, l...  35.4 us
    ppermute x21, starting transfers between devices, ring(): lax.ppermute(v, axis, [(i, (i + shift) % size) for i in range(size)])  31.4 us
    ppermute x21, waiting for transfers between devices, ring(): lax.ppermute(v, axis, [(i, (i + shift) % size) for i in range(size)])  27.8 us
    ppermute x15, waiting for transfers between devices, flip(): return lambda v: lax.ppermute(v, axis, [(i, i ^ mask) for i in range(size)])  20.5 us
    ppermute x15, starting transfers between devices, flip(): return lambda v: lax.ppermute(v, axis, [(i, i ^ mask) for i in range(size)])  12.3 us
    unnamed x50, local copies, waits for them, and re-layouts  3.63 us
    pallas_call x1, Pallas kernels, pack_call(): pl.pallas_call(functools.partial(pack_body, moves), out_shape=[jax.ShapeD...  3.4 us
  transfers between devices with their start and end apart: 36, of which 16 were waited for; matrix products, arithmetic and copies ran while one was open for 9% of the time, Pallas kernels for 25%

profile of v4, /device:TPU:0, one launch (start us, length us, event | category | flops | bytes accessed | tf_op | source)
XLA Modules:
  0.0 156.0 jit_solution(5761000334955530190)
XLA Ops:
  2.2 3.1 %collective-permute-start = (bf16[416,128]{1,0:T(8,128)(2,1)}, bf16[416,128]{1,0:T(8,128)(2,1)S(1)}, u32[]{:S(2)}, u32[]{:S(2)}) collective-permute-start(bf16[416,128]{1,0:T(8,128)(2,1)} %share.1.refs_0_), channel_id=1, source_target_pairs={{0,1},{1,2},{2,3},{3,0},{4,5},{5,6},{6,7},{7,4},{8,9},{9,10},{10,1... | collective-permute-start | bytes 319496 | tf_op jit(solution)/shard_map/ppermute | solution.py:417
  5.3 2.6 %collective-permute-start.1 = (bf16[416,128]{1,0:T(8,128)(2,1)}, bf16[416,128]{1,0:T(8,128)(2,1)S(1)}, u32[]{:S(2)}, u32[]{:S(2)}) collective-permute-start(bf16[416,128]{1,0:T(8,128)(2,1)} %share.1.refs_0_), channel_id=1, source_target_pairs={{0,2},{1,3},{2,0},{3,1},{4,6},{5,7},{6,4},{7,5},{8,10},{9,11},{10,... | collective-permute-start | bytes 319496 | tf_op jit(solution)/shard_map/ppermute | solution.py:417
  9.8 3.4 %pack.1 = (bf16[2,1,256,128]{3,2,1,0:T(8,128)(2,1)}, bf16[2,1,256,128]{3,2,1,0:T(8,128)(2,1)}, bf16[2,1,256,128]{3,2,1,0:T(8,128)(2,1)}, bf16[2,1,256,128]{3,2,1...) custom-call(s32[12]{0:T(128)} %concatenate.3.slot_ref, ...), custom_call_target="tpu_custom_call" | custom-call | tf_op jit(solution)/shard_map/pack/pallas_call | solution.py:308
  19.8 2.1 %collective-permute-start.4 = (bf16[2,1,256,128]{3,2,1,0:T(8,128)(2,1)}, bf16[2,1,256,128]{3,2,1,0:T(8,128)(2,1)S(1)}, u32[]{:S(2)}, u32[]{:S(2)}) collective-permute-start(bf16[2,1,256,128]{3,2,1,0:T(8,128)(2,1)} %get-tuple-element.107), channel_id=1, source_target_pairs={{0,1},{1,2},{2,3},{3,0},{4,5},{5,6},{6,7},{7,4},{8,9},{9,10},{10,1... | collective-permute-start | bytes 393224 | tf_op jit(solution)/shard_map/ppermute | solution.py:417
  21.9 2.2 %collective-permute-start.5 = (bf16[2,1,256,128]{3,2,1,0:T(8,128)(2,1)}, bf16[2,1,256,128]{3,2,1,0:T(8,128)(2,1)S(1)}, u32[]{:S(2)}, u32[]{:S(2)}) collective-permute-start(bf16[2,1,256,128]{3,2,1,0:T(8,128)(2,1)} %get-tuple-element.108), channel_id=1, source_target_pairs={{0,2},{1,3},{2,0},{3,1},{4,6},{5,7},{6,4},{7,5},{8,10},{9,11},{10,... | collective-permute-start | bytes 393224 | tf_op jit(solution)/shard_map/ppermute | solution.py:417
  29.8 2.8 %collective-permute-done.5.refs_3_ = bf16[2,1,256,128]{3,2,1,0:T(8,128)(2,1)S(1)} collective-permute-done((bf16[2,1,256,128]{3,2,1,0:T(8,128)(2,1)}, bf16[2,1,256,128]{3,2,1,0:T(8,128)(2,1)S(1)}, u32[]{:S(2)}, u32[]{:S(2)}) %collective-permute-start.5) | collective-permute-done | bytes 131104 | tf_op jit(solution)/shard_map/ppermute | solution.py:417
  35.2 2.8 %collective-permute-start.8 = (bf16[2,1,256,128]{3,2,1,0:T(8,128)(2,1)}, bf16[2,1,256,128]{3,2,1,0:T(8,128)(2,1)S(1)}, u32[]{:S(2)}, u32[]{:S(2)}) collective-permute-start(bf16[2,1,256,128]{3,2,1,0:T(8,128)(2,1)} %get-tuple-element.114), channel_id=1, source_target_pairs={{0,1},{1,2},{2,3},{3,0},{4,5},{5,6},{6,7},{7,4},{8,9},{9,10},{10,1... | collective-permute-start | bytes 393224 | tf_op jit(solution)/shard_map/ppermute | solution.py:417
  38.5 5.3 %collective-permute-done.8.refs_5_ = bf16[2,1,256,128]{3,2,1,0:T(8,128)(2,1)S(1)} collective-permute-done((bf16[2,1,256,128]{3,2,1,0:T(8,128)(2,1)}, bf16[2,1,256,128]{3,2,1,0:T(8,128)(2,1)S(1)}, u32[]{:S(2)}, u32[]{:S(2)}) %collective-permute-start.8) | collective-permute-done | bytes 131104 | tf_op jit(solution)/shard_map/ppermute | solution.py:417
  45.2 5.2 %collective-permute-done.9.refs_6_ = bf16[2,1,256,128]{3,2,1,0:T(8,128)(2,1)S(1)} collective-permute-done((bf16[2,1,256,128]{3,2,1,0:T(8,128)(2,1)}, bf16[2,1,256,128]{3,2,1,0:T(8,128)(2,1)S(1)}, u32[]{:S(2)}, u32[]{:S(2)}) %collective-permute-start.9) | collective-permute-done | bytes 131104 | tf_op jit(solution)/shard_map/ppermute | solution.py:417
  51.8 2.6 %collective-permute-start.17 = (bf16[2,2,256,128]{3,2,1,0:T(8,128)(2,1)}, bf16[2,2,256,128]{3,2,1,0:T(8,128)(2,1)}, u32[]{:S(2)}, u32[]{:S(2)}) collective-permute-start(bf16[2,2,256,128]{3,2,1,0:T(8,128)(2,1)} %get-tuple-element.126), channel_id=1, source_target_pairs={{0,2},{1,3},{2,0},{3,1},{4,6},{5,7},{6,4},{7,5},{8,10},{9,11},{10,... | collective-permute-start | bytes 786440 | tf_op jit(solution)/shard_map/ppermute | solution.py:417
  58.9 15.5 %block.2 = (bf16[2,2,256,128]{3,2,1,0:T(8,128)(2,1)}, bf16[2,2,256,128]{3,2,1,0:T(8,128)(2,1)}, bf16[2,2,256,128]{3,2,1,0:T(8,128)(2,1)}, bf16[2,2,256,128]{3,2,...) custom-call(s32[4]{0:T(128)} %and_select_fusion.order_ref, ...), custom_call_target="tpu_custom_call" | custom-call | tf_op jit(solution)/shard_map/block/pallas_call | solution.py:275
  74.4 3.8 %collective-permute-start.19 = (bf16[2,2,256,128]{3,2,1,0:T(8,128)(2,1)}, bf16[2,2,256,128]{3,2,1,0:T(8,128)(2,1)}, u32[]{:S(2)}, u32[]{:S(2)}) collective-permute-start(bf16[2,2,256,128]{3,2,1,0:T(8,128)(2,1)} %get-tuple-element.143), channel_id=1, source_target_pairs={{0,3},{1,0},{2,1},{3,2},{4,7},{5,4},{6,5},{7,6},{8,11},{9,8},{10,9... | collective-permute-start | bytes 786440 | tf_op jit(solution)/shard_map/ppermute | solution.py:417
  78.3 2.3 %collective-permute-start.20 = (bf16[2,2,256,128]{3,2,1,0:T(8,128)(2,1)}, bf16[2,2,256,128]{3,2,1,0:T(8,128)(2,1)}, u32[]{:S(2)}, u32[]{:S(2)}) collective-permute-start(bf16[2,2,256,128]{3,2,1,0:T(8,128)(2,1)} %get-tuple-element.144), channel_id=1, source_target_pairs={{0,2},{1,3},{2,0},{3,1},{4,6},{5,7},{6,4},{7,5},{8,10},{9,11},{10,... | collective-permute-start | bytes 786440 | tf_op jit(solution)/shard_map/ppermute | solution.py:417
  80.6 19.9 %block.3 = (bf16[2,2,256,128]{3,2,1,0:T(8,128)(2,1)}, bf16[2,2,256,128]{3,2,1,0:T(8,128)(2,1)}, bf16[2,2,256,128]{3,2,1,0:T(8,128)(2,1)}, bf16[2,2,256,128]{3,2,...) custom-call(s32[4]{0:T(128)} %and_select_fusion.order_ref, ...), custom_call_target="tpu_custom_call" | custom-call | flops 68719476736 | tf_op jit(solution)/shard_map/block/pallas_call | solution.py:275
  100.5 3.0 %collective-permute-done.20 = bf16[2,2,256,128]{3,2,1,0:T(8,128)(2,1)} collective-permute-done((bf16[2,2,256,128]{3,2,1,0:T(8,128)(2,1)}, bf16[2,2,256,128]{3,2,1,0:T(8,128)(2,1)}, u32[]{:S(2)}, u32[]{:S(2)}) %collective-permute-start.20) | collective-permute-done | bytes 262176 | tf_op jit(solution)/shard_map/ppermute | solution.py:417
  104.8 2.7 %collective-permute-done.22 = bf16[4,4,416,128]{3,2,1,0:T(8,128)(2,1)} collective-permute-done((bf16[4,4,416,128]{3,2,1,0:T(8,128)(2,1)}, bf16[4,4,416,128]{3,2,1,0:T(8,128)(2,1)}, u32[]{:S(2)}, u32[]{:S(2)}) %collective-permute-start.22) | collective-permute-done | bytes 1703968 | tf_op jit(solution)/shard_map/ppermute | solution.py:421
  107.5 2.0 %fusion.4 = (bf16[4,416,128]{2,1,0:T(8,128)(2,1)S(1)}, bf16[4,416,128]{2,1,0:T(8,128)(2,1)S(1)}, bf16[4,416,128]{2,1,0:T(8,128)(2,1)S(1)}) fusion(bf16[4,4,416,128]{3,2,1,0:T(8,128)(2,1)} %collective-permute-done.22, bf16[4,4,416,128]{3,2,1,0:T(8,128)(2,1)} %get-tuple-element.136), kind=kLoop, calls=%fused_computation.8 | loop fusion | flops 2555904 | bytes 3833856 | tf_op jit(solution)/shard_map/convert_element_type | solution.py:505
  110.6 2.4 %collective-permute-start.25 = (bf16[4,416,128]{2,1,0:T(8,128)(2,1)S(1)}, bf16[4,416,128]{2,1,0:T(8,128)(2,1)S(1)}, u32[]{:S(2)}, u32[]{:S(2)}) collective-permute-start(bf16[4,416,128]{2,1,0:T(8,128)(2,1)S(1)} %get-tuple-element.157), channel_id=1, source_target_pairs={{0,24},{4,28},{8,16},{12,20},{16,8},{20,12},{24,0},{28,4},{1,25},{... | collective-permute-start | bytes 1277960 | tf_op jit(solution)/shard_map/ppermute | solution.py:421
  119.0 3.3 %collective-permute-done.23 = bf16[4,416,128]{2,1,0:T(8,128)(2,1)S(1)} collective-permute-done((bf16[4,416,128]{2,1,0:T(8,128)(2,1)S(1)}, bf16[4,416,128]{2,1,0:T(8,128)(2,1)S(1)}, u32[]{:S(2)}, u32[]{:S(2)}) %collective-permute-start.23) | collective-permute-done | bytes 426016 | tf_op jit(solution)/shard_map/ppermute | solution.py:421
  122.3 8.5 %collective-permute-done.24 = bf16[4,416,128]{2,1,0:T(8,128)(2,1)S(1)} collective-permute-done((bf16[4,416,128]{2,1,0:T(8,128)(2,1)S(1)}, bf16[4,416,128]{2,1,0:T(8,128)(2,1)S(1)}, u32[]{:S(2)}, u32[]{:S(2)}) %collective-permute-start.24) | collective-permute-done | bytes 426016 | tf_op jit(solution)/shard_map/ppermute | solution.py:421
  134.0 2.4 %collective-permute-start.31 = (bf16[416,128]{1,0:T(8,128)(2,1)S(1)}, bf16[416,128]{1,0:T(8,128)(2,1)S(1)}, u32[]{:S(2)}, u32[]{:S(2)}) collective-permute-start(bf16[416,128]{1,0:T(8,128)(2,1)S(1)} %get-tuple-element.187), channel_id=1, source_target_pairs={{0,3},{1,0},{2,1},{3,2},{4,7},{5,4},{6,5},{7,6},{8,11},{9,8},{10,9... | collective-permute-start | bytes 319496 | tf_op jit(solution)/shard_map/ppermute | solution.py:417
  136.6 3.7 %collective-permute-done.29 = bf16[416,128]{1,0:T(8,128)(2,1)S(1)} collective-permute-done((bf16[416,128]{1,0:T(8,128)(2,1)S(1)}, bf16[416,128]{1,0:T(8,128)(2,1)S(1)}, u32[]{:S(2)}, u32[]{:S(2)}) %collective-permute-start.29) | collective-permute-done | bytes 106528 | tf_op jit(solution)/shard_map/ppermute | solution.py:417
  140.3 2.7 %collective-permute-done.30 = bf16[416,128]{1,0:T(8,128)(2,1)S(1)} collective-permute-done((bf16[416,128]{1,0:T(8,128)(2,1)S(1)}, bf16[416,128]{1,0:T(8,128)(2,1)S(1)}, u32[]{:S(2)}, u32[]{:S(2)}) %collective-permute-start.30) | collective-permute-done | bytes 106528 | tf_op jit(solution)/shard_map/ppermute | solution.py:417
  153.5 2.4 %finish.1 = (f32[512,384]{1,0:T(8,128)}, f32[384,512]{1,0:T(8,128)}, f32[64,128]{1,0:T(8,128)}, f32[64,128]{1,0:T(8,128)}, f32[7,128]{1,0:T(8,128)}, /*index=5*/...) custom-call(s32[2]{0:T(128)} %pad_add_fusion.meta_ref, bf16[4,416,128]{2,1,0:T(8,128)(2,1)} %copy-done.2, ...), custom_call_target="tpu_custom_call" | custom-call | tf_op jit(solution)/shard_map/finish/pallas_call | solution.py:406
  (137 shorter events, 47.1 us)
Async XLA Ops:
  2.2 11.0 %collective-permute-start = (bf16[416,128]{1,0:T(8,128)(2,1)}, bf16[416,128]{1,0:T(8,128)(2,1)S(1)}, u32[]{:S(2)}, u32[]{:S(2)}) collective-permute-start(bf16[416,128]{1,0:T(8,128)(2,1)} %share.1.refs_0_), channel_id=1, source_target_pairs={{0,1},{1,2},{2,3},{3,0},{4,5},{5,6},{6,7},{7,4},{8,9},{9,10},{10,1... | collective-permute-start | bytes 319496 | tf_op jit(solution)/shard_map/ppermute | solution.py:417
  5.3 9.9 %collective-permute-start.1 = (bf16[416,128]{1,0:T(8,128)(2,1)}, bf16[416,128]{1,0:T(8,128)(2,1)S(1)}, u32[]{:S(2)}, u32[]{:S(2)}) collective-permute-start(bf16[416,128]{1,0:T(8,128)(2,1)} %share.1.refs_0_), channel_id=1, source_target_pairs={{0,2},{1,3},{2,0},{3,1},{4,6},{5,7},{6,4},{7,5},{8,10},{9,11},{10,... | collective-permute-start | bytes 319496 | tf_op jit(solution)/shard_map/ppermute | solution.py:417
  18.3 15.3 %collective-permute-start.3 = (bf16[4,416,128]{2,1,0:T(8,128)(2,1)}, bf16[4,416,128]{2,1,0:T(8,128)(2,1)S(1)}, u32[]{:S(2)}, u32[]{:S(2)}) collective-permute-start(bf16[4,416,128]{2,1,0:T(8,128)(2,1)} %gathered.1.refs_8_.refs_5_), channel_id=1, source_target_pairs={{0,8},{4,12},{8,0},{12,4},{16,24},{20,28},{24,16},{28,20},{1,9},{5... | collective-permute-start | bytes 1277960 | tf_op jit(solution)/shard_map/ppermute | solution.py:421
  21.9 10.7 %collective-permute-start.5 = (bf16[2,1,256,128]{3,2,1,0:T(8,128)(2,1)}, bf16[2,1,256,128]{3,2,1,0:T(8,128)(2,1)S(1)}, u32[]{:S(2)}, u32[]{:S(2)}) collective-permute-start(bf16[2,1,256,128]{3,2,1,0:T(8,128)(2,1)} %get-tuple-element.108), channel_id=1, source_target_pairs={{0,2},{1,3},{2,0},{3,1},{4,6},{5,7},{6,4},{7,5},{8,10},{9,11},{10,... | collective-permute-start | bytes 393224 | tf_op jit(solution)/shard_map/ppermute | solution.py:417
  24.1 9.5 %collective-permute-start.6 = (bf16[2,1,256,128]{3,2,1,0:T(8,128)(2,1)}, bf16[2,1,256,128]{3,2,1,0:T(8,128)(2,1)S(1)}, u32[]{:S(2)}, u32[]{:S(2)}) collective-permute-start(bf16[2,1,256,128]{3,2,1,0:T(8,128)(2,1)} %get-tuple-element.109), channel_id=1, source_target_pairs={{0,3},{1,0},{2,1},{3,2},{4,7},{5,4},{6,5},{7,6},{8,11},{9,8},{10,9... | collective-permute-start | bytes 393224 | tf_op jit(solution)/shard_map/ppermute | solution.py:417
  24.5 13.5 %collective-permute-start.10 = (bf16[2,1,256,128]{3,2,1,0:T(8,128)(2,1)}, bf16[2,1,256,128]{3,2,1,0:T(8,128)(2,1)S(1)}, u32[]{:S(2)}, u32[]{:S(2)}) collective-permute-start(bf16[2,1,256,128]{3,2,1,0:T(8,128)(2,1)} %get-tuple-element.116), channel_id=1, source_target_pairs={{0,3},{1,0},{2,1},{3,2},{4,7},{5,4},{6,5},{7,6},{8,11},{9,8},{10,9... | collective-permute-start | bytes 393224 | tf_op jit(solution)/shard_map/ppermute | solution.py:417
  28.3 16.9 %collective-permute-start.13 = (bf16[4,416,128]{2,1,0:T(8,128)(2,1)}, bf16[4,416,128]{2,1,0:T(8,128)(2,1)S(1)}, u32[]{:S(2)}, u32[]{:S(2)}) collective-permute-start(bf16[4,416,128]{2,1,0:T(8,128)(2,1)} %gathered.1.refs_8_.refs_5_), channel_id=1, source_target_pairs={{0,16},{4,20},{8,24},{12,28},{16,0},{20,4},{24,8},{28,12},{1,17},{... | collective-permute-start | bytes 1277960 | tf_op jit(solution)/shard_map/ppermute | solution.py:421
  33.6 17.5 %collective-permute-start.7 = (bf16[4,416,128]{2,1,0:T(8,128)(2,1)S(1)}, bf16[4,416,128]{2,1,0:T(8,128)(2,1)S(1)}, u32[]{:S(2)}, u32[]{:S(2)}) collective-permute-start(bf16[4,416,128]{2,1,0:T(8,128)(2,1)S(1)} %collective-permute-done.3.refs_10_.refs_7_), channel_id=1, source_target_pairs={{0,16},{4,20},{8,24},{12,28},{16,0},{20,4},{24,8},{28,12},{1,17},{... | collective-permute-start | bytes 1277960 | tf_op jit(solution)/shard_map/ppermute | solution.py:421
  38.0 13.8 %collective-permute-start.11 = (bf16[4,416,128]{2,1,0:T(8,128)(2,1)}, bf16[4,416,128]{2,1,0:T(8,128)(2,1)S(1)}, u32[]{:S(2)}, u32[]{:S(2)}) collective-permute-start(bf16[4,416,128]{2,1,0:T(8,128)(2,1)} %gathered.1.refs_8_.refs_5_), channel_id=1, source_target_pairs={{0,4},{4,0},{8,12},{12,8},{16,20},{20,16},{24,28},{28,24},{1,5},{5... | collective-permute-start | bytes 1277960 | tf_op jit(solution)/shard_map/ppermute | solution.py:421
  38.0 16.4 %collective-permute-start.12 = (bf16[4,416,128]{2,1,0:T(8,128)(2,1)S(1)}, bf16[4,416,128]{2,1,0:T(8,128)(2,1)S(1)}, u32[]{:S(2)}, u32[]{:S(2)}) collective-permute-start(bf16[4,416,128]{2,1,0:T(8,128)(2,1)S(1)} %collective-permute-done.3.refs_10_.refs_7_), channel_id=1, source_target_pairs={{0,4},{4,0},{8,12},{12,8},{16,20},{20,16},{24,28},{28,24},{1,5},{5... | collective-permute-start | bytes 1277960 | tf_op jit(solution)/shard_map/ppermute | solution.py:421
  45.2 12.8 %collective-permute-start.14 = (bf16[4,416,128]{2,1,0:T(8,128)(2,1)S(1)}, bf16[4,416,128]{2,1,0:T(8,128)(2,1)S(1)}, u32[]{:S(2)}, u32[]{:S(2)}) collective-permute-start(bf16[4,416,128]{2,1,0:T(8,128)(2,1)S(1)} %collective-permute-done.13.refs_12_.refs_9_), channel_id=1, source_target_pairs={{0,4},{4,0},{8,12},{12,8},{16,20},{20,16},{24,28},{28,24},{1,5},{5... | collective-permute-start | bytes 1277960 | tf_op jit(solution)/shard_map/ppermute | solution.py:421
  51.7 22.7 %collective-permute-start.16 = (bf16[2,2,256,128]{3,2,1,0:T(8,128)(2,1)}, bf16[2,2,256,128]{3,2,1,0:T(8,128)(2,1)}, u32[]{:S(2)}, u32[]{:S(2)}) collective-permute-start(bf16[2,2,256,128]{3,2,1,0:T(8,128)(2,1)} %get-tuple-element.125), channel_id=1, source_target_pairs={{0,1},{1,2},{2,3},{3,0},{4,5},{5,6},{6,7},{7,4},{8,9},{9,10},{10,1... | collective-permute-start | bytes 786440 | tf_op jit(solution)/shard_map/ppermute | solution.py:417
  51.8 22.7 %collective-permute-start.17 = (bf16[2,2,256,128]{3,2,1,0:T(8,128)(2,1)}, bf16[2,2,256,128]{3,2,1,0:T(8,128)(2,1)}, u32[]{:S(2)}, u32[]{:S(2)}) collective-permute-start(bf16[2,2,256,128]{3,2,1,0:T(8,128)(2,1)} %get-tuple-element.126), channel_id=1, source_target_pairs={{0,2},{1,3},{2,0},{3,1},{4,6},{5,7},{6,4},{7,5},{8,10},{9,11},{10,... | collective-permute-start | bytes 786440 | tf_op jit(solution)/shard_map/ppermute | solution.py:417
  54.4 20.1 %collective-permute-start.18 = (bf16[2,2,256,128]{3,2,1,0:T(8,128)(2,1)}, bf16[2,2,256,128]{3,2,1,0:T(8,128)(2,1)}, u32[]{:S(2)}, u32[]{:S(2)}) collective-permute-start(bf16[2,2,256,128]{3,2,1,0:T(8,128)(2,1)} %get-tuple-element.127), channel_id=1, source_target_pairs={{0,3},{1,0},{2,1},{3,2},{4,7},{5,4},{6,5},{7,6},{8,11},{9,8},{10,9... | collective-permute-start | bytes 786440 | tf_op jit(solution)/shard_map/ppermute | solution.py:417
  74.4 26.1 %collective-permute-start.19 = (bf16[2,2,256,128]{3,2,1,0:T(8,128)(2,1)}, bf16[2,2,256,128]{3,2,1,0:T(8,128)(2,1)}, u32[]{:S(2)}, u32[]{:S(2)}) collective-permute-start(bf16[2,2,256,128]{3,2,1,0:T(8,128)(2,1)} %get-tuple-element.143), channel_id=1, source_target_pairs={{0,3},{1,0},{2,1},{3,2},{4,7},{5,4},{6,5},{7,6},{8,11},{9,8},{10,9... | collective-permute-start | bytes 786440 | tf_op jit(solution)/shard_map/ppermute | solution.py:417
  78.3 25.3 %collective-permute-start.20 = (bf16[2,2,256,128]{3,2,1,0:T(8,128)(2,1)}, bf16[2,2,256,128]{3,2,1,0:T(8,128)(2,1)}, u32[]{:S(2)}, u32[]{:S(2)}) collective-permute-start(bf16[2,2,256,128]{3,2,1,0:T(8,128)(2,1)} %get-tuple-element.144), channel_id=1, source_target_pairs={{0,2},{1,3},{2,0},{3,1},{4,6},{5,7},{6,4},{7,5},{8,10},{9,11},{10,... | collective-permute-start | bytes 786440 | tf_op jit(solution)/shard_map/ppermute | solution.py:417
  80.6 23.0 %collective-permute-start.21 = (bf16[2,2,256,128]{3,2,1,0:T(8,128)(2,1)}, bf16[2,2,256,128]{3,2,1,0:T(8,128)(2,1)}, u32[]{:S(2)}, u32[]{:S(2)}) collective-permute-start(bf16[2,2,256,128]{3,2,1,0:T(8,128)(2,1)} %get-tuple-element.145), channel_id=1, source_target_pairs={{0,1},{1,2},{2,3},{3,0},{4,5},{5,6},{6,7},{7,4},{8,9},{9,10},{10,1... | collective-permute-start | bytes 786440 | tf_op jit(solution)/shard_map/ppermute | solution.py:417
  103.9 28.3 %collective-permute-start.26 = (bf16[2,2,256,128]{3,2,1,0:T(8,128)(2,1)}, bf16[2,2,256,128]{3,2,1,0:T(8,128)(2,1)S(1)}, u32[]{:S(2)}, u32[]{:S(2)}) collective-permute-start(bf16[2,2,256,128]{3,2,1,0:T(8,128)(2,1)} %get-tuple-element.159), channel_id=1, source_target_pairs={{0,3},{1,0},{2,1},{3,2},{4,7},{5,4},{6,5},{7,6},{8,11},{9,8},{10,9... | collective-permute-start | bytes 786440 | tf_op jit(solution)/shard_map/ppermute | solution.py:417
  104.8 27.4 %collective-permute-start.27 = (bf16[2,2,256,128]{3,2,1,0:T(8,128)(2,1)}, bf16[2,2,256,128]{3,2,1,0:T(8,128)(2,1)S(1)}, u32[]{:S(2)}, u32[]{:S(2)}) collective-permute-start(bf16[2,2,256,128]{3,2,1,0:T(8,128)(2,1)} %get-tuple-element.160), channel_id=1, source_target_pairs={{0,2},{1,3},{2,0},{3,1},{4,6},{5,7},{6,4},{7,5},{8,10},{9,11},{10,... | collective-permute-start | bytes 786440 | tf_op jit(solution)/shard_map/ppermute | solution.py:417
  109.5 12.8 %collective-permute-start.23 = (bf16[4,416,128]{2,1,0:T(8,128)(2,1)S(1)}, bf16[4,416,128]{2,1,0:T(8,128)(2,1)S(1)}, u32[]{:S(2)}, u32[]{:S(2)}) collective-permute-start(bf16[4,416,128]{2,1,0:T(8,128)(2,1)S(1)} %get-tuple-element.155), channel_id=1, source_target_pairs={{0,8},{4,12},{8,0},{12,4},{16,24},{20,28},{24,16},{28,20},{1,9},{5... | collective-permute-start | bytes 1277960 | tf_op jit(solution)/shard_map/ppermute | solution.py:421
  110.1 20.7 %collective-permute-start.24 = (bf16[4,416,128]{2,1,0:T(8,128)(2,1)S(1)}, bf16[4,416,128]{2,1,0:T(8,128)(2,1)S(1)}, u32[]{:S(2)}, u32[]{:S(2)}) collective-permute-start(bf16[4,416,128]{2,1,0:T(8,128)(2,1)S(1)} %get-tuple-element.156), channel_id=1, source_target_pairs={{0,16},{4,20},{8,24},{12,28},{16,0},{20,4},{24,8},{28,12},{1,17},{... | collective-permute-start | bytes 1277960 | tf_op jit(solution)/shard_map/ppermute | solution.py:421
  110.6 20.2 %collective-permute-start.25 = (bf16[4,416,128]{2,1,0:T(8,128)(2,1)S(1)}, bf16[4,416,128]{2,1,0:T(8,128)(2,1)S(1)}, u32[]{:S(2)}, u32[]{:S(2)}) collective-permute-start(bf16[4,416,128]{2,1,0:T(8,128)(2,1)S(1)} %get-tuple-element.157), channel_id=1, source_target_pairs={{0,24},{4,28},{8,16},{12,20},{16,8},{20,12},{24,0},{28,4},{1,25},{... | collective-permute-start | bytes 1277960 | tf_op jit(solution)/shard_map/ppermute | solution.py:421
  122.3 10.0 %collective-permute-start.28 = (bf16[2,2,256,128]{3,2,1,0:T(8,128)(2,1)S(1)}, bf16[2,2,256,128]{3,2,1,0:T(8,128)(2,1)S(1)}, u32[]{:S(2)}, u32[]{:S(2)}) collective-permute-start(bf16[2,2,256,128]{3,2,1,0:T(8,128)(2,1)S(1)} %copy-done.24), channel_id=1, source_target_pairs={{0,1},{1,2},{2,3},{3,0},{4,5},{5,6},{6,7},{7,4},{8,9},{9,10},{10,1... | collective-permute-start | bytes 786440 | tf_op jit(solution)/shard_map/ppermute | solution.py:417
  132.7 10.4 %collective-permute-start.30 = (bf16[416,128]{1,0:T(8,128)(2,1)S(1)}, bf16[416,128]{1,0:T(8,128)(2,1)S(1)}, u32[]{:S(2)}, u32[]{:S(2)}) collective-permute-start(bf16[416,128]{1,0:T(8,128)(2,1)S(1)} %get-tuple-element.188), channel_id=1, source_target_pairs={{0,2},{1,3},{2,0},{3,1},{4,6},{5,7},{6,4},{7,5},{8,10},{9,11},{10,... | collective-permute-start | bytes 319496 | tf_op jit(solution)/shard_map/ppermute | solution.py:417
  (37 other events, 390.0 us)

commit v5 on v4

--- a/solution.py
+++ b/solution.py
@@ -9,6 +9,7 @@
 
 RUNS = ((1, 1), (2,))
 GROUP = 8
+GATED = True
 
 EPS = 1e-06
 ROOT_TWO_PI = 2.5066282746310002
@@ -32,17 +33,30 @@
     return lax.dot_general(a, b, (((ca,), (cb,)), ((), ())), preferred_element_type=F32)
 
 
-def body(n_blocks, taps, speakers, runs, first, last,
-         order_ref, spk_ref, live_ref, slot_ref, meta_ref, *refs):
+class Order:
+    def __init__(self, me, count):
+        self.me, self.count = me, count
+
+    def __getitem__(self, d):
+        return lax.rem(self.me + self.count - d, self.count)
+
+
+def body(n_blocks, taps, speakers, runs, first, last, each, first_slot,
+         meta_ref, spk_ref, count_ref, *refs):
     nb = n_blocks
+    order_ref = Order(meta_ref[0], nb)
     x0, g0 = refs[:2]
     k = 2
     p = []
     for _ in runs:
         p.append(refs[k:k + nb - 1])
         k += nb - 1
-    shares = refs[k:k + GROUP]
-    k += GROUP
+    if first:
+        shares = [refs[k + s % 2].at[s // 2] for s in range(GROUP)]
+        k += 2
+    else:
+        w_in, w_out, prm = refs[k:k + 3]
+        k += 3
     if not first:
         got = refs[k]
         k += 1
@@ -55,7 +69,10 @@
         keep, send = refs[k:k + 2]
         k += 2
         (gwi, gwo, *held, sems) = refs[-7:]
-    (nlow_all, blow_all, act_all, plow_all, gsm, xpad, gpad, normed, gin, slope, wide, b_in, w_in, w_out, prm) = refs[k:k + 15]
+    (nlow_all, blow_all, act_all, plow_all, gsm, *refs) = refs[k:]
+    if first:
+        w_in, w_out, prm, *refs = refs
+    xpad, gpad, normed, gin, slope, wide, b_in = refs[:7]
     i = pl.program_id(0)
     length, lanes = normed.shape[1], normed.shape[2]
     width = nb * lanes
@@ -76,21 +93,22 @@
             gpad[d, 0:PAD, :] = zero
             gpad[d, PAD + length:, :] = zero
         gsm[...] = jnp.zeros_like(gsm) if first else got[...]
-        ra, rb, rs = width // GROUP, per // GROUP, prm.shape[1] // GROUP
-        for s in range(GROUP):
-            part = meta_ref[1] ^ s
-
-            def unpack(d, carry):
-                c = order_ref[d]
-                for r in range(tiles):
-                    w_in[pl.ds(pl.multiple_of(part * ra, ra), ra), pl.ds(pl.multiple_of(c * per + r * lanes, lanes), lanes)] = shares[s][d, r * ra:(r + 1) * ra, :]
-                base = tiles * ra
-                for r in range(nb):
-                    w_out[pl.ds(pl.multiple_of(c * per + part * rb, 16), rb), r * lanes:(r + 1) * lanes] = shares[s][d, base + r * rb:base + (r + 1) * rb, :]
-                base += nb * rb
-                prm[d, pl.ds(pl.multiple_of(part * rs, rs), rs), :] = shares[s][d, base:base + rs, :].astype(F32)
-                return carry
-            lax.fori_loop(0, nb, unpack, 0)
+        if first:
+            ra, rb, rs = width // GROUP, per // GROUP, prm.shape[1] // GROUP
+            for s in range(GROUP):
+                part = meta_ref[1] ^ s
+
+                def unpack(d, carry):
+                    c = order_ref[d]
+                    for r in range(tiles):
+                        w_in[pl.ds(pl.multiple_of(part * ra, ra), ra), pl.ds(pl.multiple_of(c * per + r * lanes, lanes), lanes)] = shares[s][d, r * ra:(r + 1) * ra, :]
+                    base = tiles * ra
+                    for r in range(nb):
+                        w_out[pl.ds(pl.multiple_of(c * per + part * rb, 16), rb), r * lanes:(r + 1) * lanes] = shares[s][d, base + r * rb:base + (r + 1) * rb, :]
+                    base += nb * rb
+                    prm[d, pl.ds(pl.multiple_of(part * rs, rs), rs), :] = shares[s][d, base:base + rs, :].astype(F32)
+                    return carry
+                lax.fori_loop(0, nb, unpack, 0)
         for d in range(nb):
             for r in range(tiles):
                 at = pl.multiple_of(order_ref[d] * per + r * lanes, lanes)
@@ -114,8 +132,9 @@
                 gin[d] = part[d - 1][1, at]
         low += run
 
-    spk = spk_ref[i]
-    live = live_ref[i].astype(F32)
+    slot = meta_ref[0] * each + first_slot + i
+    spk = spk_ref[slot]
+    live = (slot < count_ref[0]).astype(F32)
     total = jnp.zeros((length, 1), F32)
     for d in range(nb):
         acc = jnp.broadcast_to(prm[d, r_cb:r_cb + 1, :], (length, lanes))
@@ -227,10 +246,11 @@
             lax.fori_loop(0, GROUP // 2, emit, 0)
 
 
-def block_call(order, spk, live, slot, meta, clips, grads, packed, shares, ff, taps, speakers, small_rows, carried, before):
+def block_call(meta, speaker, counts, low, clips, grads, packed, shares, ff, taps, speakers, small_rows, carried, before):
     nb = len(packed[0]) + 1
     runs = [part[0].shape[1] for part in packed]
     n = sum(runs)
+    each = clips.shape[0] // nb
     _, _, length, lanes = packed[0][0].shape
     width = nb * lanes
     first, last = carried is None, before is not None
@@ -239,7 +259,7 @@
     widths = (width, width, ff, ff)
     full = lambda shape: pl.BlockSpec(shape, lambda i, *_: (0,) * len(shape), pipeline_mode=pl.Buffered(1))
     step = lambda *shape: pl.BlockSpec((1,) + shape, lambda i, *_: (i,) + (0,) * len(shape))
-    own = pl.BlockSpec((1, length, lanes), lambda i, order, spk, live, slot, meta: (slot[i], 0, 0))
+    own = pl.BlockSpec((1, length, lanes), lambda i, meta, *_: (meta[0] * each + low + i, 0, 0))
     sums = (nb + 1, small_rows, lanes)
     args = [clips, grads] + [v for part in packed for v in part] + list(shares)
     in_specs = [own, own] + [full(v.shape) for v in args[2:]]
@@ -256,6 +276,9 @@
     else:
         out_shape += [jax.ShapeDtypeStruct((n, length, w), BF16) for w in widths] + [jax.ShapeDtypeStruct(sums, F32)]
         out_specs += [step(length, w) for w in widths] + [pl.BlockSpec(sums, lambda i, *_: (0, 0, 0))]
+        weights = [((width, ff), BF16), ((ff, width), BF16), ((nb, small_rows, lanes), F32)]
+        out_shape += [jax.ShapeDtypeStruct(shape, t) for shape, t in weights]
+        out_specs += [full(shape) for shape, _ in weights]
     scratch = [
         pltpu.VMEM((nb, length + 2 * PAD, lanes), F32),
         pltpu.VMEM((nb, length + 2 * PAD, lanes), F32),
@@ -264,55 +287,53 @@
         pltpu.VMEM((length, ff), F32),
         pltpu.VMEM((length, width), F32),
         pltpu.VMEM((1, ff), F32),
-        pltpu.VMEM((width, ff), BF16),
-        pltpu.VMEM((ff, width), BF16),
-        pltpu.VMEM((nb, small_rows, lanes), F32),
     ]
     if last:
         scratch = [pltpu.VMEM((n, length, w), BF16) for w in widths] + [pltpu.VMEM(sums, F32)] + scratch
         scratch += [pltpu.VMEM((ff // lanes, width, lanes), F32), pltpu.VMEM((ff, width), F32)]
         scratch += [pltpu.VMEM(v.shape, BF16) for v in before] + [pltpu.SemaphoreType.DMA((4,))]
     return pl.pallas_call(
-        functools.partial(body, nb, taps, speakers, runs, first, last),
+        functools.partial(body, nb, taps, speakers, runs, first, last, each, low),
         out_shape=out_shape,
         grid_spec=pltpu.PrefetchScalarGridSpec(
-            num_scalar_prefetch=5, grid=(n,), in_specs=in_specs, out_specs=out_specs, scratch_shapes=scratch),
+            num_scalar_prefetch=3, grid=(n,), in_specs=in_specs, out_specs=out_specs, scratch_shapes=scratch),
         cost_estimate=pl.CostEstimate(flops=HINT if last else 0, transcendentals=0, bytes_accessed=0),
         compiler_params=pltpu.CompilerParams(dimension_semantics=("arbitrary",), vmem_limit_bytes=60 << 20),
         name="block",
-    )(order, spk, live, slot, meta, *args)
-
-
-def pack_body(moves, slot_ref, clips, grads, *refs):
+    )(meta, speaker, counts, *args)
+
+
+def pack_body(runs, nb, meta_ref, clips, grads, *refs):
     blocks, sems = refs[:-1], refs[-1]
-    copies = []
-    for j, (at, r, source) in enumerate(moves):
-        for q, array in enumerate((clips, grads)):
-            copies.append(pltpu.make_async_copy(array.at[slot_ref[source]], blocks[at].at[q, r], sems.at[2 * j + q]))
+    each = clips.shape[0] // nb
+    copies, low, at = [], 0, 0
+    for run in runs:
+        for d in range(1, nb):
+            slot = lax.rem(meta_ref[0] + d, nb) * each + low
+            for q, array in enumerate((clips, grads)):
+                copies.append(pltpu.make_async_copy(array.at[pl.ds(slot, run)], blocks[at].at[q], sems.at[2 * at + q]))
+            at += 1
+        low += run
     for copy in copies:
         copy.start()
     for copy in copies:
         copy.wait()
 
 
-def pack_call(slots, blocks, clips, grads):
+def pack_call(meta, runs, nb, clips, grads):
     length, lanes = clips.shape[1:]
-    moves, source = [], 0
-    for at, run in enumerate(blocks):
-        for r in range(run):
-            moves.append((at, r, source))
-            source += 1
     hbm = pl.BlockSpec(memory_space=pl.ANY)
     sm = pl.BlockSpec(memory_space=pltpu.SMEM)
     vm = pl.BlockSpec(memory_space=pltpu.VMEM)
+    blocks = [jax.ShapeDtypeStruct((2, run, length, lanes), BF16) for run in runs for _ in range(1, nb)]
     return pl.pallas_call(
-        functools.partial(pack_body, moves),
-        out_shape=[jax.ShapeDtypeStruct((2, run, length, lanes), BF16) for run in blocks],
+        functools.partial(pack_body, runs, nb),
+        out_shape=blocks,
         in_specs=[sm, hbm, hbm],
         out_specs=[vm] * len(blocks),
-        scratch_shapes=[pltpu.SemaphoreType.DMA((2 * len(moves),))],
+        scratch_shapes=[pltpu.SemaphoreType.DMA((2 * len(blocks),))],
         name="pack",
-    )(slots, clips, grads)
+    )(meta, clips, grads)
 
 
 def share_body(taps, speakers, place_ref, w_in, w_out, scale, shift, conv, cb, bo, ls, bi, share, small):
@@ -337,7 +358,7 @@
     for r in range(w_out.shape[1] // lanes):
         share[base + r * rb:base + (r + 1) * rb, :] = w_out[:, r * lanes:(r + 1) * lanes]
     base += w_out.shape[1] // lanes * rb
-    share[base:base + rs, :] = small[pl.ds(pl.multiple_of(place_ref[0] * rs, rs), rs), :].astype(BF16)
+    share[base:base + rs, :] = small[pl.ds(pl.multiple_of(place_ref[1] * rs, rs), rs), :].astype(BF16)
 
 
 def share_call(place, w_in, w_out, small, small_rows):
@@ -346,7 +367,7 @@
     ra, rb = w_in.shape[0] // GROUP, w_out.shape[0] // GROUP
     rows = w_in.shape[1] // lanes * ra + w_out.shape[1] // lanes * rb + small_rows // GROUP
     full = lambda shape: pl.BlockSpec(shape, lambda i, *_: (0,) * len(shape))
-    share_row = lambda shape: pl.BlockSpec(shape, lambda i, place: (place[0], 0))
+    share_row = lambda shape: pl.BlockSpec(shape, lambda i, place: (place[1], 0))
     return pl.pallas_call(
         functools.partial(share_body, taps, speakers),
         out_shape=jax.ShapeDtypeStruct((rows, lanes), BF16),
@@ -422,12 +443,11 @@
 
 
 def gather_group(v, dp_count, gates):
-    core = flip("dp", dp_count, 1)
     a, b = flip("dp", dp_count, 2)(v), flip("dp", dp_count, 4)(v)
     a, *one = lax.optimization_barrier((a, *gates[0]))
-    c = flip("dp", dp_count, 4)(a)
-    c, *two = lax.optimization_barrier((c, *gates[1]))
-    return [v, core(v), a, core(a), b, core(b), c, core(c)], (one, two)
+    near = jnp.stack([v, a, b, flip("dp", dp_count, 4)(a)])
+    near, *two = lax.optimization_barrier((near, *gates[1]))
+    return [near, flip("dp", dp_count, 1)(near)], (one, two)
 
 
 def gather_small(v, dp_count):
@@ -447,25 +467,18 @@
     per = w_in.shape[1]
     tiles = per // lanes
     width = nb * lanes
-    order = (me - jnp.arange(nb, dtype=jnp.int32)) % nb
     place = dp % GROUP
     sizes = [sum(r) for r in RUNS]
-    starts = [nb * sum(sizes[:k]) for k in range(len(sizes))]
-    assert clip_num == nb * sum(sizes)
+    each = clip_num // nb
+    assert each == sum(sizes)
+    meta = jnp.stack([me, place]).astype(jnp.int32)
+
     ra, rb = width // GROUP, per // GROUP
     small = [scale_table, shift_table, conv_weight, conv_bias, b_out, layer_scale, b_in]
     used = 2 * speakers + taps + 3 + tiles
     small_rows = -(-used // (GROUP * 16)) * GROUP * 16
-    slots, blocks = [], []
-    for start, n, runs in zip(starts, sizes, RUNS):
-        low = 0
-        for run in runs:
-            for d in range(1, nb):
-                blocks.append(run)
-                slots.append(start + (me + d) % nb * n + low + jnp.arange(run))
-            low += run
-    share = share_call(place.astype(jnp.int32)[None], w_in, w_out, small, small_rows)
-    packed = pack_call(jnp.concatenate(slots).astype(jnp.int32), blocks, clips_in, grad_out)
+    share = share_call(meta, w_in, w_out, small, small_rows)
+    packed = pack_call(meta, sum(RUNS, ()), nb, clips_in, grad_out)
 
     shares = [share] + [ring("chan", nb, d)(share) for d in range(1, nb)]
     stacked = stack_call(shares)
@@ -477,27 +490,23 @@
         for _ in runs:
             packed[-1].append(came[:nb - 1])
             came = came[nb - 1:]
-    meta = jnp.stack([me, place]).astype(jnp.int32)
     gathered, packed[0] = gather_group(stacked, dp_count, packed[0])
 
-    sums, kept, back = None, None, []
-    for k, (start, n) in enumerate(zip(starts, sizes)):
-        base = start + me * n
-        slot = (base + jnp.arange(n)).astype(jnp.int32)
-        spk = lax.dynamic_slice_in_dim(speaker, base, n)
-        live = (slot < counts[0]).astype(jnp.int32)
-        out = block_call(order, spk, live, slot, meta, clips_in, grad_out, packed[k], gathered, nb * per,
+    sums, kept, back, low = None, None, [], 0
+    for k, n in enumerate(sizes):
+        out = block_call(meta, speaker, counts, low, clips_in, grad_out, packed[k], gathered, nb * per,
                          taps, speakers, small_rows, sums, kept)
         if k:
             keep, send = out[nb:]
         else:
-            kept, sums = out[nb:nb + 4], out[nb + 4]
+            kept, sums, gathered = out[nb:nb + 4], out[nb + 4], out[nb + 5:]
         sent = out[:nb]
         if k:
-            sent, back[0] = lax.optimization_barrier((sent, back[0]))
-        else:
-            sent, packed[1] = lax.optimization_barrier((sent, packed[1]))
+            sent, back[0][2] = lax.optimization_barrier((sent, back[0][2]))
+        elif GATED:
+            sent, packed[1][0][1] = lax.optimization_barrier((sent, packed[1][0][1]))
         back.append([sent[0]] + [ring("chan", nb, -d)(sent[d]) for d in range(1, nb)])
+        low += n
 
     send, *back[0] = lax.optimization_barrier((send, *back[0]))
     got = flip("dp", dp_count, 1)(send)
@@ -519,7 +528,7 @@
     grad_clips = grad_out.astype(F32)
     for k, n in enumerate(sizes):
         for d in range(nb):
-            at = starts[k] + (me + d) % nb * n
+            at = (me + d) % nb * each + sum(sizes[:k])
             clips_out = lax.dynamic_update_slice_in_dim(clips_out, back[k][d][0], at, 0)
             g = lax.dynamic_slice_in_dim(grad_out, at, n).astype(F32) + back[k][d][1].astype(F32)
             grad_clips = lax.dynamic_update_slice_in_dim(grad_clips, g, at, 0)

time: 157 us -> 150 us (0.955)
  waiting for transfers between devices: 48.3 us -> 35.5 us
  starting transfers between devices: 43.8 us -> 52.3 us
    ppermute x21, waiting for transfers between devices: 27.8 us -> 15.2 us  [ring(): lax.ppermute(v, axis, [(i, (i + shift) % size) for i in range(size)])]
    ppermute x21, starting transfers between devices: 31.4 us -> 40.4 us  [ring(): lax.ppermute(v, axis, [(i, (i + shift) % size) for i in range(size)])]
    ppermute x15 -> x12, starting transfers between devices: 12.3 us -> 11.8 us  [flip(): return lambda v: lax.ppermute(v, axis, [(i, i ^ mask) for i in range(size)])]
    unnamed x50 -> x36, local copies, waits for them, and re-layouts: 3.63 us -> 3.34 us
    ppermute x15 -> x12, waiting for transfers between devices: 20.5 us -> 20.2 us  [flip(): return lambda v: lax.ppermute(v, axis, [(i, i ^ mask) for i in range(size)])]
  transfers between devices with their start and end apart: 36 -> 33, of which waited for: 16 -> 13; matrix products, arithmetic and copies ran while one was open for 9% -> 7% of each run, Pallas kernels for 25% -> 26%
where the time goes in v5:
time: 150 us
  starting transfers between devices  52.3 us (35%)
  Pallas kernels  45.2 us (30%)
  waiting for transfers between devices  35.5 us (24%)
  other arithmetic  8.54 us (6%)
  local copies, waits for them, and re-layouts  6.51 us (4%)
  between operations  1.99 us (1%)
    ppermute x21, starting transfers between devices, ring(): lax.ppermute(v, axis, [(i, (i + shift) % size) for i in range(size)])  40.4 us
    pallas_call x2, Pallas kernels, block_call(): pl.pallas_call(functools.partial(body, nb, taps, speakers, runs, first, l...  35.3 us
    ppermute x12, waiting for transfers between devices, flip(): return lambda v: lax.ppermute(v, axis, [(i, i ^ mask) for i in range(size)])  20.2 us
    ppermute x21, waiting for transfers between devices, ring(): lax.ppermute(v, axis, [(i, (i + shift) % size) for i in range(size)])  15.2 us
    ppermute x12, starting transfers between devices, flip(): return lambda v: lax.ppermute(v, axis, [(i, i ^ mask) for i in range(size)])  11.8 us
    pallas_call x1, Pallas kernels, pack_call(): pl.pallas_call(functools.partial(pack_body, runs, nb), out_shape=blocks,...  3.41 us
    unnamed x36, local copies, waits for them, and re-layouts  3.34 us
  transfers between devices with their start and end apart: 33, of which 13 were waited for; matrix products, arithmetic and copies ran while one was open for 7% of the time, Pallas kernels for 26%

profile of v5, /device:TPU:0, one launch (start us, length us, event | category | flops | bytes accessed | tf_op | source)
XLA Modules:
  0.0 150.0 jit_solution(3121498221543136480)
XLA Ops:
  1.2 2.2 %share.1.refs_0_ = bf16[416,128]{1,0:T(8,128)(2,1)} custom-call(s32[2]{0:T(128)} %pad_add_fusion.place_ref.meta_ref, bf16[512,384]{1,0:T(8,128)(2,1)} %w_in.1, bf16[384,512]{1,0:T(8,128)(2,1)} %w_out.1, bf16[64,128]{1,0:T(8,128)(2,1)} %scale.1, bf16[64,128]{1,0:T(8,128)(2,1)} %shift.1, bf16[7,128]{1,0:T(8,128)(2,1)} %conv.1, bf16[128]{0:T(256)(128)(2,1)} %cb.1, ...), custom_call_target="tpu_custom_call" | custom-call | tf_op jit(solution)/shard_map/share/pallas_call | solution.py:371
  3.5 3.1 %collective-permute-start = (bf16[416,128]{1,0:T(8,128)(2,1)}, bf16[416,128]{1,0:T(8,128)(2,1)S(1)}, u32[]{:S(2)}, u32[]{:S(2)}) collective-permute-start(bf16[416,128]{1,0:T(8,128)(2,1)} %share.1.refs_0_), channel_id=1, source_target_pairs={{0,1},{1,2},{2,3},{3,0},{4,5},{5,6},{6,7},{7,4},{8,9},{9,10},{10,1... | collective-permute-start | bytes 319496 | tf_op jit(solution)/shard_map/ppermute | solution.py:438
  6.5 2.6 %collective-permute-start.1 = (bf16[416,128]{1,0:T(8,128)(2,1)}, bf16[416,128]{1,0:T(8,128)(2,1)S(1)}, u32[]{:S(2)}, u32[]{:S(2)}) collective-permute-start(bf16[416,128]{1,0:T(8,128)(2,1)} %share.1.refs_0_), channel_id=1, source_target_pairs={{0,2},{1,3},{2,0},{3,1},{4,6},{5,7},{6,4},{7,5},{8,10},{9,11},{10,... | collective-permute-start | bytes 319496 | tf_op jit(solution)/shard_map/ppermute | solution.py:438
  10.5 3.4 %pack.1 = (bf16[2,1,256,128]{3,2,1,0:T(8,128)(2,1)}, bf16[2,1,256,128]{3,2,1,0:T(8,128)(2,1)}, bf16[2,1,256,128]{3,2,1,0:T(8,128)(2,1)}, bf16[2,1,256,128]{3,2,1...) custom-call(s32[2]{0:T(128)} %pad_add_fusion.place_ref.meta_ref, ...), custom_call_target="tpu_custom_call" | custom-call | tf_op jit(solution)/shard_map/pack/pallas_call | solution.py:329
  13.9 2.5 %collective-permute-done.1.refs_2_ = bf16[416,128]{1,0:T(8,128)(2,1)S(1)} collective-permute-done((bf16[416,128]{1,0:T(8,128)(2,1)}, bf16[416,128]{1,0:T(8,128)(2,1)S(1)}, u32[]{:S(2)}, u32[]{:S(2)}) %collective-permute-start.1) | collective-permute-done | bytes 106528 | tf_op jit(solution)/shard_map/ppermute | solution.py:438
  21.0 2.1 %collective-permute-start.5 = (bf16[2,1,256,128]{3,2,1,0:T(8,128)(2,1)}, bf16[2,1,256,128]{3,2,1,0:T(8,128)(2,1)S(1)}, u32[]{:S(2)}, u32[]{:S(2)}) collective-permute-start(bf16[2,1,256,128]{3,2,1,0:T(8,128)(2,1)} %get-tuple-element.106), channel_id=1, source_target_pairs={{0,1},{1,2},{2,3},{3,0},{4,5},{5,6},{6,7},{7,4},{8,9},{9,10},{10,1... | collective-permute-start | bytes 393224 | tf_op jit(solution)/shard_map/ppermute | solution.py:438
  23.1 2.2 %collective-permute-start.6 = (bf16[2,1,256,128]{3,2,1,0:T(8,128)(2,1)}, bf16[2,1,256,128]{3,2,1,0:T(8,128)(2,1)S(1)}, u32[]{:S(2)}, u32[]{:S(2)}) collective-permute-start(bf16[2,1,256,128]{3,2,1,0:T(8,128)(2,1)} %get-tuple-element.107), channel_id=1, source_target_pairs={{0,2},{1,3},{2,0},{3,1},{4,6},{5,7},{6,4},{7,5},{8,10},{9,11},{10,... | collective-permute-start | bytes 393224 | tf_op jit(solution)/shard_map/ppermute | solution.py:438
  27.3 2.2 %collective-permute-done.5.refs_2_ = bf16[2,1,256,128]{3,2,1,0:T(8,128)(2,1)S(1)} collective-permute-done((bf16[2,1,256,128]{3,2,1,0:T(8,128)(2,1)}, bf16[2,1,256,128]{3,2,1,0:T(8,128)(2,1)S(1)}, u32[]{:S(2)}, u32[]{:S(2)}) %collective-permute-start.5) | collective-permute-done | bytes 131104 | tf_op jit(solution)/shard_map/ppermute | solution.py:438
  29.5 4.3 %collective-permute-done.6.refs_3_ = bf16[2,1,256,128]{3,2,1,0:T(8,128)(2,1)S(1)} collective-permute-done((bf16[2,1,256,128]{3,2,1,0:T(8,128)(2,1)}, bf16[2,1,256,128]{3,2,1,0:T(8,128)(2,1)S(1)}, u32[]{:S(2)}, u32[]{:S(2)}) %collective-permute-start.6) | collective-permute-done | bytes 131104 | tf_op jit(solution)/shard_map/ppermute | solution.py:438
  35.4 3.2 %collective-permute-start.10 = (bf16[2,1,256,128]{3,2,1,0:T(8,128)(2,1)}, bf16[2,1,256,128]{3,2,1,0:T(8,128)(2,1)S(1)}, u32[]{:S(2)}, u32[]{:S(2)}) collective-permute-start(bf16[2,1,256,128]{3,2,1,0:T(8,128)(2,1)} %get-tuple-element.113), channel_id=1, source_target_pairs={{0,1},{1,2},{2,3},{3,0},{4,5},{5,6},{6,7},{7,4},{8,9},{9,10},{10,1... | collective-permute-start | bytes 393224 | tf_op jit(solution)/shard_map/ppermute | solution.py:438
  41.0 4.8 %collective-permute-done.9 = bf16[4,416,128]{2,1,0:T(8,128)(2,1)S(1)} collective-permute-done((bf16[4,416,128]{2,1,0:T(8,128)(2,1)S(1)}, bf16[4,416,128]{2,1,0:T(8,128)(2,1)S(1)}, u32[]{:S(2)}, u32[]{:S(2)}) %collective-permute-start.9) | collective-permute-done | bytes 426016 | tf_op jit(solution)/shard_map/ppermute | solution.py:442
  48.2 2.4 %collective-permute-start.14 = (bf16[2,2,256,128]{3,2,1,0:T(8,128)(2,1)}, bf16[2,2,256,128]{3,2,1,0:T(8,128)(2,1)}, u32[]{:S(2)}, u32[]{:S(2)}) collective-permute-start(bf16[2,2,256,128]{3,2,1,0:T(8,128)(2,1)} %get-tuple-element.124), channel_id=1, source_target_pairs={{0,2},{1,3},{2,0},{3,1},{4,6},{5,7},{6,4},{7,5},{8,10},{9,11},{10,... | collective-permute-start | bytes 786440 | tf_op jit(solution)/shard_map/ppermute | solution.py:438
  50.5 3.4 %collective-permute-start.15 = (bf16[2,2,256,128]{3,2,1,0:T(8,128)(2,1)}, bf16[2,2,256,128]{3,2,1,0:T(8,128)(2,1)}, u32[]{:S(2)}, u32[]{:S(2)}) collective-permute-start(bf16[2,2,256,128]{3,2,1,0:T(8,128)(2,1)} %get-tuple-element.126), channel_id=1, source_target_pairs={{0,3},{1,0},{2,1},{3,2},{4,7},{5,4},{6,5},{7,6},{8,11},{9,8},{10,9... | collective-permute-start | bytes 786440 | tf_op jit(solution)/shard_map/ppermute | solution.py:438
  55.9 16.5 %block.2 = (bf16[2,2,256,128]{3,2,1,0:T(8,128)(2,1)}, bf16[2,2,256,128]{3,2,1,0:T(8,128)(2,1)}, bf16[2,2,256,128]{3,2,1,0:T(8,128)(2,1)}, bf16[2,2,256,128]{3,2,...) custom-call(s32[2]{0:T(128)} %pad_add_fusion.place_ref.meta_ref, ...), custom_call_target="tpu_custom_call" | custom-call | tf_op jit(solution)/shard_map/block/pallas_call | solution.py:295
  73.6 2.9 %collective-permute-start.16 = (bf16[2,2,256,128]{3,2,1,0:T(8,128)(2,1)}, bf16[2,2,256,128]{3,2,1,0:T(8,128)(2,1)}, u32[]{:S(2)}, u32[]{:S(2)}) collective-permute-start(bf16[2,2,256,128]{3,2,1,0:T(8,128)(2,1)} %get-tuple-element.138), channel_id=1, source_target_pairs={{0,3},{1,0},{2,1},{3,2},{4,7},{5,4},{6,5},{7,6},{8,11},{9,8},{10,9... | collective-permute-start | bytes 786440 | tf_op jit(solution)/shard_map/ppermute | solution.py:438
  76.8 18.9 %block.3 = (bf16[2,2,256,128]{3,2,1,0:T(8,128)(2,1)}, bf16[2,2,256,128]{3,2,1,0:T(8,128)(2,1)}, bf16[2,2,256,128]{3,2,1,0:T(8,128)(2,1)}, bf16[2,2,256,128]{3,2,...) custom-call(s32[2]{0:T(128)} %pad_add_fusion.place_ref.meta_ref, s32[16]{0:T(128)} %spk_ref.3, ...), custom_call_target="tpu_custom_call" | custom-call | flops 68719476736 | tf_op jit(solution)/shard_map/block/pallas_call | solution.py:295
  96.1 3.6 %collective-permute-start.23 = (bf16[2,2,256,128]{3,2,1,0:T(8,128)(2,1)}, bf16[2,2,256,128]{3,2,1,0:T(8,128)(2,1)S(1)}, u32[]{:S(2)}, u32[]{:S(2)}) collective-permute-start(bf16[2,2,256,128]{3,2,1,0:T(8,128)(2,1)} %get-tuple-element.155), channel_id=1, source_target_pairs={{0,3},{1,0},{2,1},{3,2},{4,7},{5,4},{6,5},{7,6},{8,11},{9,8},{10,9... | collective-permute-start | bytes 786440 | tf_op jit(solution)/shard_map/ppermute | solution.py:438
  104.2 2.5 %collective-permute-start.22 = (bf16[4,416,128]{2,1,0:T(8,128)(2,1)S(1)}, bf16[4,416,128]{2,1,0:T(8,128)(2,1)S(1)}, u32[]{:S(2)}, u32[]{:S(2)}) collective-permute-start(bf16[4,416,128]{2,1,0:T(8,128)(2,1)S(1)} %get-tuple-element.153), channel_id=1, source_target_pairs={{0,24},{4,28},{8,16},{12,20},{16,8},{20,12},{24,0},{28,4},{1,25},{... | collective-permute-start | bytes 1277960 | tf_op jit(solution)/shard_map/ppermute | solution.py:442
  112.6 3.3 %collective-permute-done.20 = bf16[4,416,128]{2,1,0:T(8,128)(2,1)S(1)} collective-permute-done((bf16[4,416,128]{2,1,0:T(8,128)(2,1)S(1)}, bf16[4,416,128]{2,1,0:T(8,128)(2,1)S(1)}, u32[]{:S(2)}, u32[]{:S(2)}) %collective-permute-start.20) | collective-permute-done | bytes 426016 | tf_op jit(solution)/shard_map/ppermute | solution.py:442
  117.9 6.2 %collective-permute-done.21 = bf16[4,416,128]{2,1,0:T(8,128)(2,1)S(1)} collective-permute-done((bf16[4,416,128]{2,1,0:T(8,128)(2,1)S(1)}, bf16[4,416,128]{2,1,0:T(8,128)(2,1)S(1)}, u32[]{:S(2)}, u32[]{:S(2)}) %collective-permute-start.21) | collective-permute-done | bytes 426016 | tf_op jit(solution)/shard_map/ppermute | solution.py:442
  125.9 2.4 %collective-permute-start.26 = (bf16[416,128]{1,0:T(8,128)(2,1)S(1)}, bf16[416,128]{1,0:T(8,128)(2,1)S(1)}, u32[]{:S(2)}, u32[]{:S(2)}) collective-permute-start(bf16[416,128]{1,0:T(8,128)(2,1)S(1)} %get-tuple-element.182), channel_id=1, source_target_pairs={{0,1},{1,2},{2,3},{3,0},{4,5},{5,6},{6,7},{7,4},{8,9},{9,10},{10,1... | collective-permute-start | bytes 319496 | tf_op jit(solution)/shard_map/ppermute | solution.py:438
  129.0 2.8 %collective-permute-start.28 = (bf16[416,128]{1,0:T(8,128)(2,1)S(1)}, bf16[416,128]{1,0:T(8,128)(2,1)S(1)}, u32[]{:S(2)}, u32[]{:S(2)}) collective-permute-start(bf16[416,128]{1,0:T(8,128)(2,1)S(1)} %get-tuple-element.183), channel_id=1, source_target_pairs={{0,3},{1,0},{2,1},{3,2},{4,7},{5,4},{6,5},{7,6},{8,11},{9,8},{10,9... | collective-permute-start | bytes 319496 | tf_op jit(solution)/shard_map/ppermute | solution.py:438
  133.7 3.3 %collective-permute-done.27 = bf16[416,128]{1,0:T(8,128)(2,1)S(1)} collective-permute-done((bf16[416,128]{1,0:T(8,128)(2,1)S(1)}, bf16[416,128]{1,0:T(8,128)(2,1)S(1)}, u32[]{:S(2)}, u32[]{:S(2)}) %collective-permute-start.27) | collective-permute-done | bytes 106528 | tf_op jit(solution)/shard_map/ppermute | solution.py:438
  147.4 2.4 %finish.1 = (f32[512,384]{1,0:T(8,128)}, f32[384,512]{1,0:T(8,128)}, f32[64,128]{1,0:T(8,128)}, f32[64,128]{1,0:T(8,128)}, f32[7,128]{1,0:T(8,128)}, /*index=5*/...) custom-call(s32[2]{0:T(128)} %pad_add_fusion.place_ref.meta_ref, bf16[4,416,128]{2,1,0:T(8,128)(2,1)} %copy-done.3, ...), custom_call_target="tpu_custom_call" | custom-call | tf_op jit(solution)/shard_map/finish/pallas_call | solution.py:427
  (110 shorter events, 44.9 us)
Async XLA Ops:
  3.5 10.4 %collective-permute-start = (bf16[416,128]{1,0:T(8,128)(2,1)}, bf16[416,128]{1,0:T(8,128)(2,1)S(1)}, u32[]{:S(2)}, u32[]{:S(2)}) collective-permute-start(bf16[416,128]{1,0:T(8,128)(2,1)} %share.1.refs_0_), channel_id=1, source_target_pairs={{0,1},{1,2},{2,3},{3,0},{4,5},{5,6},{6,7},{7,4},{8,9},{9,10},{10,1... | collective-permute-start | bytes 319496 | tf_op jit(solution)/shard_map/ppermute | solution.py:438
  6.5 9.9 %collective-permute-start.1 = (bf16[416,128]{1,0:T(8,128)(2,1)}, bf16[416,128]{1,0:T(8,128)(2,1)S(1)}, u32[]{:S(2)}, u32[]{:S(2)}) collective-permute-start(bf16[416,128]{1,0:T(8,128)(2,1)} %share.1.refs_0_), channel_id=1, source_target_pairs={{0,2},{1,3},{2,0},{3,1},{4,6},{5,7},{6,4},{7,5},{8,10},{9,11},{10,... | collective-permute-start | bytes 319496 | tf_op jit(solution)/shard_map/ppermute | solution.py:438
  19.5 14.3 %collective-permute-start.4 = (bf16[4,416,128]{2,1,0:T(8,128)(2,1)}, bf16[4,416,128]{2,1,0:T(8,128)(2,1)S(1)}, u32[]{:S(2)}, u32[]{:S(2)}) collective-permute-start(bf16[4,416,128]{2,1,0:T(8,128)(2,1)} %gathered.1), channel_id=1, source_target_pairs={{0,8},{4,12},{8,0},{12,4},{16,24},{20,28},{24,16},{28,20},{1,9},{5... | collective-permute-start | bytes 1277960 | tf_op jit(solution)/shard_map/ppermute | solution.py:442
  21.0 8.5 %collective-permute-start.5 = (bf16[2,1,256,128]{3,2,1,0:T(8,128)(2,1)}, bf16[2,1,256,128]{3,2,1,0:T(8,128)(2,1)S(1)}, u32[]{:S(2)}, u32[]{:S(2)}) collective-permute-start(bf16[2,1,256,128]{3,2,1,0:T(8,128)(2,1)} %get-tuple-element.106), channel_id=1, source_target_pairs={{0,1},{1,2},{2,3},{3,0},{4,5},{5,6},{6,7},{7,4},{8,9},{9,10},{10,1... | collective-permute-start | bytes 393224 | tf_op jit(solution)/shard_map/ppermute | solution.py:438
  23.1 10.6 %collective-permute-start.6 = (bf16[2,1,256,128]{3,2,1,0:T(8,128)(2,1)}, bf16[2,1,256,128]{3,2,1,0:T(8,128)(2,1)S(1)}, u32[]{:S(2)}, u32[]{:S(2)}) collective-permute-start(bf16[2,1,256,128]{3,2,1,0:T(8,128)(2,1)} %get-tuple-element.107), channel_id=1, source_target_pairs={{0,2},{1,3},{2,0},{3,1},{4,6},{5,7},{6,4},{7,5},{8,10},{9,11},{10,... | collective-permute-start | bytes 393224 | tf_op jit(solution)/shard_map/ppermute | solution.py:438
  25.4 8.4 %collective-permute-start.7 = (bf16[2,1,256,128]{3,2,1,0:T(8,128)(2,1)}, bf16[2,1,256,128]{3,2,1,0:T(8,128)(2,1)S(1)}, u32[]{:S(2)}, u32[]{:S(2)}) collective-permute-start(bf16[2,1,256,128]{3,2,1,0:T(8,128)(2,1)} %get-tuple-element.108), channel_id=1, source_target_pairs={{0,3},{1,0},{2,1},{3,2},{4,7},{5,4},{6,5},{7,6},{8,11},{9,8},{10,9... | collective-permute-start | bytes 393224 | tf_op jit(solution)/shard_map/ppermute | solution.py:438
  25.7 15.2 %collective-permute-start.8 = (bf16[4,416,128]{2,1,0:T(8,128)(2,1)}, bf16[4,416,128]{2,1,0:T(8,128)(2,1)S(1)}, u32[]{:S(2)}, u32[]{:S(2)}) collective-permute-start(bf16[4,416,128]{2,1,0:T(8,128)(2,1)} %gathered.1), channel_id=1, source_target_pairs={{0,16},{4,20},{8,24},{12,28},{16,0},{20,4},{24,8},{28,12},{1,17},{... | collective-permute-start | bytes 1277960 | tf_op jit(solution)/shard_map/ppermute | solution.py:442
  33.8 11.9 %collective-permute-start.9 = (bf16[4,416,128]{2,1,0:T(8,128)(2,1)S(1)}, bf16[4,416,128]{2,1,0:T(8,128)(2,1)S(1)}, u32[]{:S(2)}, u32[]{:S(2)}) collective-permute-start(bf16[4,416,128]{2,1,0:T(8,128)(2,1)S(1)} %collective-permute-done.4), channel_id=1, source_target_pairs={{0,16},{4,20},{8,24},{12,28},{16,0},{20,4},{24,8},{28,12},{1,17},{... | collective-permute-start | bytes 1277960 | tf_op jit(solution)/shard_map/ppermute | solution.py:442
  35.4 11.6 %collective-permute-start.10 = (bf16[2,1,256,128]{3,2,1,0:T(8,128)(2,1)}, bf16[2,1,256,128]{3,2,1,0:T(8,128)(2,1)S(1)}, u32[]{:S(2)}, u32[]{:S(2)}) collective-permute-start(bf16[2,1,256,128]{3,2,1,0:T(8,128)(2,1)} %get-tuple-element.113), channel_id=1, source_target_pairs={{0,1},{1,2},{2,3},{3,0},{4,5},{5,6},{6,7},{7,4},{8,9},{9,10},{10,1... | collective-permute-start | bytes 393224 | tf_op jit(solution)/shard_map/ppermute | solution.py:438
  38.6 9.6 %collective-permute-start.11 = (bf16[2,1,256,128]{3,2,1,0:T(8,128)(2,1)}, bf16[2,1,256,128]{3,2,1,0:T(8,128)(2,1)S(1)}, u32[]{:S(2)}, u32[]{:S(2)}) collective-permute-start(bf16[2,1,256,128]{3,2,1,0:T(8,128)(2,1)} %get-tuple-element.114), channel_id=1, source_target_pairs={{0,2},{1,3},{2,0},{3,1},{4,6},{5,7},{6,4},{7,5},{8,10},{9,11},{10,... | collective-permute-start | bytes 393224 | tf_op jit(solution)/shard_map/ppermute | solution.py:438
  39.7 8.5 %collective-permute-start.12 = (bf16[2,1,256,128]{3,2,1,0:T(8,128)(2,1)}, bf16[2,1,256,128]{3,2,1,0:T(8,128)(2,1)}, u32[]{:S(2)}, u32[]{:S(2)}) collective-permute-start(bf16[2,1,256,128]{3,2,1,0:T(8,128)(2,1)} %get-tuple-element.115), channel_id=1, source_target_pairs={{0,3},{1,0},{2,1},{3,2},{4,7},{5,4},{6,5},{7,6},{8,11},{9,8},{10,9... | collective-permute-start | bytes 393224 | tf_op jit(solution)/shard_map/ppermute | solution.py:438
  48.2 24.2 %collective-permute-start.14 = (bf16[2,2,256,128]{3,2,1,0:T(8,128)(2,1)}, bf16[2,2,256,128]{3,2,1,0:T(8,128)(2,1)}, u32[]{:S(2)}, u32[]{:S(2)}) collective-permute-start(bf16[2,2,256,128]{3,2,1,0:T(8,128)(2,1)} %get-tuple-element.124), channel_id=1, source_target_pairs={{0,2},{1,3},{2,0},{3,1},{4,6},{5,7},{6,4},{7,5},{8,10},{9,11},{10,... | collective-permute-start | bytes 786440 | tf_op jit(solution)/shard_map/ppermute | solution.py:438
  50.5 26.3 %collective-permute-start.15 = (bf16[2,2,256,128]{3,2,1,0:T(8,128)(2,1)}, bf16[2,2,256,128]{3,2,1,0:T(8,128)(2,1)}, u32[]{:S(2)}, u32[]{:S(2)}) collective-permute-start(bf16[2,2,256,128]{3,2,1,0:T(8,128)(2,1)} %get-tuple-element.126), channel_id=1, source_target_pairs={{0,3},{1,0},{2,1},{3,2},{4,7},{5,4},{6,5},{7,6},{8,11},{9,8},{10,9... | collective-permute-start | bytes 786440 | tf_op jit(solution)/shard_map/ppermute | solution.py:438
  53.9 22.9 %collective-permute-start.3 = (bf16[2,2,256,128]{3,2,1,0:T(8,128)(2,1)}, bf16[2,2,256,128]{3,2,1,0:T(8,128)(2,1)}, u32[]{:S(2)}, u32[]{:S(2)}) collective-permute-start(bf16[2,2,256,128]{3,2,1,0:T(8,128)(2,1)} %get-tuple-element.104), channel_id=1, source_target_pairs={{0,1},{1,2},{2,3},{3,0},{4,5},{5,6},{6,7},{7,4},{8,9},{9,10},{10,1... | collective-permute-start | bytes 786440 | tf_op jit(solution)/shard_map/ppermute | solution.py:438
  72.4 23.3 %collective-permute-start.17 = (bf16[2,2,256,128]{3,2,1,0:T(8,128)(2,1)}, bf16[2,2,256,128]{3,2,1,0:T(8,128)(2,1)}, u32[]{:S(2)}, u32[]{:S(2)}) collective-permute-start(bf16[2,2,256,128]{3,2,1,0:T(8,128)(2,1)} %get-tuple-element.143), channel_id=1, source_target_pairs={{0,2},{1,3},{2,0},{3,1},{4,6},{5,7},{6,4},{7,5},{8,10},{9,11},{10,... | collective-permute-start | bytes 786440 | tf_op jit(solution)/shard_map/ppermute | solution.py:438
  73.6 22.1 %collective-permute-start.16 = (bf16[2,2,256,128]{3,2,1,0:T(8,128)(2,1)}, bf16[2,2,256,128]{3,2,1,0:T(8,128)(2,1)}, u32[]{:S(2)}, u32[]{:S(2)}) collective-permute-start(bf16[2,2,256,128]{3,2,1,0:T(8,128)(2,1)} %get-tuple-element.138), channel_id=1, source_target_pairs={{0,3},{1,0},{2,1},{3,2},{4,7},{5,4},{6,5},{7,6},{8,11},{9,8},{10,9... | collective-permute-start | bytes 786440 | tf_op jit(solution)/shard_map/ppermute | solution.py:438
  76.5 19.2 %collective-permute-start.18 = (bf16[2,2,256,128]{3,2,1,0:T(8,128)(2,1)}, bf16[2,2,256,128]{3,2,1,0:T(8,128)(2,1)}, u32[]{:S(2)}, u32[]{:S(2)}) collective-permute-start(bf16[2,2,256,128]{3,2,1,0:T(8,128)(2,1)} %get-tuple-element.145), channel_id=1, source_target_pairs={{0,1},{1,2},{2,3},{3,0},{4,5},{5,6},{6,7},{7,4},{8,9},{9,10},{10,1... | collective-permute-start | bytes 786440 | tf_op jit(solution)/shard_map/ppermute | solution.py:438
  96.1 29.5 %collective-permute-start.23 = (bf16[2,2,256,128]{3,2,1,0:T(8,128)(2,1)}, bf16[2,2,256,128]{3,2,1,0:T(8,128)(2,1)S(1)}, u32[]{:S(2)}, u32[]{:S(2)}) collective-permute-start(bf16[2,2,256,128]{3,2,1,0:T(8,128)(2,1)} %get-tuple-element.155), channel_id=1, source_target_pairs={{0,3},{1,0},{2,1},{3,2},{4,7},{5,4},{6,5},{7,6},{8,11},{9,8},{10,9... | collective-permute-start | bytes 786440 | tf_op jit(solution)/shard_map/ppermute | solution.py:438
  99.7 25.9 %collective-permute-start.24 = (bf16[2,2,256,128]{3,2,1,0:T(8,128)(2,1)}, bf16[2,2,256,128]{3,2,1,0:T(8,128)(2,1)S(1)}, u32[]{:S(2)}, u32[]{:S(2)}) collective-permute-start(bf16[2,2,256,128]{3,2,1,0:T(8,128)(2,1)} %get-tuple-element.156), channel_id=1, source_target_pairs={{0,2},{1,3},{2,0},{3,1},{4,6},{5,7},{6,4},{7,5},{8,10},{9,11},{10,... | collective-permute-start | bytes 786440 | tf_op jit(solution)/shard_map/ppermute | solution.py:438
  103.1 12.8 %collective-permute-start.20 = (bf16[4,416,128]{2,1,0:T(8,128)(2,1)S(1)}, bf16[4,416,128]{2,1,0:T(8,128)(2,1)S(1)}, u32[]{:S(2)}, u32[]{:S(2)}) collective-permute-start(bf16[4,416,128]{2,1,0:T(8,128)(2,1)S(1)} %get-tuple-element.151), channel_id=1, source_target_pairs={{0,8},{4,12},{8,0},{12,4},{16,24},{20,28},{24,16},{28,20},{1,9},{5... | collective-permute-start | bytes 1277960 | tf_op jit(solution)/shard_map/ppermute | solution.py:442
  103.7 20.5 %collective-permute-start.21 = (bf16[4,416,128]{2,1,0:T(8,128)(2,1)S(1)}, bf16[4,416,128]{2,1,0:T(8,128)(2,1)S(1)}, u32[]{:S(2)}, u32[]{:S(2)}) collective-permute-start(bf16[4,416,128]{2,1,0:T(8,128)(2,1)S(1)} %get-tuple-element.152), channel_id=1, source_target_pairs={{0,16},{4,20},{8,24},{12,28},{16,0},{20,4},{24,8},{28,12},{1,17},{... | collective-permute-start | bytes 1277960 | tf_op jit(solution)/shard_map/ppermute | solution.py:442
  104.2 20.0 %collective-permute-start.22 = (bf16[4,416,128]{2,1,0:T(8,128)(2,1)S(1)}, bf16[4,416,128]{2,1,0:T(8,128)(2,1)S(1)}, u32[]{:S(2)}, u32[]{:S(2)}) collective-permute-start(bf16[4,416,128]{2,1,0:T(8,128)(2,1)S(1)} %get-tuple-element.153), channel_id=1, source_target_pairs={{0,24},{4,28},{8,16},{12,20},{16,8},{20,12},{24,0},{28,4},{1,25},{... | collective-permute-start | bytes 1277960 | tf_op jit(solution)/shard_map/ppermute | solution.py:442
  115.8 9.8 %collective-permute-start.25 = (bf16[2,2,256,128]{3,2,1,0:T(8,128)(2,1)S(1)}, bf16[2,2,256,128]{3,2,1,0:T(8,128)(2,1)S(1)}, u32[]{:S(2)}, u32[]{:S(2)}) collective-permute-start(bf16[2,2,256,128]{3,2,1,0:T(8,128)(2,1)S(1)} %copy-done.17), channel_id=1, source_target_pairs={{0,1},{1,2},{2,3},{3,0},{4,5},{5,6},{6,7},{7,4},{8,9},{9,10},{10,1... | collective-permute-start | bytes 786440 | tf_op jit(solution)/shard_map/ppermute | solution.py:438
  128.3 8.7 %collective-permute-start.27 = (bf16[416,128]{1,0:T(8,128)(2,1)S(1)}, bf16[416,128]{1,0:T(8,128)(2,1)S(1)}, u32[]{:S(2)}, u32[]{:S(2)}) collective-permute-start(bf16[416,128]{1,0:T(8,128)(2,1)S(1)} %get-tuple-element.184), channel_id=1, source_target_pairs={{0,2},{1,3},{2,0},{3,1},{4,6},{5,7},{6,4},{7,5},{8,10},{9,11},{10,... | collective-permute-start | bytes 319496 | tf_op jit(solution)/shard_map/ppermute | solution.py:438
  (27 other events, 237.5 us)

commit v6 on v5

--- a/solution.py
+++ b/solution.py
@@ -157,7 +157,7 @@
         sh = prm[d, pl.ds(speakers + spk, 1), :]
         nlow[:, pl.ds(cols[d], lanes)] = (v * sc + sh).astype(BF16)
 
-    step = 256
+    step = 512
     for f in range(0, ff, step):
         pre = dot(nlow[...], w_in[:, f:f + step], 1, 0) + b_in[:, f:f + step]
         a, s = gelu_pair(pre)
@@ -358,7 +358,7 @@
     for r in range(w_out.shape[1] // lanes):
         share[base + r * rb:base + (r + 1) * rb, :] = w_out[:, r * lanes:(r + 1) * lanes]
     base += w_out.shape[1] // lanes * rb
-    share[base:base + rs, :] = small[pl.ds(pl.multiple_of(place_ref[1] * rs, rs), rs), :].astype(BF16)
+    share[base:base + rs, :] = small[pl.ds(pl.multiple_of(place_ref[0] * rs, rs), rs), :].astype(BF16)
 
 
 def share_call(place, w_in, w_out, small, small_rows):
@@ -367,7 +367,7 @@
     ra, rb = w_in.shape[0] // GROUP, w_out.shape[0] // GROUP
     rows = w_in.shape[1] // lanes * ra + w_out.shape[1] // lanes * rb + small_rows // GROUP
     full = lambda shape: pl.BlockSpec(shape, lambda i, *_: (0,) * len(shape))
-    share_row = lambda shape: pl.BlockSpec(shape, lambda i, place: (place[1], 0))
+    share_row = lambda shape: pl.BlockSpec(shape, lambda i, place: (place[0], 0))
     return pl.pallas_call(
         functools.partial(share_body, taps, speakers),
         out_shape=jax.ShapeDtypeStruct((rows, lanes), BF16),
@@ -382,14 +382,21 @@
 
 
 def stack_body(*refs):
-    for d, v in enumerate(refs[:-1]):
-        refs[-1][d] = v[...]
+    out, sems = refs[-2:]
+    copies = [pltpu.make_async_copy(v, out.at[d], sems.at[d]) for d, v in enumerate(refs[:-2])]
+    for copy in copies:
+        copy.start()
+    for copy in copies:
+        copy.wait()
 
 
 def stack_call(parts):
     return pl.pallas_call(
         stack_body,
+        in_specs=[pl.BlockSpec(memory_space=pl.ANY)] * len(parts),
+        out_specs=pl.BlockSpec(memory_space=pltpu.VMEM),
         out_shape=jax.ShapeDtypeStruct((len(parts),) + parts[0].shape, BF16),
+        scratch_shapes=[pltpu.SemaphoreType.DMA((len(parts),))],
         name="gathered",
     )(*parts)
 
@@ -467,7 +474,7 @@
     per = w_in.shape[1]
     tiles = per // lanes
     width = nb * lanes
-    place = dp % GROUP
+    place = lax.rem(dp, GROUP)
     sizes = [sum(r) for r in RUNS]
     each = clip_num // nb
     assert each == sum(sizes)
@@ -477,7 +484,7 @@
     small = [scale_table, shift_table, conv_weight, conv_bias, b_out, layer_scale, b_in]
     used = 2 * speakers + taps + 3 + tiles
     small_rows = -(-used // (GROUP * 16)) * GROUP * 16
-    share = share_call(meta, w_in, w_out, small, small_rows)
+    share = share_call(place.astype(jnp.int32)[None], w_in, w_out, small, small_rows)
     packed = pack_call(meta, sum(RUNS, ()), nb, clips_in, grad_out)
 
     shares = [share] + [ring("chan", nb, d)(share) for d in range(1, nb)]

time: 150 us -> 149 us (level)
  transfers between devices with their start and end apart: 33 -> 33, of which waited for: 13 -> 13; matrix products, arithmetic and copies ran while one was open for 7% -> 8% of each run, Pallas kernels for 26% -> 26%
where the time goes in v6:
time: 149 us
  starting transfers between devices  52.4 us (35%)
  Pallas kernels  44.5 us (30%)
  waiting for transfers between devices  34.9 us (23%)
  other arithmetic  8.54 us (6%)
  local copies, waits for them, and re-layouts  6.51 us (4%)
  between operations  2 us (1%)
    ppermute x21, starting transfers between devices, ring(): lax.ppermute(v, axis, [(i, (i + shift) % size) for i in range(size)])  40.5 us
    pallas_call x2, Pallas kernels, block_call(): pl.pallas_call(functools.partial(body, nb, taps, speakers, runs, first, l...  35.3 us
    ppermute x12, waiting for transfers between devices, flip(): return lambda v: lax.ppermute(v, axis, [(i, i ^ mask) for i in range(size)])  20.2 us
    ppermute x21, waiting for transfers between devices, ring(): lax.ppermute(v, axis, [(i, (i + shift) % size) for i in range(size)])  14.7 us
    ppermute x12, starting transfers between devices, flip(): return lambda v: lax.ppermute(v, axis, [(i, i ^ mask) for i in range(size)])  11.9 us
    pallas_call x1, Pallas kernels, pack_call(): pl.pallas_call(functools.partial(pack_body, runs, nb), out_shape=blocks,...  3.41 us
    unnamed x36, local copies, waits for them, and re-layouts  3.34 us
    dynamic_update_slice x8, other arithmetic, per_device(): grad_clips = lax.dynamic_update_slice_in_dim(grad_clips, g, at, 0)  2.98 us
  transfers between devices with their start and end apart: 33, of which 13 were waited for; matrix products, arithmetic and copies ran while one was open for 8% of the time, Pallas kernels for 26%

profile of v6, /device:TPU:0, one launch (start us, length us, event | category | flops | bytes accessed | tf_op | source)
XLA Modules:
  0.0 148.8 jit_solution(14413103941683870885)
XLA Ops:
  2.2 3.1 %collective-permute-start = (bf16[416,128]{1,0:T(8,128)(2,1)}, bf16[416,128]{1,0:T(8,128)(2,1)S(1)}, u32[]{:S(2)}, u32[]{:S(2)}) collective-permute-start(bf16[416,128]{1,0:T(8,128)(2,1)} %share.1.refs_0_), channel_id=1, source_target_pairs={{0,1},{1,2},{2,3},{3,0},{4,5},{5,6},{6,7},{7,4},{8,9},{9,10},{10,1... | collective-permute-start | bytes 319496 | tf_op jit(solution)/shard_map/ppermute | solution.py:445
  5.3 2.6 %collective-permute-start.1 = (bf16[416,128]{1,0:T(8,128)(2,1)}, bf16[416,128]{1,0:T(8,128)(2,1)S(1)}, u32[]{:S(2)}, u32[]{:S(2)}) collective-permute-start(bf16[416,128]{1,0:T(8,128)(2,1)} %share.1.refs_0_), channel_id=1, source_target_pairs={{0,2},{1,3},{2,0},{3,1},{4,6},{5,7},{6,4},{7,5},{8,10},{9,11},{10,... | collective-permute-start | bytes 319496 | tf_op jit(solution)/shard_map/ppermute | solution.py:445
  9.8 3.4 %pack.1 = (bf16[2,1,256,128]{3,2,1,0:T(8,128)(2,1)}, bf16[2,1,256,128]{3,2,1,0:T(8,128)(2,1)}, bf16[2,1,256,128]{3,2,1,0:T(8,128)(2,1)}, bf16[2,1,256,128]{3,2,1...) custom-call(s32[2]{0:T(128)} %pad_add_fusion.meta_ref, ...), custom_call_target="tpu_custom_call" | custom-call | tf_op jit(solution)/shard_map/pack/pallas_call | solution.py:329
  19.8 2.1 %collective-permute-start.5 = (bf16[2,1,256,128]{3,2,1,0:T(8,128)(2,1)}, bf16[2,1,256,128]{3,2,1,0:T(8,128)(2,1)S(1)}, u32[]{:S(2)}, u32[]{:S(2)}) collective-permute-start(bf16[2,1,256,128]{3,2,1,0:T(8,128)(2,1)} %get-tuple-element.106), channel_id=1, source_target_pairs={{0,1},{1,2},{2,3},{3,0},{4,5},{5,6},{6,7},{7,4},{8,9},{9,10},{10,1... | collective-permute-start | bytes 393224 | tf_op jit(solution)/shard_map/ppermute | solution.py:445
  22.0 2.2 %collective-permute-start.6 = (bf16[2,1,256,128]{3,2,1,0:T(8,128)(2,1)}, bf16[2,1,256,128]{3,2,1,0:T(8,128)(2,1)S(1)}, u32[]{:S(2)}, u32[]{:S(2)}) collective-permute-start(bf16[2,1,256,128]{3,2,1,0:T(8,128)(2,1)} %get-tuple-element.107), channel_id=1, source_target_pairs={{0,2},{1,3},{2,0},{3,1},{4,6},{5,7},{6,4},{7,5},{8,10},{9,11},{10,... | collective-permute-start | bytes 393224 | tf_op jit(solution)/shard_map/ppermute | solution.py:445
  26.1 2.2 %collective-permute-done.5.refs_2_ = bf16[2,1,256,128]{3,2,1,0:T(8,128)(2,1)S(1)} collective-permute-done((bf16[2,1,256,128]{3,2,1,0:T(8,128)(2,1)}, bf16[2,1,256,128]{3,2,1,0:T(8,128)(2,1)S(1)}, u32[]{:S(2)}, u32[]{:S(2)}) %collective-permute-start.5) | collective-permute-done | bytes 131104 | tf_op jit(solution)/shard_map/ppermute | solution.py:445
  28.3 4.3 %collective-permute-done.6.refs_3_ = bf16[2,1,256,128]{3,2,1,0:T(8,128)(2,1)S(1)} collective-permute-done((bf16[2,1,256,128]{3,2,1,0:T(8,128)(2,1)}, bf16[2,1,256,128]{3,2,1,0:T(8,128)(2,1)S(1)}, u32[]{:S(2)}, u32[]{:S(2)}) %collective-permute-start.6) | collective-permute-done | bytes 131104 | tf_op jit(solution)/shard_map/ppermute | solution.py:445
  34.2 3.2 %collective-permute-start.10 = (bf16[2,1,256,128]{3,2,1,0:T(8,128)(2,1)}, bf16[2,1,256,128]{3,2,1,0:T(8,128)(2,1)S(1)}, u32[]{:S(2)}, u32[]{:S(2)}) collective-permute-start(bf16[2,1,256,128]{3,2,1,0:T(8,128)(2,1)} %get-tuple-element.113), channel_id=1, source_target_pairs={{0,1},{1,2},{2,3},{3,0},{4,5},{5,6},{6,7},{7,4},{8,9},{9,10},{10,1... | collective-permute-start | bytes 393224 | tf_op jit(solution)/shard_map/ppermute | solution.py:445
  39.8 4.8 %collective-permute-done.9 = bf16[4,416,128]{2,1,0:T(8,128)(2,1)S(1)} collective-permute-done((bf16[4,416,128]{2,1,0:T(8,128)(2,1)S(1)}, bf16[4,416,128]{2,1,0:T(8,128)(2,1)S(1)}, u32[]{:S(2)}, u32[]{:S(2)}) %collective-permute-start.9) | collective-permute-done | bytes 426016 | tf_op jit(solution)/shard_map/ppermute | solution.py:449
  47.0 2.4 %collective-permute-start.14 = (bf16[2,2,256,128]{3,2,1,0:T(8,128)(2,1)}, bf16[2,2,256,128]{3,2,1,0:T(8,128)(2,1)}, u32[]{:S(2)}, u32[]{:S(2)}) collective-permute-start(bf16[2,2,256,128]{3,2,1,0:T(8,128)(2,1)} %get-tuple-element.124), channel_id=1, source_target_pairs={{0,2},{1,3},{2,0},{3,1},{4,6},{5,7},{6,4},{7,5},{8,10},{9,11},{10,... | collective-permute-start | bytes 786440 | tf_op jit(solution)/shard_map/ppermute | solution.py:445
  49.4 3.4 %collective-permute-start.15 = (bf16[2,2,256,128]{3,2,1,0:T(8,128)(2,1)}, bf16[2,2,256,128]{3,2,1,0:T(8,128)(2,1)}, u32[]{:S(2)}, u32[]{:S(2)}) collective-permute-start(bf16[2,2,256,128]{3,2,1,0:T(8,128)(2,1)} %get-tuple-element.126), channel_id=1, source_target_pairs={{0,3},{1,0},{2,1},{3,2},{4,7},{5,4},{6,5},{7,6},{8,11},{9,8},{10,9... | collective-permute-start | bytes 786440 | tf_op jit(solution)/shard_map/ppermute | solution.py:445
  54.7 16.4 %block.2 = (bf16[2,2,256,128]{3,2,1,0:T(8,128)(2,1)}, bf16[2,2,256,128]{3,2,1,0:T(8,128)(2,1)}, bf16[2,2,256,128]{3,2,1,0:T(8,128)(2,1)}, bf16[2,2,256,128]{3,2,...) custom-call(s32[2]{0:T(128)} %pad_add_fusion.meta_ref, ...), custom_call_target="tpu_custom_call" | custom-call | tf_op jit(solution)/shard_map/block/pallas_call | solution.py:295
  72.4 2.9 %collective-permute-start.16 = (bf16[2,2,256,128]{3,2,1,0:T(8,128)(2,1)}, bf16[2,2,256,128]{3,2,1,0:T(8,128)(2,1)}, u32[]{:S(2)}, u32[]{:S(2)}) collective-permute-start(bf16[2,2,256,128]{3,2,1,0:T(8,128)(2,1)} %get-tuple-element.138), channel_id=1, source_target_pairs={{0,3},{1,0},{2,1},{3,2},{4,7},{5,4},{6,5},{7,6},{8,11},{9,8},{10,9... | collective-permute-start | bytes 786440 | tf_op jit(solution)/shard_map/ppermute | solution.py:445
  75.6 18.8 %block.3 = (bf16[2,2,256,128]{3,2,1,0:T(8,128)(2,1)}, bf16[2,2,256,128]{3,2,1,0:T(8,128)(2,1)}, bf16[2,2,256,128]{3,2,1,0:T(8,128)(2,1)}, bf16[2,2,256,128]{3,2,...) custom-call(s32[2]{0:T(128)} %pad_add_fusion.meta_ref, s32[16]{0:T(128)} %spk_ref.3, ...), custom_call_target="tpu_custom_call" | custom-call | flops 68719476736 | tf_op jit(solution)/shard_map/block/pallas_call | solution.py:295
  94.9 3.6 %collective-permute-start.23 = (bf16[2,2,256,128]{3,2,1,0:T(8,128)(2,1)}, bf16[2,2,256,128]{3,2,1,0:T(8,128)(2,1)S(1)}, u32[]{:S(2)}, u32[]{:S(2)}) collective-permute-start(bf16[2,2,256,128]{3,2,1,0:T(8,128)(2,1)} %get-tuple-element.155), channel_id=1, source_target_pairs={{0,3},{1,0},{2,1},{3,2},{4,7},{5,4},{6,5},{7,6},{8,11},{9,8},{10,9... | collective-permute-start | bytes 786440 | tf_op jit(solution)/shard_map/ppermute | solution.py:445
  99.9 2.0 %fusion.4 = (bf16[4,416,128]{2,1,0:T(8,128)(2,1)S(1)}, bf16[4,416,128]{2,1,0:T(8,128)(2,1)S(1)}, bf16[4,416,128]{2,1,0:T(8,128)(2,1)S(1)}) fusion(bf16[4,4,416,128]{3,2,1,0:T(8,128)(2,1)} %collective-permute-done.19, bf16[4,4,416,128]{3,2,1,0:T(8,128)(2,1)} %get-tuple-element.135), kind=kLoop, calls=%fused_computation.9 | loop fusion | flops 2555904 | bytes 3833856 | tf_op jit(solution)/shard_map/convert_element_type | solution.py:521
  103.0 2.5 %collective-permute-start.22 = (bf16[4,416,128]{2,1,0:T(8,128)(2,1)S(1)}, bf16[4,416,128]{2,1,0:T(8,128)(2,1)S(1)}, u32[]{:S(2)}, u32[]{:S(2)}) collective-permute-start(bf16[4,416,128]{2,1,0:T(8,128)(2,1)S(1)} %get-tuple-element.153), channel_id=1, source_target_pairs={{0,24},{4,28},{8,16},{12,20},{16,8},{20,12},{24,0},{28,4},{1,25},{... | collective-permute-start | bytes 1277960 | tf_op jit(solution)/shard_map/ppermute | solution.py:449
  111.4 3.3 %collective-permute-done.20 = bf16[4,416,128]{2,1,0:T(8,128)(2,1)S(1)} collective-permute-done((bf16[4,416,128]{2,1,0:T(8,128)(2,1)S(1)}, bf16[4,416,128]{2,1,0:T(8,128)(2,1)S(1)}, u32[]{:S(2)}, u32[]{:S(2)}) %collective-permute-start.20) | collective-permute-done | bytes 426016 | tf_op jit(solution)/shard_map/ppermute | solution.py:449
  114.6 2.1 %collective-permute-start.25 = (bf16[2,2,256,128]{3,2,1,0:T(8,128)(2,1)S(1)}, bf16[2,2,256,128]{3,2,1,0:T(8,128)(2,1)S(1)}, u32[]{:S(2)}, u32[]{:S(2)}) collective-permute-start(bf16[2,2,256,128]{3,2,1,0:T(8,128)(2,1)S(1)} %copy-done.17), channel_id=1, source_target_pairs={{0,1},{1,2},{2,3},{3,0},{4,5},{5,6},{6,7},{7,4},{8,9},{9,10},{10,1... | collective-permute-start | bytes 786440 | tf_op jit(solution)/shard_map/ppermute | solution.py:445
  116.8 6.2 %collective-permute-done.21 = bf16[4,416,128]{2,1,0:T(8,128)(2,1)S(1)} collective-permute-done((bf16[4,416,128]{2,1,0:T(8,128)(2,1)S(1)}, bf16[4,416,128]{2,1,0:T(8,128)(2,1)S(1)}, u32[]{:S(2)}, u32[]{:S(2)}) %collective-permute-start.21) | collective-permute-done | bytes 426016 | tf_op jit(solution)/shard_map/ppermute | solution.py:449
  124.7 2.4 %collective-permute-start.26 = (bf16[416,128]{1,0:T(8,128)(2,1)S(1)}, bf16[416,128]{1,0:T(8,128)(2,1)S(1)}, u32[]{:S(2)}, u32[]{:S(2)}) collective-permute-start(bf16[416,128]{1,0:T(8,128)(2,1)S(1)} %get-tuple-element.182), channel_id=1, source_target_pairs={{0,1},{1,2},{2,3},{3,0},{4,5},{5,6},{6,7},{7,4},{8,9},{9,10},{10,1... | collective-permute-start | bytes 319496 | tf_op jit(solution)/shard_map/ppermute | solution.py:445
  127.8 2.8 %collective-permute-start.28 = (bf16[416,128]{1,0:T(8,128)(2,1)S(1)}, bf16[416,128]{1,0:T(8,128)(2,1)S(1)}, u32[]{:S(2)}, u32[]{:S(2)}) collective-permute-start(bf16[416,128]{1,0:T(8,128)(2,1)S(1)} %get-tuple-element.183), channel_id=1, source_target_pairs={{0,3},{1,0},{2,1},{3,2},{4,7},{5,4},{6,5},{7,6},{8,11},{9,8},{10,9... | collective-permute-start | bytes 319496 | tf_op jit(solution)/shard_map/ppermute | solution.py:445
  132.5 3.3 %collective-permute-done.27 = bf16[416,128]{1,0:T(8,128)(2,1)S(1)} collective-permute-done((bf16[416,128]{1,0:T(8,128)(2,1)S(1)}, bf16[416,128]{1,0:T(8,128)(2,1)S(1)}, u32[]{:S(2)}, u32[]{:S(2)}) %collective-permute-start.27) | collective-permute-done | bytes 106528 | tf_op jit(solution)/shard_map/ppermute | solution.py:445
  146.3 2.4 %finish.1 = (f32[512,384]{1,0:T(8,128)}, f32[384,512]{1,0:T(8,128)}, f32[64,128]{1,0:T(8,128)}, f32[64,128]{1,0:T(8,128)}, f32[7,128]{1,0:T(8,128)}, /*index=5*/...) custom-call(s32[2]{0:T(128)} %pad_add_fusion.meta_ref, bf16[4,416,128]{2,1,0:T(8,128)(2,1)} %copy-done.3, ...), custom_call_target="tpu_custom_call" | custom-call | tf_op jit(solution)/shard_map/finish/pallas_call | solution.py:434
  (110 shorter events, 44.5 us)
Async XLA Ops:
  2.2 11.0 %collective-permute-start = (bf16[416,128]{1,0:T(8,128)(2,1)}, bf16[416,128]{1,0:T(8,128)(2,1)S(1)}, u32[]{:S(2)}, u32[]{:S(2)}) collective-permute-start(bf16[416,128]{1,0:T(8,128)(2,1)} %share.1.refs_0_), channel_id=1, source_target_pairs={{0,1},{1,2},{2,3},{3,0},{4,5},{5,6},{6,7},{7,4},{8,9},{9,10},{10,1... | collective-permute-start | bytes 319496 | tf_op jit(solution)/shard_map/ppermute | solution.py:445
  5.3 9.9 %collective-permute-start.1 = (bf16[416,128]{1,0:T(8,128)(2,1)}, bf16[416,128]{1,0:T(8,128)(2,1)S(1)}, u32[]{:S(2)}, u32[]{:S(2)}) collective-permute-start(bf16[416,128]{1,0:T(8,128)(2,1)} %share.1.refs_0_), channel_id=1, source_target_pairs={{0,2},{1,3},{2,0},{3,1},{4,6},{5,7},{6,4},{7,5},{8,10},{9,11},{10,... | collective-permute-start | bytes 319496 | tf_op jit(solution)/shard_map/ppermute | solution.py:445
  18.3 14.3 %collective-permute-start.4 = (bf16[4,416,128]{2,1,0:T(8,128)(2,1)}, bf16[4,416,128]{2,1,0:T(8,128)(2,1)S(1)}, u32[]{:S(2)}, u32[]{:S(2)}) collective-permute-start(bf16[4,416,128]{2,1,0:T(8,128)(2,1)} %gathered.1), channel_id=1, source_target_pairs={{0,8},{4,12},{8,0},{12,4},{16,24},{20,28},{24,16},{28,20},{1,9},{5... | collective-permute-start | bytes 1277960 | tf_op jit(solution)/shard_map/ppermute | solution.py:449
  19.8 8.5 %collective-permute-start.5 = (bf16[2,1,256,128]{3,2,1,0:T(8,128)(2,1)}, bf16[2,1,256,128]{3,2,1,0:T(8,128)(2,1)S(1)}, u32[]{:S(2)}, u32[]{:S(2)}) collective-permute-start(bf16[2,1,256,128]{3,2,1,0:T(8,128)(2,1)} %get-tuple-element.106), channel_id=1, source_target_pairs={{0,1},{1,2},{2,3},{3,0},{4,5},{5,6},{6,7},{7,4},{8,9},{9,10},{10,1... | collective-permute-start | bytes 393224 | tf_op jit(solution)/shard_map/ppermute | solution.py:445
  22.0 10.6 %collective-permute-start.6 = (bf16[2,1,256,128]{3,2,1,0:T(8,128)(2,1)}, bf16[2,1,256,128]{3,2,1,0:T(8,128)(2,1)S(1)}, u32[]{:S(2)}, u32[]{:S(2)}) collective-permute-start(bf16[2,1,256,128]{3,2,1,0:T(8,128)(2,1)} %get-tuple-element.107), channel_id=1, source_target_pairs={{0,2},{1,3},{2,0},{3,1},{4,6},{5,7},{6,4},{7,5},{8,10},{9,11},{10,... | collective-permute-start | bytes 393224 | tf_op jit(solution)/shard_map/ppermute | solution.py:445
  24.2 8.4 %collective-permute-start.7 = (bf16[2,1,256,128]{3,2,1,0:T(8,128)(2,1)}, bf16[2,1,256,128]{3,2,1,0:T(8,128)(2,1)S(1)}, u32[]{:S(2)}, u32[]{:S(2)}) collective-permute-start(bf16[2,1,256,128]{3,2,1,0:T(8,128)(2,1)} %get-tuple-element.108), channel_id=1, source_target_pairs={{0,3},{1,0},{2,1},{3,2},{4,7},{5,4},{6,5},{7,6},{8,11},{9,8},{10,9... | collective-permute-start | bytes 393224 | tf_op jit(solution)/shard_map/ppermute | solution.py:445
  24.6 15.2 %collective-permute-start.8 = (bf16[4,416,128]{2,1,0:T(8,128)(2,1)}, bf16[4,416,128]{2,1,0:T(8,128)(2,1)S(1)}, u32[]{:S(2)}, u32[]{:S(2)}) collective-permute-start(bf16[4,416,128]{2,1,0:T(8,128)(2,1)} %gathered.1), channel_id=1, source_target_pairs={{0,16},{4,20},{8,24},{12,28},{16,0},{20,4},{24,8},{28,12},{1,17},{... | collective-permute-start | bytes 1277960 | tf_op jit(solution)/shard_map/ppermute | solution.py:449
  32.6 11.9 %collective-permute-start.9 = (bf16[4,416,128]{2,1,0:T(8,128)(2,1)S(1)}, bf16[4,416,128]{2,1,0:T(8,128)(2,1)S(1)}, u32[]{:S(2)}, u32[]{:S(2)}) collective-permute-start(bf16[4,416,128]{2,1,0:T(8,128)(2,1)S(1)} %collective-permute-done.4), channel_id=1, source_target_pairs={{0,16},{4,20},{8,24},{12,28},{16,0},{20,4},{24,8},{28,12},{1,17},{... | collective-permute-start | bytes 1277960 | tf_op jit(solution)/shard_map/ppermute | solution.py:449
  34.2 11.6 %collective-permute-start.10 = (bf16[2,1,256,128]{3,2,1,0:T(8,128)(2,1)}, bf16[2,1,256,128]{3,2,1,0:T(8,128)(2,1)S(1)}, u32[]{:S(2)}, u32[]{:S(2)}) collective-permute-start(bf16[2,1,256,128]{3,2,1,0:T(8,128)(2,1)} %get-tuple-element.113), channel_id=1, source_target_pairs={{0,1},{1,2},{2,3},{3,0},{4,5},{5,6},{6,7},{7,4},{8,9},{9,10},{10,1... | collective-permute-start | bytes 393224 | tf_op jit(solution)/shard_map/ppermute | solution.py:445
  37.4 9.6 %collective-permute-start.11 = (bf16[2,1,256,128]{3,2,1,0:T(8,128)(2,1)}, bf16[2,1,256,128]{3,2,1,0:T(8,128)(2,1)S(1)}, u32[]{:S(2)}, u32[]{:S(2)}) collective-permute-start(bf16[2,1,256,128]{3,2,1,0:T(8,128)(2,1)} %get-tuple-element.114), channel_id=1, source_target_pairs={{0,2},{1,3},{2,0},{3,1},{4,6},{5,7},{6,4},{7,5},{8,10},{9,11},{10,... | collective-permute-start | bytes 393224 | tf_op jit(solution)/shard_map/ppermute | solution.py:445
  38.5 8.5 %collective-permute-start.12 = (bf16[2,1,256,128]{3,2,1,0:T(8,128)(2,1)}, bf16[2,1,256,128]{3,2,1,0:T(8,128)(2,1)}, u32[]{:S(2)}, u32[]{:S(2)}) collective-permute-start(bf16[2,1,256,128]{3,2,1,0:T(8,128)(2,1)} %get-tuple-element.115), channel_id=1, source_target_pairs={{0,3},{1,0},{2,1},{3,2},{4,7},{5,4},{6,5},{7,6},{8,11},{9,8},{10,9... | collective-permute-start | bytes 393224 | tf_op jit(solution)/shard_map/ppermute | solution.py:445
  47.0 24.2 %collective-permute-start.14 = (bf16[2,2,256,128]{3,2,1,0:T(8,128)(2,1)}, bf16[2,2,256,128]{3,2,1,0:T(8,128)(2,1)}, u32[]{:S(2)}, u32[]{:S(2)}) collective-permute-start(bf16[2,2,256,128]{3,2,1,0:T(8,128)(2,1)} %get-tuple-element.124), channel_id=1, source_target_pairs={{0,2},{1,3},{2,0},{3,1},{4,6},{5,7},{6,4},{7,5},{8,10},{9,11},{10,... | collective-permute-start | bytes 786440 | tf_op jit(solution)/shard_map/ppermute | solution.py:445
  49.4 26.3 %collective-permute-start.15 = (bf16[2,2,256,128]{3,2,1,0:T(8,128)(2,1)}, bf16[2,2,256,128]{3,2,1,0:T(8,128)(2,1)}, u32[]{:S(2)}, u32[]{:S(2)}) collective-permute-start(bf16[2,2,256,128]{3,2,1,0:T(8,128)(2,1)} %get-tuple-element.126), channel_id=1, source_target_pairs={{0,3},{1,0},{2,1},{3,2},{4,7},{5,4},{6,5},{7,6},{8,11},{9,8},{10,9... | collective-permute-start | bytes 786440 | tf_op jit(solution)/shard_map/ppermute | solution.py:445
  52.7 22.9 %collective-permute-start.3 = (bf16[2,2,256,128]{3,2,1,0:T(8,128)(2,1)}, bf16[2,2,256,128]{3,2,1,0:T(8,128)(2,1)}, u32[]{:S(2)}, u32[]{:S(2)}) collective-permute-start(bf16[2,2,256,128]{3,2,1,0:T(8,128)(2,1)} %get-tuple-element.104), channel_id=1, source_target_pairs={{0,1},{1,2},{2,3},{3,0},{4,5},{5,6},{6,7},{7,4},{8,9},{9,10},{10,1... | collective-permute-start | bytes 786440 | tf_op jit(solution)/shard_map/ppermute | solution.py:445
  71.2 23.3 %collective-permute-start.17 = (bf16[2,2,256,128]{3,2,1,0:T(8,128)(2,1)}, bf16[2,2,256,128]{3,2,1,0:T(8,128)(2,1)}, u32[]{:S(2)}, u32[]{:S(2)}) collective-permute-start(bf16[2,2,256,128]{3,2,1,0:T(8,128)(2,1)} %get-tuple-element.143), channel_id=1, source_target_pairs={{0,2},{1,3},{2,0},{3,1},{4,6},{5,7},{6,4},{7,5},{8,10},{9,11},{10,... | collective-permute-start | bytes 786440 | tf_op jit(solution)/shard_map/ppermute | solution.py:445
  72.4 22.1 %collective-permute-start.16 = (bf16[2,2,256,128]{3,2,1,0:T(8,128)(2,1)}, bf16[2,2,256,128]{3,2,1,0:T(8,128)(2,1)}, u32[]{:S(2)}, u32[]{:S(2)}) collective-permute-start(bf16[2,2,256,128]{3,2,1,0:T(8,128)(2,1)} %get-tuple-element.138), channel_id=1, source_target_pairs={{0,3},{1,0},{2,1},{3,2},{4,7},{5,4},{6,5},{7,6},{8,11},{9,8},{10,9... | collective-permute-start | bytes 786440 | tf_op jit(solution)/shard_map/ppermute | solution.py:445
  75.3 19.2 %collective-permute-start.18 = (bf16[2,2,256,128]{3,2,1,0:T(8,128)(2,1)}, bf16[2,2,256,128]{3,2,1,0:T(8,128)(2,1)}, u32[]{:S(2)}, u32[]{:S(2)}) collective-permute-start(bf16[2,2,256,128]{3,2,1,0:T(8,128)(2,1)} %get-tuple-element.145), channel_id=1, source_target_pairs={{0,1},{1,2},{2,3},{3,0},{4,5},{5,6},{6,7},{7,4},{8,9},{9,10},{10,1... | collective-permute-start | bytes 786440 | tf_op jit(solution)/shard_map/ppermute | solution.py:445
  94.9 29.5 %collective-permute-start.23 = (bf16[2,2,256,128]{3,2,1,0:T(8,128)(2,1)}, bf16[2,2,256,128]{3,2,1,0:T(8,128)(2,1)S(1)}, u32[]{:S(2)}, u32[]{:S(2)}) collective-permute-start(bf16[2,2,256,128]{3,2,1,0:T(8,128)(2,1)} %get-tuple-element.155), channel_id=1, source_target_pairs={{0,3},{1,0},{2,1},{3,2},{4,7},{5,4},{6,5},{7,6},{8,11},{9,8},{10,9... | collective-permute-start | bytes 786440 | tf_op jit(solution)/shard_map/ppermute | solution.py:445
  98.5 25.9 %collective-permute-start.24 = (bf16[2,2,256,128]{3,2,1,0:T(8,128)(2,1)}, bf16[2,2,256,128]{3,2,1,0:T(8,128)(2,1)S(1)}, u32[]{:S(2)}, u32[]{:S(2)}) collective-permute-start(bf16[2,2,256,128]{3,2,1,0:T(8,128)(2,1)} %get-tuple-element.156), channel_id=1, source_target_pairs={{0,2},{1,3},{2,0},{3,1},{4,6},{5,7},{6,4},{7,5},{8,10},{9,11},{10,... | collective-permute-start | bytes 786440 | tf_op jit(solution)/shard_map/ppermute | solution.py:445
  101.9 12.8 %collective-permute-start.20 = (bf16[4,416,128]{2,1,0:T(8,128)(2,1)S(1)}, bf16[4,416,128]{2,1,0:T(8,128)(2,1)S(1)}, u32[]{:S(2)}, u32[]{:S(2)}) collective-permute-start(bf16[4,416,128]{2,1,0:T(8,128)(2,1)S(1)} %get-tuple-element.151), channel_id=1, source_target_pairs={{0,8},{4,12},{8,0},{12,4},{16,24},{20,28},{24,16},{28,20},{1,9},{5... | collective-permute-start | bytes 1277960 | tf_op jit(solution)/shard_map/ppermute | solution.py:449
  102.5 20.5 %collective-permute-start.21 = (bf16[4,416,128]{2,1,0:T(8,128)(2,1)S(1)}, bf16[4,416,128]{2,1,0:T(8,128)(2,1)S(1)}, u32[]{:S(2)}, u32[]{:S(2)}) collective-permute-start(bf16[4,416,128]{2,1,0:T(8,128)(2,1)S(1)} %get-tuple-element.152), channel_id=1, source_target_pairs={{0,16},{4,20},{8,24},{12,28},{16,0},{20,4},{24,8},{28,12},{1,17},{... | collective-permute-start | bytes 1277960 | tf_op jit(solution)/shard_map/ppermute | solution.py:449
  103.0 20.0 %collective-permute-start.22 = (bf16[4,416,128]{2,1,0:T(8,128)(2,1)S(1)}, bf16[4,416,128]{2,1,0:T(8,128)(2,1)S(1)}, u32[]{:S(2)}, u32[]{:S(2)}) collective-permute-start(bf16[4,416,128]{2,1,0:T(8,128)(2,1)S(1)} %get-tuple-element.153), channel_id=1, source_target_pairs={{0,24},{4,28},{8,16},{12,20},{16,8},{20,12},{24,0},{28,4},{1,25},{... | collective-permute-start | bytes 1277960 | tf_op jit(solution)/shard_map/ppermute | solution.py:449
  114.6 9.8 %collective-permute-start.25 = (bf16[2,2,256,128]{3,2,1,0:T(8,128)(2,1)S(1)}, bf16[2,2,256,128]{3,2,1,0:T(8,128)(2,1)S(1)}, u32[]{:S(2)}, u32[]{:S(2)}) collective-permute-start(bf16[2,2,256,128]{3,2,1,0:T(8,128)(2,1)S(1)} %copy-done.17), channel_id=1, source_target_pairs={{0,1},{1,2},{2,3},{3,0},{4,5},{5,6},{6,7},{7,4},{8,9},{9,10},{10,1... | collective-permute-start | bytes 786440 | tf_op jit(solution)/shard_map/ppermute | solution.py:445
  127.1 8.7 %collective-permute-start.27 = (bf16[416,128]{1,0:T(8,128)(2,1)S(1)}, bf16[416,128]{1,0:T(8,128)(2,1)S(1)}, u32[]{:S(2)}, u32[]{:S(2)}) collective-permute-start(bf16[416,128]{1,0:T(8,128)(2,1)S(1)} %get-tuple-element.184), channel_id=1, source_target_pairs={{0,2},{1,3},{2,0},{3,1},{4,6},{5,7},{6,4},{7,5},{8,10},{9,11},{10,... | collective-permute-start | bytes 319496 | tf_op jit(solution)/shard_map/ppermute | solution.py:445
  (27 other events, 237.0 us)

commit v7 on v6

--- a/solution.py
+++ b/solution.py
@@ -539,7 +539,7 @@
             clips_out = lax.dynamic_update_slice_in_dim(clips_out, back[k][d][0], at, 0)
             g = lax.dynamic_slice_in_dim(grad_out, at, n).astype(F32) + back[k][d][1].astype(F32)
             grad_clips = lax.dynamic_update_slice_in_dim(grad_clips, g, at, 0)
-    mine, clips_out, grad_clips = lax.optimization_barrier((mine, clips_out, grad_clips))
+    mine, clips_out = lax.optimization_barrier((mine, clips_out))
 
     g_in, g_out, g_scale, g_shift, g_conv, g_cb, g_bo, g_ls, g_bi = finish_call(
         meta, gather_small(mine.astype(BF16), dp_count), nb, ra, rb, small_rows // GROUP, tiles, taps, speakers)

time: 149 us -> 155 us (1.040)
  starting transfers between devices: 52.4 us -> 58.7 us
    ppermute x21, starting transfers between devices: 40.5 us -> 46.8 us  [ring(): lax.ppermute(v, axis, [(i, (i + shift) % size) for i in range(size)])]
    ppermute x12, waiting for transfers between devices: 20.2 us -> 21.9 us  [flip(): return lambda v: lax.ppermute(v, axis, [(i, i ^ mask) for i in range(size)])]
    unnamed x36 -> x34, local copies, waits for them, and re-layouts: 3.34 us -> 3.13 us
  transfers between devices with their start and end apart: 33 -> 33, of which waited for: 13 -> 12; matrix products, arithmetic and copies ran while one was open for 8% -> 6% of each run, Pallas kernels for 26% -> 25%
where the time goes in v7:
time: 155 us; the launch traced here: 154 us
  starting transfers between devices  58.7 us (38%)
  Pallas kernels  44.4 us (29%)
  waiting for transfers between devices  36 us (23%)
  other arithmetic  7.76 us (5%)
  local copies, waits for them, and re-layouts  5.35 us (3%)
  between operations  2.03 us (1%)
    ppermute x21, starting transfers between devices, ring(): lax.ppermute(v, axis, [(i, (i + shift) % size) for i in range(size)])  46.8 us
    pallas_call x2, Pallas kernels, block_call(): pl.pallas_call(functools.partial(body, nb, taps, speakers, runs, first, l...  35.2 us
    ppermute x12, waiting for transfers between devices, flip(): return lambda v: lax.ppermute(v, axis, [(i, i ^ mask) for i in range(size)])  21.9 us
    ppermute x21, waiting for transfers between devices, ring(): lax.ppermute(v, axis, [(i, (i + shift) % size) for i in range(size)])  14.1 us
    ppermute x12, starting transfers between devices, flip(): return lambda v: lax.ppermute(v, axis, [(i, i ^ mask) for i in range(size)])  11.9 us
    pallas_call x1, Pallas kernels, pack_call(): pl.pallas_call(functools.partial(pack_body, runs, nb), out_shape=blocks,...  3.42 us
    unnamed x34, local copies, waits for them, and re-layouts  3.13 us
  transfers between devices with their start and end apart: 33, of which 12 were waited for; matrix products, arithmetic and copies ran while one was open for 6% of the time, Pallas kernels for 25%

profile of v7, /device:TPU:0, one launch (start us, length us, event | category | flops | bytes accessed | tf_op | source)
XLA Modules:
  0.0 154.3 jit_solution(3882151828037604010)
XLA Ops:
  2.2 3.1 %collective-permute-start = (bf16[416,128]{1,0:T(8,128)(2,1)}, bf16[416,128]{1,0:T(8,128)(2,1)S(1)}, u32[]{:S(2)}, u32[]{:S(2)}) collective-permute-start(bf16[416,128]{1,0:T(8,128)(2,1)} %share.1.refs_0_), channel_id=1, source_target_pairs={{0,1},{1,2},{2,3},{3,0},{4,5},{5,6},{6,7},{7,4},{8,9},{9,10},{10,1... | collective-permute-start | bytes 319496 | tf_op jit(solution)/shard_map/ppermute | solution.py:445
  5.3 2.6 %collective-permute-start.1 = (bf16[416,128]{1,0:T(8,128)(2,1)}, bf16[416,128]{1,0:T(8,128)(2,1)S(1)}, u32[]{:S(2)}, u32[]{:S(2)}) collective-permute-start(bf16[416,128]{1,0:T(8,128)(2,1)} %share.1.refs_0_), channel_id=1, source_target_pairs={{0,2},{1,3},{2,0},{3,1},{4,6},{5,7},{6,4},{7,5},{8,10},{9,11},{10,... | collective-permute-start | bytes 319496 | tf_op jit(solution)/shard_map/ppermute | solution.py:445
  9.9 3.4 %pack.1 = (bf16[2,1,256,128]{3,2,1,0:T(8,128)(2,1)}, bf16[2,1,256,128]{3,2,1,0:T(8,128)(2,1)}, bf16[2,1,256,128]{3,2,1,0:T(8,128)(2,1)}, bf16[2,1,256,128]{3,2,1...) custom-call(s32[2]{0:T(128)} %pad_add_fusion.meta_ref, ...), custom_call_target="tpu_custom_call" | custom-call | tf_op jit(solution)/shard_map/pack/pallas_call | solution.py:329
  19.8 2.1 %collective-permute-start.5 = (bf16[2,1,256,128]{3,2,1,0:T(8,128)(2,1)}, bf16[2,1,256,128]{3,2,1,0:T(8,128)(2,1)S(1)}, u32[]{:S(2)}, u32[]{:S(2)}) collective-permute-start(bf16[2,1,256,128]{3,2,1,0:T(8,128)(2,1)} %get-tuple-element.105), channel_id=1, source_target_pairs={{0,1},{1,2},{2,3},{3,0},{4,5},{5,6},{6,7},{7,4},{8,9},{9,10},{10,1... | collective-permute-start | bytes 393224 | tf_op jit(solution)/shard_map/ppermute | solution.py:445
  22.0 2.2 %collective-permute-start.6 = (bf16[2,1,256,128]{3,2,1,0:T(8,128)(2,1)}, bf16[2,1,256,128]{3,2,1,0:T(8,128)(2,1)S(1)}, u32[]{:S(2)}, u32[]{:S(2)}) collective-permute-start(bf16[2,1,256,128]{3,2,1,0:T(8,128)(2,1)} %get-tuple-element.106), channel_id=1, source_target_pairs={{0,2},{1,3},{2,0},{3,1},{4,6},{5,7},{6,4},{7,5},{8,10},{9,11},{10,... | collective-permute-start | bytes 393224 | tf_op jit(solution)/shard_map/ppermute | solution.py:445
  26.1 2.2 %collective-permute-done.5.refs_2_ = bf16[2,1,256,128]{3,2,1,0:T(8,128)(2,1)S(1)} collective-permute-done((bf16[2,1,256,128]{3,2,1,0:T(8,128)(2,1)}, bf16[2,1,256,128]{3,2,1,0:T(8,128)(2,1)S(1)}, u32[]{:S(2)}, u32[]{:S(2)}) %collective-permute-start.5) | collective-permute-done | bytes 131104 | tf_op jit(solution)/shard_map/ppermute | solution.py:445
  28.3 4.3 %collective-permute-done.6.refs_3_ = bf16[2,1,256,128]{3,2,1,0:T(8,128)(2,1)S(1)} collective-permute-done((bf16[2,1,256,128]{3,2,1,0:T(8,128)(2,1)}, bf16[2,1,256,128]{3,2,1,0:T(8,128)(2,1)S(1)}, u32[]{:S(2)}, u32[]{:S(2)}) %collective-permute-start.6) | collective-permute-done | bytes 131104 | tf_op jit(solution)/shard_map/ppermute | solution.py:445
  34.2 3.2 %collective-permute-start.10 = (bf16[2,1,256,128]{3,2,1,0:T(8,128)(2,1)}, bf16[2,1,256,128]{3,2,1,0:T(8,128)(2,1)S(1)}, u32[]{:S(2)}, u32[]{:S(2)}) collective-permute-start(bf16[2,1,256,128]{3,2,1,0:T(8,128)(2,1)} %get-tuple-element.112), channel_id=1, source_target_pairs={{0,1},{1,2},{2,3},{3,0},{4,5},{5,6},{6,7},{7,4},{8,9},{9,10},{10,1... | collective-permute-start | bytes 393224 | tf_op jit(solution)/shard_map/ppermute | solution.py:445
  39.8 4.8 %collective-permute-done.9 = bf16[4,416,128]{2,1,0:T(8,128)(2,1)S(1)} collective-permute-done((bf16[4,416,128]{2,1,0:T(8,128)(2,1)S(1)}, bf16[4,416,128]{2,1,0:T(8,128)(2,1)S(1)}, u32[]{:S(2)}, u32[]{:S(2)}) %collective-permute-start.9) | collective-permute-done | bytes 426016 | tf_op jit(solution)/shard_map/ppermute | solution.py:449
  47.0 2.4 %collective-permute-start.14 = (bf16[2,2,256,128]{3,2,1,0:T(8,128)(2,1)}, bf16[2,2,256,128]{3,2,1,0:T(8,128)(2,1)}, u32[]{:S(2)}, u32[]{:S(2)}) collective-permute-start(bf16[2,2,256,128]{3,2,1,0:T(8,128)(2,1)} %get-tuple-element.123), channel_id=1, source_target_pairs={{0,2},{1,3},{2,0},{3,1},{4,6},{5,7},{6,4},{7,5},{8,10},{9,11},{10,... | collective-permute-start | bytes 786440 | tf_op jit(solution)/shard_map/ppermute | solution.py:445
  49.3 3.4 %collective-permute-start.15 = (bf16[2,2,256,128]{3,2,1,0:T(8,128)(2,1)}, bf16[2,2,256,128]{3,2,1,0:T(8,128)(2,1)}, u32[]{:S(2)}, u32[]{:S(2)}) collective-permute-start(bf16[2,2,256,128]{3,2,1,0:T(8,128)(2,1)} %get-tuple-element.125), channel_id=1, source_target_pairs={{0,3},{1,0},{2,1},{3,2},{4,7},{5,4},{6,5},{7,6},{8,11},{9,8},{10,9... | collective-permute-start | bytes 786440 | tf_op jit(solution)/shard_map/ppermute | solution.py:445
  54.7 16.4 %block.2 = (bf16[2,2,256,128]{3,2,1,0:T(8,128)(2,1)}, bf16[2,2,256,128]{3,2,1,0:T(8,128)(2,1)}, bf16[2,2,256,128]{3,2,1,0:T(8,128)(2,1)}, bf16[2,2,256,128]{3,2,...) custom-call(s32[2]{0:T(128)} %pad_add_fusion.meta_ref, ...), custom_call_target="tpu_custom_call" | custom-call | tf_op jit(solution)/shard_map/block/pallas_call | solution.py:295
  72.4 2.9 %collective-permute-start.16 = (bf16[2,2,256,128]{3,2,1,0:T(8,128)(2,1)}, bf16[2,2,256,128]{3,2,1,0:T(8,128)(2,1)}, u32[]{:S(2)}, u32[]{:S(2)}) collective-permute-start(bf16[2,2,256,128]{3,2,1,0:T(8,128)(2,1)} %get-tuple-element.137), channel_id=1, source_target_pairs={{0,3},{1,0},{2,1},{3,2},{4,7},{5,4},{6,5},{7,6},{8,11},{9,8},{10,9... | collective-permute-start | bytes 786440 | tf_op jit(solution)/shard_map/ppermute | solution.py:445
  75.6 18.8 %block.3 = (bf16[2,2,256,128]{3,2,1,0:T(8,128)(2,1)}, bf16[2,2,256,128]{3,2,1,0:T(8,128)(2,1)}, bf16[2,2,256,128]{3,2,1,0:T(8,128)(2,1)}, bf16[2,2,256,128]{3,2,...) custom-call(s32[2]{0:T(128)} %pad_add_fusion.meta_ref, s32[16]{0:T(128)} %spk_ref.3, ...), custom_call_target="tpu_custom_call" | custom-call | flops 68719476736 | tf_op jit(solution)/shard_map/block/pallas_call | solution.py:295
  94.9 3.6 %collective-permute-start.23 = (bf16[2,2,256,128]{3,2,1,0:T(8,128)(2,1)}, bf16[2,2,256,128]{3,2,1,0:T(8,128)(2,1)S(1)}, u32[]{:S(2)}, u32[]{:S(2)}) collective-permute-start(bf16[2,2,256,128]{3,2,1,0:T(8,128)(2,1)} %get-tuple-element.154), channel_id=1, source_target_pairs={{0,3},{1,0},{2,1},{3,2},{4,7},{5,4},{6,5},{7,6},{8,11},{9,8},{10,9... | collective-permute-start | bytes 786440 | tf_op jit(solution)/shard_map/ppermute | solution.py:445
  98.4 7.4 %collective-permute-start.24 = (bf16[2,2,256,128]{3,2,1,0:T(8,128)(2,1)}, bf16[2,2,256,128]{3,2,1,0:T(8,128)(2,1)S(1)}, u32[]{:S(2)}, u32[]{:S(2)}) collective-permute-start(bf16[2,2,256,128]{3,2,1,0:T(8,128)(2,1)} %get-tuple-element.155), channel_id=1, source_target_pairs={{0,2},{1,3},{2,0},{3,1},{4,6},{5,7},{6,4},{7,5},{8,10},{9,11},{10,... | collective-permute-start | bytes 786440 | tf_op jit(solution)/shard_map/ppermute | solution.py:445
  105.9 2.0 %fusion.4 = (bf16[4,416,128]{2,1,0:T(8,128)(2,1)S(1)}, bf16[4,416,128]{2,1,0:T(8,128)(2,1)S(1)}, bf16[4,416,128]{2,1,0:T(8,128)(2,1)S(1)}) fusion(bf16[4,4,416,128]{3,2,1,0:T(8,128)(2,1)} %collective-permute-done.19, bf16[4,4,416,128]{3,2,1,0:T(8,128)(2,1)} %get-tuple-element.134), kind=kLoop, calls=%fused_computation.9 | loop fusion | flops 2555904 | bytes 3833856 | tf_op jit(solution)/shard_map/convert_element_type | solution.py:521
  109.0 2.4 %collective-permute-start.22 = (bf16[4,416,128]{2,1,0:T(8,128)(2,1)S(1)}, bf16[4,416,128]{2,1,0:T(8,128)(2,1)S(1)}, u32[]{:S(2)}, u32[]{:S(2)}) collective-permute-start(bf16[4,416,128]{2,1,0:T(8,128)(2,1)S(1)} %get-tuple-element.152), channel_id=1, source_target_pairs={{0,24},{4,28},{8,16},{12,20},{16,8},{20,12},{24,0},{28,4},{1,25},{... | collective-permute-start | bytes 1277960 | tf_op jit(solution)/shard_map/ppermute | solution.py:449
  115.6 5.1 %collective-permute-done.20 = bf16[4,416,128]{2,1,0:T(8,128)(2,1)S(1)} collective-permute-done((bf16[4,416,128]{2,1,0:T(8,128)(2,1)S(1)}, bf16[4,416,128]{2,1,0:T(8,128)(2,1)S(1)}, u32[]{:S(2)}, u32[]{:S(2)}) %collective-permute-start.20) | collective-permute-done | bytes 426016 | tf_op jit(solution)/shard_map/ppermute | solution.py:449
  122.6 6.4 %collective-permute-done.21 = bf16[4,416,128]{2,1,0:T(8,128)(2,1)S(1)} collective-permute-done((bf16[4,416,128]{2,1,0:T(8,128)(2,1)S(1)}, bf16[4,416,128]{2,1,0:T(8,128)(2,1)S(1)}, u32[]{:S(2)}, u32[]{:S(2)}) %collective-permute-start.21) | collective-permute-done | bytes 426016 | tf_op jit(solution)/shard_map/ppermute | solution.py:449
  134.1 2.8 %collective-permute-start.28 = (bf16[416,128]{1,0:T(8,128)(2,1)S(1)}, bf16[416,128]{1,0:T(8,128)(2,1)S(1)}, u32[]{:S(2)}, u32[]{:S(2)}) collective-permute-start(bf16[416,128]{1,0:T(8,128)(2,1)S(1)} %get-tuple-element.181), channel_id=1, source_target_pairs={{0,3},{1,0},{2,1},{3,2},{4,7},{5,4},{6,5},{7,6},{8,11},{9,8},{10,9... | collective-permute-start | bytes 319496 | tf_op jit(solution)/shard_map/ppermute | solution.py:445
  137.7 4.0 %collective-permute-done.27 = bf16[416,128]{1,0:T(8,128)(2,1)S(1)} collective-permute-done((bf16[416,128]{1,0:T(8,128)(2,1)S(1)}, bf16[416,128]{1,0:T(8,128)(2,1)S(1)}, u32[]{:S(2)}, u32[]{:S(2)}) %collective-permute-start.27) | collective-permute-done | bytes 106528 | tf_op jit(solution)/shard_map/ppermute | solution.py:445
  147.0 2.7 %collective-permute-done.30 = bf16[416,128]{1,0:T(8,128)(2,1)S(1)} collective-permute-done((bf16[416,128]{1,0:T(8,128)(2,1)S(1)}, bf16[416,128]{1,0:T(8,128)(2,1)S(1)}, u32[]{:S(2)}, u32[]{:S(2)}) %collective-permute-start.30) | collective-permute-done | bytes 106528 | tf_op jit(solution)/shard_map/ppermute | solution.py:449
  151.8 2.4 %finish.1 = (f32[512,384]{1,0:T(8,128)}, f32[384,512]{1,0:T(8,128)}, f32[64,128]{1,0:T(8,128)}, f32[64,128]{1,0:T(8,128)}, f32[7,128]{1,0:T(8,128)}, /*index=5*/...) custom-call(s32[2]{0:T(128)} %pad_add_fusion.meta_ref, bf16[4,416,128]{2,1,0:T(8,128)(2,1)} %copy-done.3, ...), custom_call_target="tpu_custom_call" | custom-call | tf_op jit(solution)/shard_map/finish/pallas_call | solution.py:434
  (108 shorter events, 41.5 us)
Async XLA Ops:
  2.2 11.1 %collective-permute-start = (bf16[416,128]{1,0:T(8,128)(2,1)}, bf16[416,128]{1,0:T(8,128)(2,1)S(1)}, u32[]{:S(2)}, u32[]{:S(2)}) collective-permute-start(bf16[416,128]{1,0:T(8,128)(2,1)} %share.1.refs_0_), channel_id=1, source_target_pairs={{0,1},{1,2},{2,3},{3,0},{4,5},{5,6},{6,7},{7,4},{8,9},{9,10},{10,1... | collective-permute-start | bytes 319496 | tf_op jit(solution)/shard_map/ppermute | solution.py:445
  5.3 9.9 %collective-permute-start.1 = (bf16[416,128]{1,0:T(8,128)(2,1)}, bf16[416,128]{1,0:T(8,128)(2,1)S(1)}, u32[]{:S(2)}, u32[]{:S(2)}) collective-permute-start(bf16[416,128]{1,0:T(8,128)(2,1)} %share.1.refs_0_), channel_id=1, source_target_pairs={{0,2},{1,3},{2,0},{3,1},{4,6},{5,7},{6,4},{7,5},{8,10},{9,11},{10,... | collective-permute-start | bytes 319496 | tf_op jit(solution)/shard_map/ppermute | solution.py:445
  18.3 14.3 %collective-permute-start.4 = (bf16[4,416,128]{2,1,0:T(8,128)(2,1)}, bf16[4,416,128]{2,1,0:T(8,128)(2,1)S(1)}, u32[]{:S(2)}, u32[]{:S(2)}) collective-permute-start(bf16[4,416,128]{2,1,0:T(8,128)(2,1)} %gathered.1), channel_id=1, source_target_pairs={{0,8},{4,12},{8,0},{12,4},{16,24},{20,28},{24,16},{28,20},{1,9},{5... | collective-permute-start | bytes 1277960 | tf_op jit(solution)/shard_map/ppermute | solution.py:449
  19.8 8.5 %collective-permute-start.5 = (bf16[2,1,256,128]{3,2,1,0:T(8,128)(2,1)}, bf16[2,1,256,128]{3,2,1,0:T(8,128)(2,1)S(1)}, u32[]{:S(2)}, u32[]{:S(2)}) collective-permute-start(bf16[2,1,256,128]{3,2,1,0:T(8,128)(2,1)} %get-tuple-element.105), channel_id=1, source_target_pairs={{0,1},{1,2},{2,3},{3,0},{4,5},{5,6},{6,7},{7,4},{8,9},{9,10},{10,1... | collective-permute-start | bytes 393224 | tf_op jit(solution)/shard_map/ppermute | solution.py:445
  22.0 10.6 %collective-permute-start.6 = (bf16[2,1,256,128]{3,2,1,0:T(8,128)(2,1)}, bf16[2,1,256,128]{3,2,1,0:T(8,128)(2,1)S(1)}, u32[]{:S(2)}, u32[]{:S(2)}) collective-permute-start(bf16[2,1,256,128]{3,2,1,0:T(8,128)(2,1)} %get-tuple-element.106), channel_id=1, source_target_pairs={{0,2},{1,3},{2,0},{3,1},{4,6},{5,7},{6,4},{7,5},{8,10},{9,11},{10,... | collective-permute-start | bytes 393224 | tf_op jit(solution)/shard_map/ppermute | solution.py:445
  24.5 15.2 %collective-permute-start.8 = (bf16[4,416,128]{2,1,0:T(8,128)(2,1)}, bf16[4,416,128]{2,1,0:T(8,128)(2,1)S(1)}, u32[]{:S(2)}, u32[]{:S(2)}) collective-permute-start(bf16[4,416,128]{2,1,0:T(8,128)(2,1)} %gathered.1), channel_id=1, source_target_pairs={{0,16},{4,20},{8,24},{12,28},{16,0},{20,4},{24,8},{28,12},{1,17},{... | collective-permute-start | bytes 1277960 | tf_op jit(solution)/shard_map/ppermute | solution.py:449
  32.6 11.9 %collective-permute-start.9 = (bf16[4,416,128]{2,1,0:T(8,128)(2,1)S(1)}, bf16[4,416,128]{2,1,0:T(8,128)(2,1)S(1)}, u32[]{:S(2)}, u32[]{:S(2)}) collective-permute-start(bf16[4,416,128]{2,1,0:T(8,128)(2,1)S(1)} %collective-permute-done.4), channel_id=1, source_target_pairs={{0,16},{4,20},{8,24},{12,28},{16,0},{20,4},{24,8},{28,12},{1,17},{... | collective-permute-start | bytes 1277960 | tf_op jit(solution)/shard_map/ppermute | solution.py:449
  34.2 11.6 %collective-permute-start.10 = (bf16[2,1,256,128]{3,2,1,0:T(8,128)(2,1)}, bf16[2,1,256,128]{3,2,1,0:T(8,128)(2,1)S(1)}, u32[]{:S(2)}, u32[]{:S(2)}) collective-permute-start(bf16[2,1,256,128]{3,2,1,0:T(8,128)(2,1)} %get-tuple-element.112), channel_id=1, source_target_pairs={{0,1},{1,2},{2,3},{3,0},{4,5},{5,6},{6,7},{7,4},{8,9},{9,10},{10,1... | collective-permute-start | bytes 393224 | tf_op jit(solution)/shard_map/ppermute | solution.py:445
  37.4 9.6 %collective-permute-start.11 = (bf16[2,1,256,128]{3,2,1,0:T(8,128)(2,1)}, bf16[2,1,256,128]{3,2,1,0:T(8,128)(2,1)S(1)}, u32[]{:S(2)}, u32[]{:S(2)}) collective-permute-start(bf16[2,1,256,128]{3,2,1,0:T(8,128)(2,1)} %get-tuple-element.113), channel_id=1, source_target_pairs={{0,2},{1,3},{2,0},{3,1},{4,6},{5,7},{6,4},{7,5},{8,10},{9,11},{10,... | collective-permute-start | bytes 393224 | tf_op jit(solution)/shard_map/ppermute | solution.py:445
  38.5 8.5 %collective-permute-start.12 = (bf16[2,1,256,128]{3,2,1,0:T(8,128)(2,1)}, bf16[2,1,256,128]{3,2,1,0:T(8,128)(2,1)}, u32[]{:S(2)}, u32[]{:S(2)}) collective-permute-start(bf16[2,1,256,128]{3,2,1,0:T(8,128)(2,1)} %get-tuple-element.114), channel_id=1, source_target_pairs={{0,3},{1,0},{2,1},{3,2},{4,7},{5,4},{6,5},{7,6},{8,11},{9,8},{10,9... | collective-permute-start | bytes 393224 | tf_op jit(solution)/shard_map/ppermute | solution.py:445
  47.0 24.2 %collective-permute-start.14 = (bf16[2,2,256,128]{3,2,1,0:T(8,128)(2,1)}, bf16[2,2,256,128]{3,2,1,0:T(8,128)(2,1)}, u32[]{:S(2)}, u32[]{:S(2)}) collective-permute-start(bf16[2,2,256,128]{3,2,1,0:T(8,128)(2,1)} %get-tuple-element.123), channel_id=1, source_target_pairs={{0,2},{1,3},{2,0},{3,1},{4,6},{5,7},{6,4},{7,5},{8,10},{9,11},{10,... | collective-permute-start | bytes 786440 | tf_op jit(solution)/shard_map/ppermute | solution.py:445
  49.3 26.3 %collective-permute-start.15 = (bf16[2,2,256,128]{3,2,1,0:T(8,128)(2,1)}, bf16[2,2,256,128]{3,2,1,0:T(8,128)(2,1)}, u32[]{:S(2)}, u32[]{:S(2)}) collective-permute-start(bf16[2,2,256,128]{3,2,1,0:T(8,128)(2,1)} %get-tuple-element.125), channel_id=1, source_target_pairs={{0,3},{1,0},{2,1},{3,2},{4,7},{5,4},{6,5},{7,6},{8,11},{9,8},{10,9... | collective-permute-start | bytes 786440 | tf_op jit(solution)/shard_map/ppermute | solution.py:445
  52.7 22.9 %collective-permute-start.3 = (bf16[2,2,256,128]{3,2,1,0:T(8,128)(2,1)}, bf16[2,2,256,128]{3,2,1,0:T(8,128)(2,1)}, u32[]{:S(2)}, u32[]{:S(2)}) collective-permute-start(bf16[2,2,256,128]{3,2,1,0:T(8,128)(2,1)} %get-tuple-element.103), channel_id=1, source_target_pairs={{0,1},{1,2},{2,3},{3,0},{4,5},{5,6},{6,7},{7,4},{8,9},{9,10},{10,1... | collective-permute-start | bytes 786440 | tf_op jit(solution)/shard_map/ppermute | solution.py:445
  71.1 23.3 %collective-permute-start.17 = (bf16[2,2,256,128]{3,2,1,0:T(8,128)(2,1)}, bf16[2,2,256,128]{3,2,1,0:T(8,128)(2,1)S(1)}, u32[]{:S(2)}, u32[]{:S(2)}) collective-permute-start(bf16[2,2,256,128]{3,2,1,0:T(8,128)(2,1)} %get-tuple-element.142), channel_id=1, source_target_pairs={{0,2},{1,3},{2,0},{3,1},{4,6},{5,7},{6,4},{7,5},{8,10},{9,11},{10,... | collective-permute-start | bytes 786440 | tf_op jit(solution)/shard_map/ppermute | solution.py:445
  72.4 22.1 %collective-permute-start.16 = (bf16[2,2,256,128]{3,2,1,0:T(8,128)(2,1)}, bf16[2,2,256,128]{3,2,1,0:T(8,128)(2,1)}, u32[]{:S(2)}, u32[]{:S(2)}) collective-permute-start(bf16[2,2,256,128]{3,2,1,0:T(8,128)(2,1)} %get-tuple-element.137), channel_id=1, source_target_pairs={{0,3},{1,0},{2,1},{3,2},{4,7},{5,4},{6,5},{7,6},{8,11},{9,8},{10,9... | collective-permute-start | bytes 786440 | tf_op jit(solution)/shard_map/ppermute | solution.py:445
  75.3 19.2 %collective-permute-start.18 = (bf16[2,2,256,128]{3,2,1,0:T(8,128)(2,1)}, bf16[2,2,256,128]{3,2,1,0:T(8,128)(2,1)}, u32[]{:S(2)}, u32[]{:S(2)}) collective-permute-start(bf16[2,2,256,128]{3,2,1,0:T(8,128)(2,1)} %get-tuple-element.144), channel_id=1, source_target_pairs={{0,1},{1,2},{2,3},{3,0},{4,5},{5,6},{6,7},{7,4},{8,9},{9,10},{10,1... | collective-permute-start | bytes 786440 | tf_op jit(solution)/shard_map/ppermute | solution.py:445
  94.5 11.4 %collective-permute-start.19 = (bf16[4,4,416,128]{3,2,1,0:T(8,128)(2,1)}, bf16[4,4,416,128]{3,2,1,0:T(8,128)(2,1)}, u32[]{:S(2)}, u32[]{:S(2)}) collective-permute-start(bf16[4,4,416,128]{3,2,1,0:T(8,128)(2,1)} %get-tuple-element.145), channel_id=1, source_target_pairs={{0,4},{4,0},{8,12},{12,8},{16,20},{20,16},{24,28},{28,24},{1,5},{5... | collective-permute-start | bytes 5111816 | tf_op jit(solution)/shard_map/ppermute | solution.py:449
  94.9 35.6 %collective-permute-start.23 = (bf16[2,2,256,128]{3,2,1,0:T(8,128)(2,1)}, bf16[2,2,256,128]{3,2,1,0:T(8,128)(2,1)S(1)}, u32[]{:S(2)}, u32[]{:S(2)}) collective-permute-start(bf16[2,2,256,128]{3,2,1,0:T(8,128)(2,1)} %get-tuple-element.154), channel_id=1, source_target_pairs={{0,3},{1,0},{2,1},{3,2},{4,7},{5,4},{6,5},{7,6},{8,11},{9,8},{10,9... | collective-permute-start | bytes 786440 | tf_op jit(solution)/shard_map/ppermute | solution.py:445
  98.4 32.0 %collective-permute-start.24 = (bf16[2,2,256,128]{3,2,1,0:T(8,128)(2,1)}, bf16[2,2,256,128]{3,2,1,0:T(8,128)(2,1)S(1)}, u32[]{:S(2)}, u32[]{:S(2)}) collective-permute-start(bf16[2,2,256,128]{3,2,1,0:T(8,128)(2,1)} %get-tuple-element.155), channel_id=1, source_target_pairs={{0,2},{1,3},{2,0},{3,1},{4,6},{5,7},{6,4},{7,5},{8,10},{9,11},{10,... | collective-permute-start | bytes 786440 | tf_op jit(solution)/shard_map/ppermute | solution.py:445
  107.9 12.8 %collective-permute-start.20 = (bf16[4,416,128]{2,1,0:T(8,128)(2,1)S(1)}, bf16[4,416,128]{2,1,0:T(8,128)(2,1)S(1)}, u32[]{:S(2)}, u32[]{:S(2)}) collective-permute-start(bf16[4,416,128]{2,1,0:T(8,128)(2,1)S(1)} %get-tuple-element.150), channel_id=1, source_target_pairs={{0,8},{4,12},{8,0},{12,4},{16,24},{20,28},{24,16},{28,20},{1,9},{5... | collective-permute-start | bytes 1277960 | tf_op jit(solution)/shard_map/ppermute | solution.py:449
  108.0 21.1 %collective-permute-start.21 = (bf16[4,416,128]{2,1,0:T(8,128)(2,1)S(1)}, bf16[4,416,128]{2,1,0:T(8,128)(2,1)S(1)}, u32[]{:S(2)}, u32[]{:S(2)}) collective-permute-start(bf16[4,416,128]{2,1,0:T(8,128)(2,1)S(1)} %get-tuple-element.151), channel_id=1, source_target_pairs={{0,16},{4,20},{8,24},{12,28},{16,0},{20,4},{24,8},{28,12},{1,17},{... | collective-permute-start | bytes 1277960 | tf_op jit(solution)/shard_map/ppermute | solution.py:449
  109.0 20.0 %collective-permute-start.22 = (bf16[4,416,128]{2,1,0:T(8,128)(2,1)S(1)}, bf16[4,416,128]{2,1,0:T(8,128)(2,1)S(1)}, u32[]{:S(2)}, u32[]{:S(2)}) collective-permute-start(bf16[4,416,128]{2,1,0:T(8,128)(2,1)S(1)} %get-tuple-element.152), channel_id=1, source_target_pairs={{0,24},{4,28},{8,16},{12,20},{16,8},{20,12},{24,0},{28,4},{1,25},{... | collective-permute-start | bytes 1277960 | tf_op jit(solution)/shard_map/ppermute | solution.py:449
  120.7 9.8 %collective-permute-start.25 = (bf16[2,2,256,128]{3,2,1,0:T(8,128)(2,1)S(1)}, bf16[2,2,256,128]{3,2,1,0:T(8,128)(2,1)S(1)}, u32[]{:S(2)}, u32[]{:S(2)}) collective-permute-start(bf16[2,2,256,128]{3,2,1,0:T(8,128)(2,1)S(1)} %copy-done.16), channel_id=1, source_target_pairs={{0,1},{1,2},{2,3},{3,0},{4,5},{5,6},{6,7},{7,4},{8,9},{9,10},{10,1... | collective-permute-start | bytes 786440 | tf_op jit(solution)/shard_map/ppermute | solution.py:445
  132.3 9.4 %collective-permute-start.27 = (bf16[416,128]{1,0:T(8,128)(2,1)S(1)}, bf16[416,128]{1,0:T(8,128)(2,1)S(1)}, u32[]{:S(2)}, u32[]{:S(2)}) collective-permute-start(bf16[416,128]{1,0:T(8,128)(2,1)S(1)} %get-tuple-element.182), channel_id=1, source_target_pairs={{0,2},{1,3},{2,0},{3,1},{4,6},{5,7},{6,4},{7,5},{8,10},{9,11},{10,... | collective-permute-start | bytes 319496 | tf_op jit(solution)/shard_map/ppermute | solution.py:445
  (26 other events, 225.2 us)
